TPU v7x, 512 devices: a whole 4x8x8 slice. The times are simulated.
512 devices in a mesh: grp: 16 (over z, core), dev: 32 (over y, x).
Axes of the slice: x: 4, y: 8, z: 8, core: 2. Of those that a mesh axis runs over, the one named last changes fastest.
Arguments:
- old_fields: float32 [3, 4096, 32, 1024], P(None, ('grp', 'dev')), as said below
- old_counts: int32 [512], replicated, may hold values from 2 to 6, as said below
Outputs:
- pressure_out: float32 [512, 1024, 128], P('grp', 'dev')
- residual: float32 [512, 1024, 128], P('grp', 'dev')
Inputs may be any that keep to these rules, and one draw needn't show every extreme that they name: `old_counts`: the counts sum to 2048; each device's first box number, start[e], lies between e * 4 and e * 4 + 4 / 2; the slots of a device beyond its count hold data that belongs to no box. `old_fields`: coefficient entries (component 2) are positive; components 0 and 1 are real-valued of order one.
All inputs are finite; a program needn't handle non-finite values.
Results may differ from a plain program's by a relative error of at most 0.0003.
Values sent between devices are 32-bit elements; how exact they have to be, the bound alone decides.
No kernel may reach another device: no remote copies, remote signals or barrier semaphores. Data moves between devices by JAX's collectives and lax.ppermute only.
A program may use at most 64 MiB of HBM per device.

v0:
```python
import jax
import jax.numpy as jnp
from jax import lax
from jax.sharding import PartitionSpec as P


def from_behind(value, axis, steps):
    count = lax.axis_size(axis)
    leading, last = (max(0, -steps), min(count, count - steps))
    return lax.ppermute(value, axis, [(source, source + steps) for source in range(leading, last)])


def extended(array, sides, width):
    for axis, dim in sides:
        size, length = (lax.axis_size(axis), array.shape[dim])
        up = [(i, (i + 1) % size) for i in range(size - 1)]
        down = [(j, i) for i, j in up]
        last = lax.slice_in_dim(array, length - width, length, axis=dim)
        leading = lax.slice_in_dim(array, 0, width, axis=dim)
        before = lax.ppermute(last, axis, up)
        after = lax.ppermute(leading, axis, down)
        array = jnp.concatenate([before, array, after], axis=dim)
    return array


def shifted_slices(padded):
    sizes = (padded.shape[0] - 2, padded.shape[1] - 2, padded.shape[2] - 2)
    pieces = []
    for axis_id in range(3):
        for offset in (0, 2):
            starts = [1, 1, 1]
            starts[axis_id] = offset
            pieces.append(lax.dynamic_slice(padded, starts, sizes))
    return pieces


def beta_phi(padded_phi, betas):
    total = jnp.zeros(betas[0].shape, jnp.float32)
    for beta, neighbour in zip(betas, shifted_slices(padded_phi)):
        total = total + beta * neighbour
    return total


def per_device(old_fields, old_counts):
    slot_count = old_fields.shape[1]
    box_edge = old_fields.shape[2]
    box_count = slot_count // 2
    device_id = lax.axis_index("grp") * lax.axis_size("dev") + lax.axis_index("dev")
    ends = jnp.cumsum(old_counts)
    starts = jnp.concatenate([jnp.zeros((1,), jnp.int32), ends])
    wanted = device_id * box_count + jnp.arange(box_count, dtype=jnp.int32)
    own_start = starts[device_id]
    is_below = wanted < own_start
    owner_dev = device_id - is_below.astype(jnp.int32)
    local_slot = wanted - starts[owner_dev]
    from_lower = from_behind(old_fields, ("grp", "dev"), 1)
    lower_rows = jnp.take(from_lower, jnp.clip(local_slot, 0, from_lower.shape[1] - 1), axis=1)
    own_rows = jnp.take(old_fields, jnp.clip(local_slot, 0, slot_count - 1), axis=1)
    moved = jnp.where(is_below[None, :, None, None], lower_rows, own_rows)
    moved = moved.reshape(3, box_count, box_edge, box_edge, box_edge)
    moved = jnp.transpose(moved, (0, 2, 3, 1, 4)).reshape(
        3, box_edge, box_edge, box_count * box_edge
    )
    pressure = moved[0]
    right_side = moved[1]
    coefficient = moved[2]
    padded = extended(jnp.stack([pressure, coefficient]), (("grp", 1), ("dev", 2)), 1)
    padded = jnp.pad(padded, ((0, 0), (0, 0), (0, 0), (1, 1)))
    betas = [0.5 * (coefficient + neighbour) for neighbour in shifted_slices(padded[1])]
    beta_sum = betas[0]
    for beta in betas[1:]:
        beta_sum = beta_sum + beta
    shape = pressure.shape
    parity = (
        lax.broadcasted_iota(jnp.int32, shape, 0)
        + lax.broadcasted_iota(jnp.int32, shape, 1)
        + lax.broadcasted_iota(jnp.int32, shape, 2)
    ) % 2
    red_mask = parity == 0
    first = jnp.where(red_mask, (right_side + beta_phi(padded[0], betas)) / beta_sum, pressure)
    padded_first = extended(first, (("grp", 0), ("dev", 1)), 1)
    padded_first = jnp.pad(padded_first, ((0, 0), (0, 0), (1, 1)))
    second = jnp.where(red_mask, first, (right_side + beta_phi(padded_first, betas)) / beta_sum)
    padded_second = extended(second, (("grp", 0), ("dev", 1)), 1)
    padded_second = jnp.pad(padded_second, ((0, 0), (0, 0), (1, 1)))
    residual = right_side - (beta_sum * second - beta_phi(padded_second, betas))
    return (second, residual)


def solution(mesh):
    placed = (P(None, ("grp", "dev"), None, None), P())
    return jax.shard_map(
        per_device,
        mesh=mesh,
        in_specs=placed,
        out_specs=(P("grp", "dev", None), P("grp", "dev", None)),
        check_vma=False,
    )
```

profile of v0, /device:TPU:223, one launch (start us, length us, event | category | flops | bytes accessed | tf_op | source)
XLA Modules:
  0.0 174.6 jit_solution(4209563329145930393)
XLA Ops:
  0.6 4.3 %collective-permute-start = (f32[3,8,32,1024]{3,2,1,0:T(8,128)}, f32[3,8,32,1024]{3,2,1,0:T(8,128)}, u32[]{:S(2)}, u32[]{:S(2)}) collective-permute-start(f32[3,8,32,1024]{3,2,1,0:T(8,128)} %param.4), channel_id=1, source_target_pairs={{0,1},{1,2},{2,3},{3,4},{4,5},{5,6},{6,7},{7,8},{8,9},{9,10},{10,1... | collective-permute-start | bytes 9437192 | tf_op jit(solution)/shard_map/ppermute | solution.py:10
  8.9 2.5 %gather_fusion.2 = f32[4,3,32,1024]{3,2,1,0:T(8,128)S(1)} fusion(f32[3,8,32,1024]{3,2,1,0:T(8,128)} %param.4, s32[1024]{0:T(1024)S(1)} %pad_clamp_fusion), kind=kCustom, calls=%fused_computation.1.clone | custom fusion | bytes 3145744 | tf_op jit(solution)/shard_map/jit(_take)/gather | solution.py:58
  11.5 60.6 %collective-permute-done = f32[3,8,32,1024]{3,2,1,0:T(8,128)} collective-permute-done((f32[3,8,32,1024]{3,2,1,0:T(8,128)}, f32[3,8,32,1024]{3,2,1,0:T(8,128)}, u32[]{:S(2)}, u32[]{:S(2)}) %collective-permute-start) | collective-permute-done | bytes 3145760 | tf_op jit(solution)/shard_map/ppermute | solution.py:10
  72.0 2.5 %gather_fusion.1 = f32[4,3,32,1024]{3,2,1,0:T(8,128)S(1)} fusion(f32[3,8,32,1024]{3,2,1,0:T(8,128)} %collective-permute-done, s32[1024]{0:T(1024)S(1)} %pad_clamp_fusion), kind=kCustom, calls=%fused_computation.clone | custom fusion | bytes 3145744 | tf_op jit(solution)/shard_map/jit(_take)/gather | solution.py:57
  76.1 5.3 %reshape.65 = f32[3,4,32,32,32]{4,3,2,0,1:T(8,128)} reshape(f32[3,4,32,1024]{3,2,0,1:T(8,128)} %bitcast_select_fusion) | data formatting | bytes 3145728 | tf_op jit(solution)/shard_map/reshape | solution.py:60
  81.4 8.9 %copy.7 = f32[3,4,32,32,32]{4,1,3,2,0:T(4,128)S(1)} copy(f32[3,4,32,32,32]{4,3,2,0,1:T(8,128)} %reshape.65) | data formatting | bytes 3145728 | tf_op jit(solution)/shard_map/reshape | solution.py:60
  90.3 2.4 %fusion.44 = (f32[1,32,32,4,32]{4,3,2,1,0:T(4,128)}, f32[1,32,32,4,32]{4,3,2,1,0:T(4,128)S(1)}, f32[1,32,32,4,32]{4,3,2,1,0:T(4,128)}) fusion(f32[3,32,32,4,32]{4,3,2,1,0:T(4,128)S(1)} %bitcast.21), kind=kLoop, calls=%fused_computation.124 | loop fusion | bytes 3145728 | tf_op jit(solution)/shard_map/slice | solution.py:66
  92.7 2.4 %slice.91 = f32[1,32,32,128]{3,2,1,0:T(8,128)S(1)} reshape(f32[1,32,32,4,32]{4,3,2,1,0:T(4,128)} %get-tuple-element.5) | data formatting | bytes 1048576 | tf_op jit(solution)/shard_map/slice | solution.py:66
  96.2 6.6 %collective-permute-start.1 = (f32[2,1,32,128]{3,2,1,0:T(8,128)S(1)}, f32[2,1,32,128]{3,2,1,0:T(8,128)S(1)}, u32[]{:S(2)}, u32[]{:S(2)}) collective-permute-start(f32[2,1,32,128]{3,2,1,0:T(8,128)S(1)} %get-tuple-element.12), channel_id=1, source_target_pairs={{0,32},{32,64},{64,96},{96,128},{128,160},{160,192},{192,224},{224... | collective-permute-start | bytes 98312 | tf_op jit(solution)/shard_map/ppermute | solution.py:20
  104.7 4.5 %collective-permute-done.2 = f32[2,1,32,128]{3,2,1,0:T(8,128)S(1)} collective-permute-done((f32[2,1,32,128]{3,2,1,0:T(8,128)S(1)}, f32[2,1,32,128]{3,2,1,0:T(8,128)S(1)}, u32[]{:S(2)}, u32[]{:S(2)}) %collective-permute-start.2) | collective-permute-done | bytes 32800 | tf_op jit(solution)/shard_map/ppermute | solution.py:21
  109.3 7.4 %collective-permute-start.3 = (f32[2,34,1,128]{3,2,1,0:T(1,128)S(1)}, f32[2,34,1,128]{3,2,1,0:T(1,128)S(1)}, u32[]{:S(2)}, u32[]{:S(2)}) collective-permute-start(f32[2,34,1,128]{3,2,1,0:T(1,128)S(1)} %get-tuple-element.10), channel_id=1, source_target_pairs={{0,1},{1,2},{2,3},{3,4},{4,5},{5,6},{6,7},{7,8},{8,9},{9,10},{10,1... | collective-permute-start | bytes 104456 | tf_op jit(solution)/shard_map/ppermute | solution.py:20
  116.7 2.1 %collective-permute-start.4 = (f32[2,34,1,128]{3,2,1,0:T(1,128)S(1)}, f32[2,34,1,128]{3,2,1,0:T(1,128)S(1)}, u32[]{:S(2)}, u32[]{:S(2)}) collective-permute-start(f32[2,34,1,128]{3,2,1,0:T(1,128)S(1)} %get-tuple-element.11), channel_id=1, source_target_pairs={{1,0},{2,1},{3,2},{4,3},{5,4},{6,5},{7,6},{8,7},{9,8},{10,9},{11,1... | collective-permute-start | bytes 104456 | tf_op jit(solution)/shard_map/ppermute | solution.py:21
  118.8 2.4 %squeeze.20 = f32[32,32,128]{2,1,0:T(8,128)S(1)} reshape(f32[1,32,32,4,32]{4,3,2,1,0:T(4,128)} %get-tuple-element.5) | data formatting | bytes 1048576 | tf_op jit(solution)/shard_map/squeeze | solution.py:66
  122.2 2.5 %squeeze.19 = f32[32,32,128]{2,1,0:T(8,128)S(1)} reshape(f32[1,32,32,4,32]{4,3,2,1,0:T(4,128)} %get-tuple-element.7) | data formatting | bytes 1048576 | tf_op jit(solution)/shard_map/squeeze | solution.py:65
  127.5 3.3 %collective-permute-start.5 = (f32[1,32,128]{2,1,0:T(8,128)S(1)}, f32[1,32,128]{2,1,0:T(8,128)S(1)}, u32[]{:S(2)}, u32[]{:S(2)}) collective-permute-start(f32[1,32,128]{2,1,0:T(8,128)S(1)} %get-tuple-element.20), channel_id=1, source_target_pairs={{0,32},{32,64},{64,96},{96,128},{128,160},{160,192},{192,224},{224... | collective-permute-start | bytes 49160 | tf_op jit(solution)/shard_map/ppermute | solution.py:20
  132.8 4.3 %collective-permute-done.6 = f32[1,32,128]{2,1,0:T(8,128)S(1)} collective-permute-done((f32[1,32,128]{2,1,0:T(8,128)S(1)}, f32[1,32,128]{2,1,0:T(8,128)S(1)}, u32[]{:S(2)}, u32[]{:S(2)}) %collective-permute-start.6) | collective-permute-done | bytes 16416 | tf_op jit(solution)/shard_map/ppermute | solution.py:21
  137.2 5.8 %collective-permute-start.7 = (f32[34,1,128]{2,1,0:T(1,128)S(1)}, f32[34,1,128]{2,1,0:T(1,128)S(1)}, u32[]{:S(2)}, u32[]{:S(2)}) collective-permute-start(f32[34,1,128]{2,1,0:T(1,128)S(1)} %get-tuple-element.16), channel_id=1, source_target_pairs={{0,1},{1,2},{2,3},{3,4},{4,5},{5,6},{6,7},{7,8},{8,9},{9,10},{10,1... | collective-permute-start | bytes 52232 | tf_op jit(solution)/shard_map/ppermute | solution.py:20
  144.9 5.9 %collective-permute-done.8 = f32[34,1,128]{2,1,0:T(1,128)S(1)} collective-permute-done((f32[34,1,128]{2,1,0:T(1,128)S(1)}, f32[34,1,128]{2,1,0:T(1,128)S(1)}, u32[]{:S(2)}, u32[]{:S(2)}) %collective-permute-start.8) | collective-permute-done | bytes 17440 | tf_op jit(solution)/shard_map/ppermute | solution.py:21
  152.7 3.4 %collective-permute-start.9 = (f32[1,32,128]{2,1,0:T(8,128)S(1)}, f32[1,32,128]{2,1,0:T(8,128)S(1)}, u32[]{:S(2)}, u32[]{:S(2)}) collective-permute-start(f32[1,32,128]{2,1,0:T(8,128)S(1)} %get-tuple-element.18), channel_id=1, source_target_pairs={{0,32},{32,64},{64,96},{96,128},{128,160},{160,192},{192,224},{224... | collective-permute-start | bytes 49160 | tf_op jit(solution)/shard_map/ppermute | solution.py:20
  156.1 1.9 %collective-permute-start.10 = (f32[1,32,128]{2,1,0:T(8,128)S(1)}, f32[1,32,128]{2,1,0:T(8,128)S(1)}, u32[]{:S(2)}, u32[]{:S(2)}) collective-permute-start(f32[1,32,128]{2,1,0:T(8,128)S(1)} %get-tuple-element.19), channel_id=1, source_target_pairs={{32,0},{64,32},{96,64},{128,96},{160,128},{192,160},{224,192},{256... | collective-permute-start | bytes 49160 | tf_op jit(solution)/shard_map/ppermute | solution.py:21
  158.0 4.3 %collective-permute-done.10 = f32[1,32,128]{2,1,0:T(8,128)S(1)} collective-permute-done((f32[1,32,128]{2,1,0:T(8,128)S(1)}, f32[1,32,128]{2,1,0:T(8,128)S(1)}, u32[]{:S(2)}, u32[]{:S(2)}) %collective-permute-start.10) | collective-permute-done | bytes 16416 | tf_op jit(solution)/shard_map/ppermute | solution.py:21
  164.3 3.4 %collective-permute-start.12 = (f32[34,1,128]{2,1,0:T(1,128)S(1)}, f32[34,1,128]{2,1,0:T(1,128)S(1)}, u32[]{:S(2)}, u32[]{:S(2)}) collective-permute-start(f32[34,1,128]{2,1,0:T(1,128)S(1)} %get-tuple-element.15), channel_id=1, source_target_pairs={{1,0},{2,1},{3,2},{4,3},{5,4},{6,5},{7,6},{8,7},{9,8},{10,9},{11,1... | collective-permute-start | bytes 52232 | tf_op jit(solution)/shard_map/ppermute | solution.py:21
  167.7 4.4 %collective-permute-done.12 = f32[34,1,128]{2,1,0:T(1,128)S(1)} collective-permute-done((f32[34,1,128]{2,1,0:T(1,128)S(1)}, f32[34,1,128]{2,1,0:T(1,128)S(1)}, u32[]{:S(2)}, u32[]{:S(2)}) %collective-permute-start.12) | collective-permute-done | bytes 17440 | tf_op jit(solution)/shard_map/ppermute | solution.py:21
  172.7 1.9 %fusion.6 = f32[32,32,128]{2,1,0:T(8,128)} fusion(f32[32,32,128]{2,1,0:T(8,128)S(1)} %squeeze.19, f32[34,34,130]{2,1,0:T(8,128)S(1)} %select_maximum_fusion.4, f32[34,1,128]{2,1,0:T(1,128)S(1)} %collective-permute-done.12, f32[1,32,128]{2,1,0:T(8,128)S(1)} %collective-permute-done.10, f32[32,32,128]{2,1,0:T(8,128)S(1)} %fusion.18, ...), kind=kLoop, calls=%fused_computation.33 | loop fusion | flops 5111808 | bytes 6359040 | tf_op jit(solution)/shard_map/sub | solution.py:86
  (46 shorter events, 20.3 us)
Async XLA Ops:
  0.6 71.4 %collective-permute-start = (f32[3,8,32,1024]{3,2,1,0:T(8,128)}, f32[3,8,32,1024]{3,2,1,0:T(8,128)}, u32[]{:S(2)}, u32[]{:S(2)}) collective-permute-start(f32[3,8,32,1024]{3,2,1,0:T(8,128)} %param.4), channel_id=1, source_target_pairs={{0,1},{1,2},{2,3},{3,4},{4,5},{5,6},{6,7},{7,8},{8,9},{9,10},{10,1... | collective-permute-start | bytes 9437192 | tf_op jit(solution)/shard_map/ppermute | solution.py:10
  96.1 20.6 %copy-start.1 = (f32[2,32,32,128]{3,2,1,0:T(8,128)}, f32[2,32,32,128]{3,2,1,0:T(8,128)S(1)}, u32[]{:S(2)}) copy-start(f32[2,32,32,128]{3,2,1,0:T(8,128)S(1)} %constant_dynamic-update-slice_fusion) | copy-start | bytes 3145732
  96.2 8.6 %collective-permute-start.1 = (f32[2,1,32,128]{3,2,1,0:T(8,128)S(1)}, f32[2,1,32,128]{3,2,1,0:T(8,128)S(1)}, u32[]{:S(2)}, u32[]{:S(2)}) collective-permute-start(f32[2,1,32,128]{3,2,1,0:T(8,128)S(1)} %get-tuple-element.12), channel_id=1, source_target_pairs={{0,32},{32,64},{64,96},{96,128},{128,160},{160,192},{192,224},{224... | collective-permute-start | bytes 98312 | tf_op jit(solution)/shard_map/ppermute | solution.py:20
  102.8 6.4 %collective-permute-start.2 = (f32[2,1,32,128]{3,2,1,0:T(8,128)S(1)}, f32[2,1,32,128]{3,2,1,0:T(8,128)S(1)}, u32[]{:S(2)}, u32[]{:S(2)}) collective-permute-start(f32[2,1,32,128]{3,2,1,0:T(8,128)S(1)} %get-tuple-element.13), channel_id=1, source_target_pairs={{32,0},{64,32},{96,64},{128,96},{160,128},{192,160},{224,192},{256... | collective-permute-start | bytes 98312 | tf_op jit(solution)/shard_map/ppermute | solution.py:21
  109.3 15.4 %collective-permute-start.3 = (f32[2,34,1,128]{3,2,1,0:T(1,128)S(1)}, f32[2,34,1,128]{3,2,1,0:T(1,128)S(1)}, u32[]{:S(2)}, u32[]{:S(2)}) collective-permute-start(f32[2,34,1,128]{3,2,1,0:T(1,128)S(1)} %get-tuple-element.10), channel_id=1, source_target_pairs={{0,1},{1,2},{2,3},{3,4},{4,5},{5,6},{6,7},{7,8},{8,9},{9,10},{10,1... | collective-permute-start | bytes 104456 | tf_op jit(solution)/shard_map/ppermute | solution.py:20
  116.7 8.0 %collective-permute-start.4 = (f32[2,34,1,128]{3,2,1,0:T(1,128)S(1)}, f32[2,34,1,128]{3,2,1,0:T(1,128)S(1)}, u32[]{:S(2)}, u32[]{:S(2)}) collective-permute-start(f32[2,34,1,128]{3,2,1,0:T(1,128)S(1)} %get-tuple-element.11), channel_id=1, source_target_pairs={{1,0},{2,1},{3,2},{4,3},{5,4},{6,5},{7,6},{8,7},{9,8},{10,9},{11,1... | collective-permute-start | bytes 104456 | tf_op jit(solution)/shard_map/ppermute | solution.py:21
  122.2 2.6 %copy-start.2 = (f32[2,32,32,128]{3,2,1,0:T(8,128)S(1)}, f32[2,32,32,128]{3,2,1,0:T(8,128)}, u32[]{:S(2)}) copy-start(f32[2,32,32,128]{3,2,1,0:T(8,128)} %copy-done.1) | copy-start | bytes 3145732
  127.5 5.3 %collective-permute-start.5 = (f32[1,32,128]{2,1,0:T(8,128)S(1)}, f32[1,32,128]{2,1,0:T(8,128)S(1)}, u32[]{:S(2)}, u32[]{:S(2)}) collective-permute-start(f32[1,32,128]{2,1,0:T(8,128)S(1)} %get-tuple-element.20), channel_id=1, source_target_pairs={{0,32},{32,64},{64,96},{96,128},{128,160},{160,192},{192,224},{224... | collective-permute-start | bytes 49160 | tf_op jit(solution)/shard_map/ppermute | solution.py:20
  130.9 6.3 %collective-permute-start.6 = (f32[1,32,128]{2,1,0:T(8,128)S(1)}, f32[1,32,128]{2,1,0:T(8,128)S(1)}, u32[]{:S(2)}, u32[]{:S(2)}) collective-permute-start(f32[1,32,128]{2,1,0:T(8,128)S(1)} %get-tuple-element.21), channel_id=1, source_target_pairs={{32,0},{64,32},{96,64},{128,96},{160,128},{192,160},{224,192},{256... | collective-permute-start | bytes 49160 | tf_op jit(solution)/shard_map/ppermute | solution.py:21
  137.2 7.8 %collective-permute-start.7 = (f32[34,1,128]{2,1,0:T(1,128)S(1)}, f32[34,1,128]{2,1,0:T(1,128)S(1)}, u32[]{:S(2)}, u32[]{:S(2)}) collective-permute-start(f32[34,1,128]{2,1,0:T(1,128)S(1)} %get-tuple-element.16), channel_id=1, source_target_pairs={{0,1},{1,2},{2,3},{3,4},{4,5},{5,6},{6,7},{7,8},{8,9},{9,10},{10,1... | collective-permute-start | bytes 52232 | tf_op jit(solution)/shard_map/ppermute | solution.py:20
  143.0 7.8 %collective-permute-start.8 = (f32[34,1,128]{2,1,0:T(1,128)S(1)}, f32[34,1,128]{2,1,0:T(1,128)S(1)}, u32[]{:S(2)}, u32[]{:S(2)}) collective-permute-start(f32[34,1,128]{2,1,0:T(1,128)S(1)} %get-tuple-element.17), channel_id=1, source_target_pairs={{1,0},{2,1},{3,2},{4,3},{5,4},{6,5},{7,6},{8,7},{9,8},{10,9},{11,1... | collective-permute-start | bytes 52232 | tf_op jit(solution)/shard_map/ppermute | solution.py:21
  152.7 22.0 %copy-start = (f32[32,32,128]{2,1,0:T(8,128)}, f32[32,32,128]{2,1,0:T(8,128)S(1)}, u32[]{:S(2)}) copy-start(f32[32,32,128]{2,1,0:T(8,128)S(1)} %fusion.18) | copy-start | bytes 1572868
  152.7 5.3 %collective-permute-start.9 = (f32[1,32,128]{2,1,0:T(8,128)S(1)}, f32[1,32,128]{2,1,0:T(8,128)S(1)}, u32[]{:S(2)}, u32[]{:S(2)}) collective-permute-start(f32[1,32,128]{2,1,0:T(8,128)S(1)} %get-tuple-element.18), channel_id=1, source_target_pairs={{0,32},{32,64},{64,96},{96,128},{128,160},{160,192},{192,224},{224... | collective-permute-start | bytes 49160 | tf_op jit(solution)/shard_map/ppermute | solution.py:20
  156.1 6.3 %collective-permute-start.10 = (f32[1,32,128]{2,1,0:T(8,128)S(1)}, f32[1,32,128]{2,1,0:T(8,128)S(1)}, u32[]{:S(2)}, u32[]{:S(2)}) collective-permute-start(f32[1,32,128]{2,1,0:T(8,128)S(1)} %get-tuple-element.19), channel_id=1, source_target_pairs={{32,0},{64,32},{96,64},{128,96},{160,128},{192,160},{224,192},{256... | collective-permute-start | bytes 49160 | tf_op jit(solution)/shard_map/ppermute | solution.py:21
  162.4 5.3 %collective-permute-start.11 = (f32[34,1,128]{2,1,0:T(1,128)S(1)}, f32[34,1,128]{2,1,0:T(1,128)S(1)}, u32[]{:S(2)}, u32[]{:S(2)}) collective-permute-start(f32[34,1,128]{2,1,0:T(1,128)S(1)} %get-tuple-element.14), channel_id=1, source_target_pairs={{0,1},{1,2},{2,3},{3,4},{4,5},{5,6},{6,7},{7,8},{8,9},{9,10},{10,1... | collective-permute-start | bytes 52232 | tf_op jit(solution)/shard_map/ppermute | solution.py:20
  164.3 7.8 %collective-permute-start.12 = (f32[34,1,128]{2,1,0:T(1,128)S(1)}, f32[34,1,128]{2,1,0:T(1,128)S(1)}, u32[]{:S(2)}, u32[]{:S(2)}) collective-permute-start(f32[34,1,128]{2,1,0:T(1,128)S(1)} %get-tuple-element.15), channel_id=1, source_target_pairs={{1,0},{2,1},{3,2},{4,3},{5,4},{6,5},{7,6},{8,7},{9,8},{10,9},{11,1... | collective-permute-start | bytes 52232 | tf_op jit(solution)/shard_map/ppermute | solution.py:21
where the time goes:
time: 175 us
  waiting for transfers between devices  84.1 us (48%)
  starting transfers between devices  46 us (26%)
  local copies, waits for them, and re-layouts  32.5 us (19%)
  other arithmetic  11 us (6%)
    ppermute x1, waiting for transfers between devices, from_behind(): lax.ppermute(value, axis, [(source, source + steps) for source in range(l...  60.6 us
    ppermute x6, starting transfers between devices, extended(): before = lax.ppermute(last, axis, up)  28.5 us
    ppermute x6, waiting for transfers between devices, extended(): after = lax.ppermute(leading, axis, down)  23.5 us
    reshape x2, local copies, waits for them, and re-layouts, per_device(): moved = moved.reshape(3, box_count, box_edge, box_edge, box_edge)  14.2 us
    ppermute x6, starting transfers between devices, extended(): after = lax.ppermute(leading, axis, down)  13.1 us
    slice x2, local copies, waits for them, and re-layouts, per_device(): coefficient = moved[2]  4.82 us
    ppermute x1, starting transfers between devices, from_behind(): lax.ppermute(value, axis, [(source, source + steps) for source in range(l...  4.33 us
  transfers between devices with their start and end apart: 13, of which 6 were waited for; matrix products, arithmetic and copies ran while one was open for 7% of the time, Pallas kernels for 0%

commit v1 on v0

v1 whole, which is shorter than its diff:
```python
import jax
import jax.numpy as jnp
from jax import lax
from jax.experimental import pallas as pl
from jax.experimental.pallas import tpu as pltpu
from jax.sharding import PartitionSpec as P

EDGE = 32
LANES = 128
GROUPS = EDGE * EDGE // LANES
COLUMN = 4
FIELDS = 3
MOVED = 2
KINDS = 5
SHELL = GROUPS + 6
CORE = 3 * (GROUPS - 2)
TALL = EDGE + 8
SLABS = EDGE + 6
XMSG = EDGE + 4
F32 = jnp.float32
VMEM = pltpu.VMEM


def iota(shape, dim):
    return lax.broadcasted_iota(jnp.int32, shape, dim)


def moved_boxes(counts_ref):
    device = lax.axis_index("grp") * lax.axis_size("dev") + lax.axis_index("dev")
    counts = counts_ref[...]
    index = iota(counts.shape, 0) * LANES + iota(counts.shape, 1)
    start = jnp.sum(jnp.where(index < device, counts, 0))
    return jnp.clip(start - device * COLUMN, 0, MOVED)


def lane_group(g):
    return pl.ds(g * LANES, LANES)


def fetch_moved(old_ref, boxes, sems, moved):
    copies = []
    for f in range(FIELDS):
        for c in range(MOVED):
            copies.append(pltpu.make_async_copy(old_ref.at[f, COLUMN + c - moved], boxes.at[f, c], sems.at[f, c]))
    for copy in copies:
        copy.start()
    for copy in copies:
        copy.wait()


def box_tiles(boxes, f, c, g, which):
    low = iota((8, LANES), 0) < 4
    if which == "edge":
        return jnp.where(low, boxes[f, c, 0:8, lane_group(g)], boxes[f, c, 24:32, lane_group(g)])
    if which == 0:
        return jnp.where(low, boxes[f, c, 24:32, lane_group(g)], boxes[f, c, 0:8, lane_group(g)])
    return boxes[f, c, 8 * which : 8 * which + 8, lane_group(g)]


def pack(boxes, out, at, g, which):
    shape = (8, LANES)
    lane = iota(shape, 1)
    block = lane // EDGE
    black = (iota(shape, 0) + block + lane) % 2 == 1
    even = block % 2 == 0
    first, second = [[box_tiles(boxes, f, c, g, which) for f in range(FIELDS)] for c in range(MOVED)]
    turned = [pltpu.roll(v, EDGE, 1) for v in second]
    out[0, at] = jnp.where(black, first[0], turned[0])
    for f in (1, 2):
        out[2 * f - 1, at] = jnp.where(even, first[f], turned[f])
        out[2 * f, at] = jnp.where(even, turned[f], first[f])


def pack_shell(counts_ref, old_ref, out, boxes, sems):
    fetch_moved(old_ref, boxes, sems, moved_boxes(counts_ref))
    for g in range(GROUPS):
        pack(boxes, out, g, g, "edge")
    for side, g in enumerate((0, GROUPS - 1)):
        for which in range(3):
            pack(boxes, out, GROUPS + 3 * side + which, g, which)


def pack_core(counts_ref, old_ref, out, boxes, sems):
    fetch_moved(old_ref, boxes, sems, moved_boxes(counts_ref))
    for g in range(1, GROUPS - 1):
        for which in range(3):
            pack(boxes, out, 3 * (g - 1) + which, g, which)


def relayout(counts_ref, old_ref, out, edge_out, boxes, sems):
    moved = moved_boxes(counts_ref)
    copies = []
    for f in range(FIELDS):
        for c in range(COLUMN):
            slot = jnp.maximum(c - moved, 0)
            copies.append(pltpu.make_async_copy(old_ref.at[f, slot], boxes.at[f, c], sems.at[f, c]))
    for copy in copies:
        copy.start()
    lane = iota((EDGE, LANES), 1)
    half = lane < 2 * EDGE
    even = (lane // EDGE) % 2 == 0
    low = iota((8, LANES), 0) < 4
    for f in range(FIELDS):
        for c in range(COLUMN):
            copies[f * COLUMN + c].wait()
        for g in range(GROUPS):
            v = [boxes[f, c, :, lane_group(g)] for c in range(COLUMN)]
            w = [pltpu.roll(a, 2 * EDGE, 1) for a in v]
            a0, a1 = jnp.where(half, v[0], w[2]), jnp.where(half, v[1], w[3])
            a2, a3 = jnp.where(half, w[0], v[2]), jnp.where(half, w[1], v[3])
            rows = []
            for a, b in ((a0, a1), (a2, a3)):
                rows.append(jnp.where(even, a, pltpu.roll(b, EDGE, 1)))
                rows.append(jnp.where(even, pltpu.roll(a, LANES - EDGE, 1), b))
            for r, row in enumerate(rows):
                out[f, 4 * g + r] = row
                edge_out[f, 4 * g + r] = jnp.where(low, row[0:8], row[24:32])


def unmix(kinds, f):
    if f == 0:
        a = b = kinds[0]
    else:
        a, b = kinds[2 * f - 1], kinds[2 * f]
    return [a, pltpu.roll(b, LANES - EDGE, 1), pltpu.roll(a, 2 * EDGE, 1), pltpu.roll(b, EDGE, 1)]


def wire_rows(shell, core, k, g):
    low = iota((8, LANES), 0) < 4
    edge = shell[k, g]
    if g in (0, GROUPS - 1):
        base = GROUPS + (3 if g else 0)
        mid = [shell[k, base + which] for which in range(3)]
    else:
        mid = [core[k, 3 * (g - 1) + which] for which in range(3)]
    return jnp.concatenate([jnp.where(low, edge, mid[0]), mid[1], mid[2], jnp.where(low, mid[0], edge)], axis=0)


def pack_x(pressure, right_side, coefficient):
    row = iota((8, LANES), 0)
    high = jnp.where(
        row >= 5, coefficient, jnp.where(row >= 2, pltpu.roll(pressure, 5, 0), pltpu.roll(right_side, 2, 0))
    )
    low = jnp.where(
        row < 3, coefficient, jnp.where(row < 6, pltpu.roll(pressure, 3, 0), pltpu.roll(right_side, 6, 0))
    )
    return high, low


def make_faces(counts_ref, shell, own, own_edge, y_up, y_down, x_up, x_down, slabs, sems):
    copies = []
    for f in range(FIELDS):
        for side in range(2):
            copies.append(pltpu.make_async_copy(own.at[f, pl.ds(28 * side, 4)], slabs.at[f, side], sems.at[f, side]))
    for copy in copies:
        copy.start()
    limit = moved_boxes(counts_ref) * EDGE
    taken = iota((8, LANES), 1) < limit
    for g in range(GROUPS):
        kinds = [shell[k, g] for k in range(KINDS)]
        rows = [unmix(kinds, f) for f in range(FIELDS)]
        for r in range(4):
            y = 4 * g + r
            edge = [jnp.where(taken, rows[f][r], own_edge[f, y]) for f in range(FIELDS)]
            x_up[y + 2], x_down[y + 2] = pack_x(*edge)
    for copy in copies:
        copy.wait()
    taken = iota((EDGE, LANES), 1) < limit
    for side, g in enumerate((0, GROUPS - 1)):
        out = y_up if side else y_down
        kinds = [wire_rows(shell, None, k, g) for k in range(KINDS)]
        for f, at, depth in ((2, 0, 3), (0, 3, 3), (1, 6, 2)):
            rows = unmix(kinds, f)
            for j in range(depth):
                r = 4 - depth + j if side else j
                out[at + j] = jnp.where(taken, rows[r], slabs[f, side, r])


def add_corners(before, after, x_up_in, x_down_in, x_up, x_down, tiles, sems):
    del x_up_in, x_down_in
    low = iota((8, LANES), 0) < 4
    places = ((before, 1, 4, 6), (before, 2, 5, 7), (after, 0, 3, 6), (after, 1, 4, 7))
    for at, (ref, b, p, f) in enumerate(places):
        edge = [jnp.where(low, ref[i, 0:8], ref[i, 24:32]) for i in (p, f, b)]
        tiles[0, at], tiles[1, at] = pack_x(*edge)
    copies = []
    for way, out in enumerate((x_up, x_down)):
        for side in range(2):
            copies.append(
                pltpu.make_async_copy(
                    tiles.at[way, pl.ds(2 * side, 2)], out.at[pl.ds((XMSG - 2) * side, 2)], sems.at[way, side]
                )
            )
    for copy in copies:
        copy.start()
    for copy in copies:
        copy.wait()


def plane_sum(value):
    lane = iota(value.shape, 1)
    rows = value.shape[0]
    below = jnp.where(lane == 0, 0.0, pltpu.roll(value, 1, 1))
    above = jnp.where(lane == LANES - 1, 0.0, pltpu.roll(value, LANES - 1, 1))
    return (pltpu.roll(value, 1, 0) + pltpu.roll(value, rows - 1, 0)) + (below + above)


def sweep(counts_ref, own, shell, core, y_before, y_after, x_before, x_after, out_p, out_r, prs, rhs, cof, mid, tot, inv):
    grp, dev = lax.axis_index("grp"), lax.axis_index("dev")
    limit = moved_boxes(counts_ref) * EDGE
    taken = iota((EDGE, LANES), 1) < limit
    fields = (prs, rhs, cof)
    for g in range(GROUPS):
        kinds = [wire_rows(shell, core, k, g) for k in range(KINDS)]
        for f, ref in enumerate(fields):
            rows = unmix(kinds, f)
            for r in range(4):
                y = 4 * g + r
                ref[y + 3, 0:EDGE] = jnp.where(taken, rows[r], own[f, y])
    for j in range(3):
        cof[j, 0:EDGE] = y_before[j]
        prs[j, 0:EDGE] = y_before[3 + j]
        cof[EDGE + 3 + j, 0:EDGE] = y_after[j]
        prs[EDGE + 3 + j, 0:EDGE] = y_after[3 + j]
    for j in range(2):
        rhs[1 + j, 0:EDGE] = y_before[6 + j]
        rhs[EDGE + 3 + j, 0:EDGE] = y_after[6 + j]
    row8 = iota((8, LANES), 0)
    zero = jnp.zeros((8, LANES), F32)
    for ref in fields:
        ref[0, EDGE:TALL] = zero
        ref[SLABS - 1, EDGE:TALL] = zero

    def halo(i, carry):
        low, high = x_before[i], x_after[i]
        at = i + 1
        cof[at, EDGE:TALL] = jnp.where(row8 < 4, high, low)
        prs[at, EDGE:TALL] = jnp.where(row8 < 4, pltpu.roll(high, 5, 0), pltpu.roll(low, 3, 0))
        rhs[at, EDGE:TALL] = jnp.where(row8 < 4, pltpu.roll(high, 2, 0), pltpu.roll(low, 6, 0))
        return carry

    lax.fori_loop(0, XMSG, halo, 0)

    shape = (TALL, LANES)
    row, lane = iota(shape, 0), iota(shape, 1)
    base = row + lane
    near = (row >= EDGE) & (row < EDGE + 4)
    far = row >= EDGE + 4
    has_after = (grp < lax.axis_size("grp") - 1).astype(jnp.int32)
    has_before = (grp > 0).astype(jnp.int32)
    inside_x = jnp.where(near, has_after, jnp.where(far, has_before, 1))
    y_low = (dev > 0).astype(jnp.int32)
    y_high = (dev < lax.axis_size("dev") - 1).astype(jnp.int32)

    def colour(at, which):
        y_ok = jnp.where(at < 3, y_low, jnp.where(at >= EDGE + 3, y_high, 1))
        return ((base + at + which) % 2) * inside_x * y_ok > 0

    def flows(ref, at):
        b, p, pm, pp = cof[at], ref[at], ref[at - 1], ref[at + 1]
        near_p = plane_sum(p) + (pm + pp)
        near_q = plane_sum(b * p) + (cof[at - 1] * pm + cof[at + 1] * pp)
        return p, 0.5 * (b * near_p + near_q)

    def red(at, carry):
        b = cof[at]
        total = 3.0 * b + 0.5 * (plane_sum(b) + (cof[at - 1] + cof[at + 1]))
        inverse = 1.0 / total
        tot[at] = total
        inv[at] = inverse
        p, flow = flows(prs, at)
        mid[at] = jnp.where(colour(at, 0), (rhs[at] + flow) * inverse, p)
        return carry

    def black(at, carry):
        p, flow = flows(mid, at)
        prs[at] = jnp.where(colour(at, 1), (rhs[at] + flow) * inv[at], p)
        return carry

    def finish(at, carry):
        p, flow = flows(prs, at)
        rest = rhs[at] - (tot[at] * p - flow)
        rows = pl.ds(at - 3, EDGE, stride=EDGE)
        out_p[rows, :] = p[0:EDGE]
        out_r[rows, :] = rest[0:EDGE]
        return carry

    lax.fori_loop(1, SLABS - 1, red, 0)
    lax.fori_loop(2, SLABS - 2, black, 0)
    lax.fori_loop(3, SLABS - 3, finish, 0)


def call(body, inputs, outputs, scratch, flops, moved, aliases=None, anywhere=(), out_anywhere=False):
    vmem, place = pl.BlockSpec(memory_space=pltpu.VMEM), pl.BlockSpec(memory_space=pl.ANY)
    hbm = pl.BlockSpec(memory_space=pltpu.HBM)
    out_specs = [place if out_anywhere else vmem for _ in outputs]
    out_shape = [jax.ShapeDtypeStruct(shape, F32) for shape in outputs]
    return pl.pallas_call(
        body,
        out_shape=out_shape,
        in_specs=[hbm if x.ndim == 4 and x.shape[1] == 2 * COLUMN else place if i in anywhere else vmem for i, x in enumerate(inputs)],
        out_specs=out_specs,
        scratch_shapes=scratch,
        input_output_aliases=aliases or {},
        cost_estimate=pl.CostEstimate(flops=flops, bytes_accessed=moved, transcendentals=0),
        compiler_params=pltpu.CompilerParams(vmem_limit_bytes=40 * 2**20),
        name=body.__name__,
    )(*inputs)


def per_device(old_fields, old_counts):
    groups, columns = lax.axis_size("grp"), lax.axis_size("dev")
    devices = groups * columns
    counts = jnp.pad(old_counts, (0, -devices % LANES)).reshape(-1, LANES)
    chain = [(i, i + 1) for i in range(devices - 1)]

    def ends(count):
        up = [(i, i + 1) for i in range(count - 1)]
        return up, [(j, i) for i, j in up]

    y_ways, x_ways = ends(columns), ends(groups)
    pair = [VMEM((FIELDS, MOVED, EDGE, EDGE * EDGE), F32), pltpu.SemaphoreType.DMA((FIELDS, MOVED))]
    (shell,) = call(pack_shell, (counts, old_fields), [(KINDS, SHELL, 8, LANES)], pair, 10**6, 2 * 10**6, anywhere=(1,))
    shell = lax.ppermute(shell, ("grp", "dev"), chain)
    (core,) = call(pack_core, (counts, old_fields), [(KINDS, CORE, 8, LANES)], pair, 10**6, 2 * 10**6, anywhere=(1,))
    core = lax.ppermute(core, ("grp", "dev"), chain)
    own, own_edge = call(
        relayout,
        (counts, old_fields),
        [(FIELDS, EDGE, EDGE, LANES), (FIELDS, EDGE, 8, LANES)],
        [VMEM((FIELDS, COLUMN, EDGE, EDGE * EDGE), F32), pltpu.SemaphoreType.DMA((FIELDS, COLUMN))],
        10**6,
        4 * 10**6,
        anywhere=(1,),
    )
    face, strip = (8, EDGE, LANES), (XMSG, 8, LANES)
    y_up, y_down, x_up, x_down = call(
        make_faces,
        (counts, shell, own, own_edge),
        [face, face, strip, strip],
        [VMEM((FIELDS, 2, 4, EDGE, LANES), F32), pltpu.SemaphoreType.DMA((FIELDS, 2))],
        10**6,
        10**6,
        anywhere=(2,),
    )
    y_before = lax.ppermute(y_up, "dev", y_ways[0])
    y_after = lax.ppermute(y_down, "dev", y_ways[1])
    x_up, x_down = call(
        add_corners,
        (y_before, y_after, x_up, x_down),
        [strip, strip],
        [VMEM((2, 4, 8, LANES), F32), pltpu.SemaphoreType.DMA((2, 2))],
        10**4,
        10**5,
        aliases={2: 0, 3: 1},
        anywhere=(2, 3),
        out_anywhere=True,
    )
    x_before = lax.ppermute(x_up, "grp", x_ways[0])
    x_after = lax.ppermute(x_down, "grp", x_ways[1])
    tall = VMEM((SLABS, TALL, LANES), F32)
    flat = (EDGE * EDGE, LANES)
    outs = call(
        sweep,
        (counts, own, shell, core, y_before, y_after, x_before, x_after),
        [flat, flat],
        [tall] * 6,
        10**8,
        5 * 10**6,
    )
    return tuple(out.reshape(EDGE, EDGE, LANES) for out in outs)


def solution(mesh):
    placed = (P(None, ("grp", "dev"), None, None), P())
    return jax.shard_map(
        per_device,
        mesh=mesh,
        in_specs=placed,
        out_specs=(P("grp", "dev", None), P("grp", "dev", None)),
        check_vma=False,
    )
```

time: 175 us -> 61.6 us (0.35)
  waiting for transfers between devices: 84.1 us -> 12.8 us
  local copies, waits for them, and re-layouts: 32.5 us -> 2.56 us
  starting transfers between devices: 46 us -> 24.6 us
  Pallas kernels: 0 us -> 20.6 us
  other arithmetic: 11 us -> 0 us
    ppermute x13 -> x6, waiting for transfers between devices: 84.1 us -> 12.8 us  [the longest x1 6.9 us: per_device(): y_after = lax.ppermute(y_down, 'dev', y_ways[1])]
    ppermute x13 -> x6, starting transfers between devices: 46 us -> 24.6 us  [the longest x1 9.19 us: per_device(): x_before = lax.ppermute(x_up, 'grp', x_ways[0])]
    pallas_call x0 -> x6, Pallas kernels: none -> 20.6 us  [call(): pl.pallas_call(body, out_shape=out_shape, in_specs=[hbm if x.ndim == 4 an...]
    reshape x2 -> x0, local copies, waits for them, and re-layouts: 14.2 us -> none  [per_device(): moved = moved.reshape(3, box_count, box_edge, box_edge, box_edge)]
    squeeze x4 -> x0, local copies, waits for them, and re-layouts: 6.02 us -> none  [the longest x1 2.52 us: per_device(): right_side = moved[1]]
    slice x7 -> x0, local copies, waits for them, and re-layouts: 5.79 us -> none  [the longest x2 4.82 us: per_device(): coefficient = moved[2]]
    gather x3 -> x0, local copies, waits for them, and re-layouts: 5.7 us -> none  [the longest x1 2.54 us: per_device(): jnp.take(old_fields, jnp.clip(local_slot, 0, slot_count - 1), axis=1)]
    select_n x4 -> x0, other arithmetic: 4.89 us -> none  [the longest x1 1.52 us: per_device(): moved = jnp.where(is_below[None, :, None, None], lower_rows, own_rows)]
  transfers between devices with their start and end apart: 13 -> 6, of which waited for: 6 -> 4; matrix products, arithmetic and copies ran while one was open for 7% -> 0% of each run, Pallas kernels for 0% -> 11%
where the time goes in v1:
time: 61.6 us; the launch traced here: 61.3 us
  starting transfers between devices  24.6 us (40%)
  Pallas kernels  20.6 us (33%)
  waiting for transfers between devices  12.8 us (21%)
  local copies, waits for them, and re-layouts  2.56 us (4%)
  between operations  0.74 us (1%)
    pallas_call x6, Pallas kernels, call(): pl.pallas_call(body, out_shape=out_shape, in_specs=[hbm if x.ndim == 4 an...  20.6 us
    ppermute x1, starting transfers between devices, per_device(): x_before = lax.ppermute(x_up, 'grp', x_ways[0])  9.19 us
    ppermute x1, waiting for transfers between devices, per_device(): y_after = lax.ppermute(y_down, 'dev', y_ways[1])  6.9 us
    ppermute x1, waiting for transfers between devices, per_device(): x_after = lax.ppermute(x_down, 'grp', x_ways[1])  5.59 us
    ppermute x1, starting transfers between devices, per_device(): shell = lax.ppermute(shell, ('grp', 'dev'), chain)  4.33 us
    ppermute x1, starting transfers between devices, per_device(): y_before = lax.ppermute(y_up, 'dev', y_ways[0])  4.08 us
    ppermute x1, starting transfers between devices, per_device(): core = lax.ppermute(core, ('grp', 'dev'), chain)  3.12 us
    unnamed x4, local copies, waits for them, and re-layouts  2.56 us
  transfers between devices with their start and end apart: 6, of which 4 were waited for; matrix products, arithmetic and copies ran while one was open for 0% of the time, Pallas kernels for 11%

profile of v1, /device:TPU:223, one launch (start us, length us, event | category | flops | bytes accessed | tf_op | source)
XLA Modules:
  0.0 61.3 jit_solution(14109245128658897448)
XLA Ops:
  0.6 0.0 copy-start
  0.6 1.9 %copy-done = f32[3,8,32,1024]{3,2,1,0:T(8,128)S(1)} copy-done((f32[3,8,32,1024]{3,2,1,0:T(8,128)S(1)}, f32[3,8,32,1024]{3,2,1,0:T(8,128)}, u32[]{:S(2)}) %copy-start) | copy-done | bytes 3145752
  2.5 0.0 copy-start.1
  2.5 0.7 %copy-done.1 = s32[512]{0:T(512)S(1)} copy-done((s32[512]{0:T(512)S(1)}, s32[512]{0:T(512)}, u32[]{:S(2)}) %copy-start.1) | copy-done | bytes 2072
  3.2 1.3 %pack_shell.1 = f32[5,14,8,128]{3,2,1,0:T(8,128)S(1)} custom-call(s32[4,128]{1,0:T(4,128)S(1)} %bitcast.3, f32[3,8,32,1024]{3,2,1,0:T(8,128)S(1)} %copy-done), custom_call_target="tpu_custom_call" | custom-call | flops 1000000 | bytes 2000000 | tf_op jit(solution)/shard_map/pack_shell/pallas_call | solution.py:298
  4.5 4.3 %collective-permute-start = (f32[5,14,8,128]{3,2,1,0:T(8,128)S(1)}, f32[5,14,8,128]{3,2,1,0:T(8,128)S(1)}, u32[]{:S(2)}, u32[]{:S(2)}) collective-permute-start(f32[5,14,8,128]{3,2,1,0:T(8,128)S(1)} %pack_shell.1), channel_id=1, source_target_pairs={{0,1},{1,2},{2,3},{3,4},{4,5},{5,6},{6,7},{7,8},{8,9},{9,10},{10,1... | collective-permute-start | bytes 860168 | tf_op jit(solution)/shard_map/ppermute | solution.py:324
  8.9 1.3 %pack_core.1 = f32[5,18,8,128]{3,2,1,0:T(8,128)S(1)} custom-call(s32[4,128]{1,0:T(4,128)S(1)} %bitcast.4, f32[3,8,32,1024]{3,2,1,0:T(8,128)S(1)} %copy-done), custom_call_target="tpu_custom_call" | custom-call | flops 1000000 | bytes 2000000 | tf_op jit(solution)/shard_map/pack_core/pallas_call | solution.py:298
  10.2 3.1 %collective-permute-start.1 = (f32[5,18,8,128]{3,2,1,0:T(8,128)S(1)}, f32[5,18,8,128]{3,2,1,0:T(8,128)S(1)}, u32[]{:S(2)}, u32[]{:S(2)}) collective-permute-start(f32[5,18,8,128]{3,2,1,0:T(8,128)S(1)} %pack_core.1), channel_id=1, source_target_pairs={{0,1},{1,2},{2,3},{3,4},{4,5},{5,6},{6,7},{7,8},{8,9},{9,10},{10,1... | collective-permute-start | bytes 1105928 | tf_op jit(solution)/shard_map/ppermute | solution.py:326
  13.3 4.3 %relayout.1 = (f32[3,32,32,128]{3,2,1,0:T(8,128)S(1)}, f32[3,32,8,128]{3,2,1,0:T(8,128)S(1)}) custom-call(s32[4,128]{1,0:T(4,128)S(1)} %bitcast.5, f32[3,8,32,1024]{3,2,1,0:T(8,128)S(1)} %copy-done), custom_call_target="tpu_custom_call" | custom-call | flops 1000000 | bytes 4000000 | tf_op jit(solution)/shard_map/relayout/pallas_call | solution.py:298
  17.7 0.0 collective-permute-done.shell
  17.7 0.9 %make_faces.1 = (f32[8,32,128]{2,1,0:T(8,128)S(1)}, f32[8,32,128]{2,1,0:T(8,128)S(1)}, f32[36,8,128]{2,1,0:T(8,128)S(1)}, f32[36,8,128]{2,1,0:T(8,128)S(1)}) custom-call(s32[4,128]{1,0:T(4,128)S(1)} %bitcast.6, f32[5,14,8,128]{3,2,1,0:T(8,128)S(1)} %collective-permute-done.shell, f32[3,32,32,128]{3,2,1,0:T(8,128)S(1)} %get-tuple-element.12.own, ...), custom_call_target="tpu_custom_call" | custom-call | flops 1000000 | bytes 1000000 | tf_op jit(solution)/shard_map/make_faces/pallas_call | solution.py:298
  18.6 4.1 %collective-permute-start.2 = (f32[8,32,128]{2,1,0:T(8,128)S(1)}, f32[8,32,128]{2,1,0:T(8,128)S(1)}, u32[]{:S(2)}, u32[]{:S(2)}) collective-permute-start(f32[8,32,128]{2,1,0:T(8,128)S(1)} %get-tuple-element.14), channel_id=1, source_target_pairs={{0,1},{1,2},{2,3},{3,4},{4,5},{5,6},{6,7},{7,8},{8,9},{9,10},{10,1... | collective-permute-start | bytes 393224 | tf_op jit(solution)/shard_map/ppermute | solution.py:346
  22.7 1.9 %collective-permute-start.3 = (f32[8,32,128]{2,1,0:T(8,128)S(1)}, f32[8,32,128]{2,1,0:T(8,128)S(1)}, u32[]{:S(2)}, u32[]{:S(2)}) collective-permute-start(f32[8,32,128]{2,1,0:T(8,128)S(1)} %get-tuple-element.15), channel_id=1, source_target_pairs={{1,0},{2,1},{3,2},{4,3},{5,4},{6,5},{7,6},{8,7},{9,8},{10,9},{11,1... | collective-permute-start | bytes 393224 | tf_op jit(solution)/shard_map/ppermute | solution.py:347
  24.6 0.2 collective-permute-done.2.before.y_before
  24.8 6.9 %collective-permute-done.3.after.y_after = f32[8,32,128]{2,1,0:T(8,128)S(1)} collective-permute-done((f32[8,32,128]{2,1,0:T(8,128)S(1)}, f32[8,32,128]{2,1,0:T(8,128)S(1)}, u32[]{:S(2)}, u32[]{:S(2)}) %collective-permute-start.3) | collective-permute-done | bytes 131104 | tf_op jit(solution)/shard_map/ppermute | solution.py:347
  31.7 0.1 add_corners.1
  31.8 9.2 %collective-permute-start.4 = (f32[36,8,128]{2,1,0:T(8,128)S(1)}, f32[36,8,128]{2,1,0:T(8,128)S(1)}, u32[]{:S(2)}, u32[]{:S(2)}) collective-permute-start(f32[36,8,128]{2,1,0:T(8,128)S(1)} %get-tuple-element.18), channel_id=1, source_target_pairs={{0,32},{32,64},{64,96},{96,128},{128,160},{160,192},{192,224},{224... | collective-permute-start | bytes 442376 | tf_op jit(solution)/shard_map/ppermute | solution.py:359
  41.0 1.9 %collective-permute-start.5 = (f32[36,8,128]{2,1,0:T(8,128)S(1)}, f32[36,8,128]{2,1,0:T(8,128)S(1)}, u32[]{:S(2)}, u32[]{:S(2)}) collective-permute-start(f32[36,8,128]{2,1,0:T(8,128)S(1)} %get-tuple-element.19), channel_id=1, source_target_pairs={{32,0},{64,32},{96,64},{128,96},{160,128},{192,160},{224,192},{256... | collective-permute-start | bytes 442376 | tf_op jit(solution)/shard_map/ppermute | solution.py:360
  42.9 0.0 collective-permute-done.1.core
  42.9 0.1 collective-permute-done.4.x_before
  43.1 5.6 %collective-permute-done.5.x_after = f32[36,8,128]{2,1,0:T(8,128)S(1)} collective-permute-done((f32[36,8,128]{2,1,0:T(8,128)S(1)}, f32[36,8,128]{2,1,0:T(8,128)S(1)}, u32[]{:S(2)}, u32[]{:S(2)}) %collective-permute-start.5) | collective-permute-done | bytes 147488 | tf_op jit(solution)/shard_map/ppermute | solution.py:360
  48.7 12.6 %sweep.1 = (f32[1024,128]{1,0:T(8,128)}, f32[1024,128]{1,0:T(8,128)}) custom-call(s32[4,128]{1,0:T(4,128)S(1)} %bitcast.7, f32[3,32,32,128]{3,2,1,0:T(8,128)S(1)} %get-tuple-element.12.own, f32[5,14,8,128]{3,2,1,0:T(8,128)S(1)} %collective-permute-done.shell, f32[5,18,8,128]{3,2,1,0:T(8,128)S(1)} %collective-permute-done.1.core, ...), custom_call_target="tpu_custom_call" | custom-call | flops 100000000 | bytes 5000000 | tf_op jit(solution)/shard_map/sweep/pallas_call | solution.py:298
Async XLA Ops:
  0.6 1.9 %copy-start = (f32[3,8,32,1024]{3,2,1,0:T(8,128)S(1)}, f32[3,8,32,1024]{3,2,1,0:T(8,128)}, u32[]{:S(2)}) copy-start(f32[3,8,32,1024]{3,2,1,0:T(8,128)} %old_ref.5) | copy-start | bytes 9437188
  2.5 0.7 %copy-start.1 = (s32[512]{0:T(512)S(1)}, s32[512]{0:T(512)}, u32[]{:S(2)}) copy-start(s32[512]{0:T(512)} %param.3) | copy-start | bytes 6148
  4.5 13.1 %collective-permute-start = (f32[5,14,8,128]{3,2,1,0:T(8,128)S(1)}, f32[5,14,8,128]{3,2,1,0:T(8,128)S(1)}, u32[]{:S(2)}, u32[]{:S(2)}) collective-permute-start(f32[5,14,8,128]{3,2,1,0:T(8,128)S(1)} %pack_shell.1), channel_id=1, source_target_pairs={{0,1},{1,2},{2,3},{3,4},{4,5},{5,6},{6,7},{7,8},{8,9},{9,10},{10,1... | collective-permute-start | bytes 860168 | tf_op jit(solution)/shard_map/ppermute | solution.py:324
  10.2 32.7 %collective-permute-start.1 = (f32[5,18,8,128]{3,2,1,0:T(8,128)S(1)}, f32[5,18,8,128]{3,2,1,0:T(8,128)S(1)}, u32[]{:S(2)}, u32[]{:S(2)}) collective-permute-start(f32[5,18,8,128]{3,2,1,0:T(8,128)S(1)} %pack_core.1), channel_id=1, source_target_pairs={{0,1},{1,2},{2,3},{3,4},{4,5},{5,6},{6,7},{7,8},{8,9},{9,10},{10,1... | collective-permute-start | bytes 1105928 | tf_op jit(solution)/shard_map/ppermute | solution.py:326
  18.6 6.2 %collective-permute-start.2 = (f32[8,32,128]{2,1,0:T(8,128)S(1)}, f32[8,32,128]{2,1,0:T(8,128)S(1)}, u32[]{:S(2)}, u32[]{:S(2)}) collective-permute-start(f32[8,32,128]{2,1,0:T(8,128)S(1)} %get-tuple-element.14), channel_id=1, source_target_pairs={{0,1},{1,2},{2,3},{3,4},{4,5},{5,6},{6,7},{7,8},{8,9},{9,10},{10,1... | collective-permute-start | bytes 393224 | tf_op jit(solution)/shard_map/ppermute | solution.py:346
  22.7 9.0 %collective-permute-start.3 = (f32[8,32,128]{2,1,0:T(8,128)S(1)}, f32[8,32,128]{2,1,0:T(8,128)S(1)}, u32[]{:S(2)}, u32[]{:S(2)}) collective-permute-start(f32[8,32,128]{2,1,0:T(8,128)S(1)} %get-tuple-element.15), channel_id=1, source_target_pairs={{1,0},{2,1},{3,2},{4,3},{5,4},{6,5},{7,6},{8,7},{9,8},{10,9},{11,1... | collective-permute-start | bytes 393224 | tf_op jit(solution)/shard_map/ppermute | solution.py:347
  31.8 11.3 %collective-permute-start.4 = (f32[36,8,128]{2,1,0:T(8,128)S(1)}, f32[36,8,128]{2,1,0:T(8,128)S(1)}, u32[]{:S(2)}, u32[]{:S(2)}) collective-permute-start(f32[36,8,128]{2,1,0:T(8,128)S(1)} %get-tuple-element.18), channel_id=1, source_target_pairs={{0,32},{32,64},{64,96},{96,128},{128,160},{160,192},{192,224},{224... | collective-permute-start | bytes 442376 | tf_op jit(solution)/shard_map/ppermute | solution.py:359
  41.0 7.7 %collective-permute-start.5 = (f32[36,8,128]{2,1,0:T(8,128)S(1)}, f32[36,8,128]{2,1,0:T(8,128)S(1)}, u32[]{:S(2)}, u32[]{:S(2)}) collective-permute-start(f32[36,8,128]{2,1,0:T(8,128)S(1)} %get-tuple-element.19), channel_id=1, source_target_pairs={{32,0},{64,32},{96,64},{128,96},{160,128},{192,160},{224,192},{256... | collective-permute-start | bytes 442376 | tf_op jit(solution)/shard_map/ppermute | solution.py:360

commit v2 on v1

v2 whole, which is shorter than its diff:
```python
import jax
import jax.numpy as jnp
from jax import lax
from jax.experimental import pallas as pl
from jax.experimental.pallas import tpu as pltpu
from jax.sharding import PartitionSpec as P

EDGE = 32
LANES = 128
GROUPS = EDGE * EDGE // LANES
COLUMN = 4
FIELDS = 3
MOVED = 2
KINDS = 5
SHELL = GROUPS + 6
CORE = 3 * (GROUPS - 2)
ROWS = EDGE + 16
DEEP = EDGE + 8
XMSG = EDGE + 4
F32 = jnp.float32
VMEM = pltpu.VMEM


def iota(shape, dim):
    return lax.broadcasted_iota(jnp.int32, shape, dim)


def moved_boxes(counts_ref):
    device = lax.axis_index("grp") * lax.axis_size("dev") + lax.axis_index("dev")
    counts = counts_ref[...]
    index = iota(counts.shape, 0) * LANES + iota(counts.shape, 1)
    start = jnp.sum(jnp.where(index < device, counts, 0))
    return jnp.clip(start - device * COLUMN, 0, MOVED)


def lane_group(g):
    return pl.ds(g * LANES, LANES)


def fetch(counts_ref, old_ref, counts, boxes, sems, first):
    copies = [pltpu.make_async_copy(counts_ref, counts, sems.at[FIELDS])]
    for f in range(FIELDS):
        copies.append(pltpu.make_async_copy(old_ref.at[f, pl.ds(first, COLUMN)], boxes.at[f], sems.at[f]))
    for copy in copies:
        copy.start()
    copies[0].wait()
    return copies[1:], moved_boxes(counts)


def box_tiles(boxes, f, c, g, which):
    low = iota((8, LANES), 0) < 4
    if which == "edge":
        return jnp.where(low, boxes[f, c, 0:8, lane_group(g)], boxes[f, c, 24:32, lane_group(g)])
    if which == 0:
        return jnp.where(low, boxes[f, c, 24:32, lane_group(g)], boxes[f, c, 0:8, lane_group(g)])
    return boxes[f, c, 8 * which : 8 * which + 8, lane_group(g)]


def pack(boxes, moved, out, at, g, which):
    shape = (8, LANES)
    lane = iota(shape, 1)
    block = lane // EDGE
    black = (iota(shape, 0) + block + lane) % 2 == 1
    even = block % 2 == 0
    first, second = [
        [box_tiles(boxes, f, MOVED + c - moved, g, which) for f in range(FIELDS)] for c in range(MOVED)
    ]
    turned = [pltpu.roll(v, EDGE, 1) for v in second]
    out[0, at] = jnp.where(black, first[0], turned[0])
    for f in (1, 2):
        out[2 * f - 1, at] = jnp.where(even, first[f], turned[f])
        out[2 * f, at] = jnp.where(even, turned[f], first[f])


def pack_shell(counts_ref, old_ref, out, counts, boxes, sems):
    copies, moved = fetch(counts_ref, old_ref, counts, boxes, sems, MOVED)
    for copy in copies:
        copy.wait()
    for g in range(GROUPS):
        pack(boxes, moved, out, g, g, "edge")
    for side, g in enumerate((0, GROUPS - 1)):
        for which in range(3):
            pack(boxes, moved, out, GROUPS + 3 * side + which, g, which)


def pack_core(counts_ref, old_ref, out, counts, boxes, sems):
    copies, moved = fetch(counts_ref, old_ref, counts, boxes, sems, MOVED)
    for copy in copies:
        copy.wait()
    for g in range(1, GROUPS - 1):
        for which in range(3):
            pack(boxes, moved, out, 3 * (g - 1) + which, g, which)


def interleave(v):
    lane = iota(v[0].shape, 1)
    half = lane < 2 * EDGE
    even = (lane // EDGE) % 2 == 0
    w = [pltpu.roll(a, 2 * EDGE, 1) for a in v]
    a0, a1 = jnp.where(half, v[0], w[2]), jnp.where(half, v[1], w[3])
    a2, a3 = jnp.where(half, w[0], v[2]), jnp.where(half, w[1], v[3])
    rows = []
    for a, b in ((a0, a1), (a2, a3)):
        rows.append(jnp.where(even, a, pltpu.roll(b, EDGE, 1)))
        rows.append(jnp.where(even, pltpu.roll(a, LANES - EDGE, 1), b))
    return rows


def relayout_edges(counts_ref, old_ref, edges, slabs, counts, boxes, sems):
    copies, moved = fetch(counts_ref, old_ref, counts, boxes, sems, 0)
    slots = [jnp.maximum(c - moved, 0) for c in range(COLUMN)]
    for f in range(FIELDS):
        copies[f].wait()
        for g in range(GROUPS):
            for r, row in enumerate(interleave([box_tiles(boxes, f, slot, g, "edge") for slot in slots])):
                edges[f, 4 * g + r] = row
        for side, g in enumerate((0, GROUPS - 1)):
            for r, row in enumerate(interleave([boxes[f, slot, :, lane_group(g)] for slot in slots])):
                slabs[f, side, r] = row


def relayout(counts_ref, old_ref, out, counts, boxes, sems):
    copies, moved = fetch(counts_ref, old_ref, counts, boxes, sems, 0)
    slots = [jnp.maximum(c - moved, 0) for c in range(COLUMN)]
    for f in range(FIELDS):
        copies[f].wait()
        for g in range(GROUPS):
            for r, row in enumerate(interleave([boxes[f, slot, :, lane_group(g)] for slot in slots])):
                out[f, 4 * g + r] = row


def unmix(kinds, f):
    if f == 0:
        a = b = kinds[0]
    else:
        a, b = kinds[2 * f - 1], kinds[2 * f]
    return [a, pltpu.roll(b, LANES - EDGE, 1), pltpu.roll(a, 2 * EDGE, 1), pltpu.roll(b, EDGE, 1)]


def wire_rows(shell, core, k, g):
    low = iota((8, LANES), 0) < 4
    edge = shell[k, g]
    if g in (0, GROUPS - 1):
        base = GROUPS + (3 if g else 0)
        mid = [shell[k, base + which] for which in range(3)]
    else:
        mid = [core[k, 3 * (g - 1) + which] for which in range(3)]
    return jnp.concatenate([jnp.where(low, edge, mid[0]), mid[1], mid[2], jnp.where(low, mid[0], edge)], axis=0)


def pack_x(pressure, right_side, coefficient):
    row = iota((8, LANES), 0)
    high = jnp.where(
        row >= 5, coefficient, jnp.where(row >= 2, pltpu.roll(pressure, 5, 0), pltpu.roll(right_side, 2, 0))
    )
    low = jnp.where(
        row < 3, coefficient, jnp.where(row < 6, pltpu.roll(pressure, 3, 0), pltpu.roll(right_side, 6, 0))
    )
    return high, low


def make_faces(counts_ref, shell, edges, slabs, y_up, y_down, x_up, x_down):
    limit = moved_boxes(counts_ref) * EDGE
    taken = iota((EDGE, LANES), 1) < limit
    for side, g in enumerate((0, GROUPS - 1)):
        out = y_up if side else y_down
        kinds = [wire_rows(shell, None, k, g) for k in range(KINDS)]
        for f, at, depth in ((2, 0, 3), (0, 3, 3), (1, 6, 2)):
            rows = unmix(kinds, f)
            for j in range(depth):
                r = 4 - depth + j if side else j
                out[at + j] = jnp.where(taken, rows[r], slabs[f, side, r])
    taken = iota((8, LANES), 1) < limit
    for g in range(GROUPS):
        kinds = [shell[k, g] for k in range(KINDS)]
        rows = [unmix(kinds, f) for f in range(FIELDS)]
        for r in range(4):
            y = 4 * g + r
            edge = [jnp.where(taken, rows[f][r], edges[f, y]) for f in range(FIELDS)]
            x_up[y + 2], x_down[y + 2] = pack_x(*edge)


def add_corners(before, after, x_up_in, x_down_in, x_up, x_down, tiles, sems):
    del x_up_in, x_down_in
    low = iota((8, LANES), 0) < 4
    places = ((before, 1, 4, 6), (before, 2, 5, 7), (after, 0, 3, 6), (after, 1, 4, 7))
    for at, (ref, b, p, f) in enumerate(places):
        edge = [jnp.where(low, ref[i, 0:8], ref[i, 24:32]) for i in (p, f, b)]
        tiles[0, at], tiles[1, at] = pack_x(*edge)
    copies = []
    for way, out in enumerate((x_up, x_down)):
        for side in range(2):
            copies.append(
                pltpu.make_async_copy(
                    tiles.at[way, pl.ds(2 * side, 2)], out.at[pl.ds((XMSG - 2) * side, 2)], sems.at[way, side]
                )
            )
    for copy in copies:
        copy.start()
    for copy in copies:
        copy.wait()


def is_red(shape, shift):
    return (iota(shape, 0) + iota(shape, 1) + shift) & 1 == 0


def assemble(counts_ref, own, shell, core, half, mix, rhs):
    limit = moved_boxes(counts_ref) * EDGE
    taken = iota((EDGE, LANES), 1) < limit
    reds = [is_red((EDGE, LANES), y) for y in range(2)]
    before = None
    for g in range(GROUPS):
        kinds = [wire_rows(shell, core, k, g) for k in range(KINDS)]
        parts = [unmix(kinds, f) for f in range(FIELDS)]
        for r in range(4):
            y = 4 * g + r
            p, f, b = [jnp.where(taken, parts[i][r], own[i, y]) for i in range(FIELDS)]
            h = 0.5 * b
            half[y] = h
            rhs[y] = f
            if y:
                mix[y - 1] = jnp.where(reds[(y - 1) % 2], h * p, before)
            before = p
    mix[EDGE - 1] = before


def tile(row):
    return pl.ds(row, 8)


def sweep(
    half_in,
    mix_in,
    rhs_in,
    y_before,
    y_after,
    x_before,
    x_after,
    out_p,
    out_r,
    half,
    mix,
    rhs,
    mix2,
    mix3,
    new1,
    new2,
    inv,
    tot,
    rest,
):
    grp, dev = lax.axis_index("grp"), lax.axis_index("dev")
    inner = pl.ds(8, EDGE)
    red_rows = [is_red((EDGE, LANES), y) for y in range(2)]
    reds = [is_red((8, LANES), y) for y in range(2)]
    pressures, flux = {}, {}
    for y in (-3, -2, -1, 32, 33, 34):
        ref, k = (y_before, y + 3) if y < 0 else (y_after, y - 32)
        h = 0.5 * ref[k]
        half[y + 4, inner] = h
        pressures[y] = ref[3 + k]
        flux[y] = h * ref[3 + k]
        k = k - 1 if y < 0 else k
        if 0 <= k < 2:
            rhs[y + 4, inner] = ref[6 + k]
    flux[0] = half_in[0] * mix_in[0]
    pressures[EDGE - 1] = mix_in[EDGE - 1]

    def take_in(k, carry):
        for d in range(4):
            y = 4 * k + d
            half[y + 4, inner] = half_in[y]
            mix[y + 4, inner] = mix_in[y]
            rhs[y + 4, inner] = rhs_in[y]
        return carry

    lax.fori_loop(0, EDGE // 4, take_in, 0)
    zero = jnp.zeros((EDGE, LANES), F32)
    for y in (-4, -3, -2, -1, 31, 32, 33, 34):
        mix[y + 4, inner] = jnp.where(red_rows[y % 2], flux.get(y + 1, zero), pressures.get(y, zero))

    def strip(i, odd, last):
        j = i + 2
        rows = []
        for ref, at, turn_p, turn_f, kept in ((x_before, 0, 3, 6, last[0]), (x_after, ROWS - 8, 5, 2, last[1])):
            v = ref[i]
            h = 0.5 * v
            p = pltpu.roll(v, turn_p, 0)
            half[j, tile(at)] = h
            rhs[j, tile(at)] = pltpu.roll(v, turn_f, 0)
            mix[j, tile(at)] = jnp.where(reds[odd], kept, p)
            rows.append(h * p)
        return rows

    def strips(k, carry):
        i = XMSG - 1 - 4 * k
        for d in range(4):
            carry = strip(i - d, (1 + d) % 2, carry)
        return tuple(carry)

    nothing = jnp.zeros((8, LANES), F32)
    last = lax.fori_loop(0, XMSG // 4, strips, (nothing, nothing))
    mix[1, tile(0)], mix[1, tile(ROWS - 8)] = last

    lane = iota((8, LANES), 1)
    row = iota((8, LANES), 0)
    first_lane, last_lane = lane == 0, lane == LANES - 1

    def six(ref, j, top, count):
        sums = []
        for t in range(count):
            r = top + 8 * t
            v = ref[j, tile(r)]
            z = jnp.where(first_lane, 0.0, pltpu.roll(v, 1, 1)) + jnp.where(last_lane, 0.0, pltpu.roll(v, LANES - 1, 1))
            x = ref[j, tile(r - 1)] + ref[j, tile(r + 1)]
            sums.append((z + x) + (ref[j - 1, tile(r)] + ref[j + 1, tile(r)]))
        return sums

    open_x = [row >= 2 * (grp == 0).astype(jnp.int32), None, None, None]
    open_x.append(row < 8 - 6 * (grp == lax.axis_size("grp") - 1).astype(jnp.int32))

    def red(j, odd, carry, shut=None):
        flow_before, new_before = carry
        around = six(half, j, 6, 5)
        flow = six(mix, j, 6, 5)
        news = []
        for t in range(5):
            r = tile(6 + 8 * t)
            h = half[j, r]
            total = 6.0 * h + around[t]
            inverse = 1.0 / total
            if open_x[t] is not None:
                inverse = jnp.where(open_x[t], inverse, 0.0)
            if shut is not None:
                inverse = jnp.where(row >= 8 * shut, inverse, 0.0)
            new = (rhs[j, r] + (h * flow[t] + flow_before[t])) * inverse
            new1[j, r] = new
            inv[j, r] = inverse
            tot[j, r] = total
            mix2[j - 1, r] = jnp.where(reds[1 - odd], new_before[t], h * new)
            news.append(new)
        return flow, news

    def black(j, odd, carry):
        flow_before, new_before = carry
        flow = six(mix2, j, 7, 5)
        news = []
        for t in range(5):
            r = tile(7 + 8 * t)
            h = half[j, r]
            full = rhs[j, r] + (h * flow[t] + flow_before[t])
            new = full * inv[j, r]
            new2[j, r] = new
            rest[j, r] = full - tot[j, r] * new
            mix3[j - 1, r] = jnp.where(reds[1 - odd], new_before[t], h * new)
            news.append(new)
        return flow, news

    def finish(j, odd, flow_before):
        flow = six(mix3, j, 8, 4)
        for t in range(4):
            r = tile(8 + 8 * t)
            mine = new1[j, r]
            left = (rhs[j, r] + (half[j, r] * flow[t] + flow_before[t])) - tot[j, r] * mine
            rows = pl.ds(j - 4 + 8 * t * EDGE, 8, stride=EDGE)
            out_p[rows, :] = jnp.where(reds[odd], mine, new2[j, r])
            out_r[rows, :] = jnp.where(reds[odd], left, rest[j, r])
        return flow

    low_shut = (dev == 0).astype(jnp.int32)
    high_shut = (dev == lax.axis_size("dev") - 1).astype(jnp.int32)

    def reds_step(k, carry):
        for d in range(4):
            carry = red(4 + 4 * k + d, d % 2, carry)
        return carry

    carry = (six(mix, 1, 6, 5), [nothing] * 5)
    carry = red(2, 0, carry, low_shut)
    carry = red(3, 1, carry, low_shut)
    carry = lax.fori_loop(0, EDGE // 4, reds_step, carry)
    carry = red(EDGE + 4, 0, carry, high_shut)
    carry = red(EDGE + 5, 1, carry, high_shut)
    for t in range(5):
        mix2[EDGE + 5, tile(6 + 8 * t)] = carry[1][t]

    def blacks_step(k, carry):
        for d in range(4):
            carry = black(4 + 4 * k + d, d % 2, carry)
        return carry

    carry = (six(mix2, 2, 7, 5), [nothing] * 5)
    carry = black(3, 1, carry)
    carry = lax.fori_loop(0, EDGE // 4, blacks_step, carry)
    carry = black(EDGE + 4, 0, carry)
    for t in range(5):
        mix3[EDGE + 4, tile(7 + 8 * t)] = carry[1][t]

    def finish_step(k, flow):
        for d in range(4):
            flow = finish(4 + 4 * k + d, d % 2, flow)
        return flow

    lax.fori_loop(0, EDGE // 4, finish_step, six(mix3, 3, 8, 4))


def call(body, inputs, outputs, scratch, flops, moved, aliases=None, hbm=(), anywhere=False, limit=40 * 2**20):
    vmem, place, far = [pl.BlockSpec(memory_space=m) for m in (pltpu.VMEM, pl.ANY, pltpu.HBM)]
    kept = set(aliases or {}) if anywhere else ()
    return pl.pallas_call(
        body,
        out_shape=[jax.ShapeDtypeStruct(shape, F32) for shape in outputs],
        in_specs=[far if i in hbm else place if i in kept else vmem for i in range(len(inputs))],
        out_specs=[place if anywhere else vmem for _ in outputs],
        scratch_shapes=scratch,
        input_output_aliases=aliases or {},
        cost_estimate=pl.CostEstimate(flops=flops, bytes_accessed=moved, transcendentals=0),
        compiler_params=pltpu.CompilerParams(vmem_limit_bytes=limit),
        name=body.__name__,
    )(*inputs)


def per_device(old_fields, old_counts):
    groups, columns = lax.axis_size("grp"), lax.axis_size("dev")
    devices = groups * columns
    counts = jnp.pad(old_counts, (0, -devices % LANES)).reshape(-1, LANES)
    chain = [(i, i + 1) for i in range(devices - 1)]

    def ends(count):
        up = [(i, i + 1) for i in range(count - 1)]
        return up, [(j, i) for i, j in up]

    y_ways, x_ways = ends(columns), ends(groups)

    def read(body, outputs, after=None):
        table = counts if after is None else lax.optimization_barrier((counts, after))[0]
        scratch = [
            VMEM(counts.shape, jnp.int32),
            VMEM((FIELDS, COLUMN, EDGE, EDGE * EDGE), F32),
            pltpu.SemaphoreType.DMA((FIELDS + 1,)),
        ]
        return call(body, (table, old_fields), outputs, scratch, 10**6, 2 * 10**6, hbm=(0, 1), limit=40 * 2**20 if after is not None else 54400000)

    face, strip = (8, EDGE, LANES), (XMSG, 8, LANES)
    deep = (DEEP, ROWS, LANES)
    (shell,) = read(pack_shell, [(KINDS, SHELL, 8, LANES)])
    shell = lax.ppermute(shell, ("grp", "dev"), chain)
    (core,) = read(pack_core, [(KINDS, CORE, 8, LANES)])
    core = lax.ppermute(core, ("grp", "dev"), chain)
    edges, slabs = read(relayout_edges, [(FIELDS, EDGE, 8, LANES), (FIELDS, 2, 4, EDGE, LANES)])
    y_up, y_down, x_up, x_down = call(
        make_faces, (counts, shell, edges, slabs), [face, face, strip, strip], [], 10**6, 10**6
    )
    (own,) = read(relayout, [(FIELDS, EDGE, EDGE, LANES)], y_up)
    y_before = lax.ppermute(y_up, "dev", y_ways[0])
    y_after = lax.ppermute(y_down, "dev", y_ways[1])
    x_up, x_down = call(
        add_corners,
        (y_before, y_after, x_up, x_down),
        [strip, strip],
        [VMEM((2, 4, 8, LANES), F32), pltpu.SemaphoreType.DMA((2, 2))],
        10**4,
        10**5,
        aliases={2: 0, 3: 1},
        anywhere=True,
    )
    x_before = lax.ppermute(x_up, "grp", x_ways[0])
    x_after = lax.ppermute(x_down, "grp", x_ways[1])
    table = lax.optimization_barrier((counts, x_up))[0]
    half, mix, rhs = call(assemble, (table, own, shell, core), [(EDGE, EDGE, LANES)] * 3, [], 10**6, 10**6)
    flat = (EDGE * EDGE, LANES)
    outs = call(
        sweep,
        (half, mix, rhs, y_before, y_after, x_before, x_after),
        [flat, flat],
        [VMEM(deep, F32)] * 10,
        10**8,
        5 * 10**6,
    )
    return tuple(out.reshape(EDGE, EDGE, LANES) for out in outs)


def solution(mesh):
    placed = (P(None, ("grp", "dev"), None, None), P())
    return jax.shard_map(
        per_device,
        mesh=mesh,
        in_specs=placed,
        out_specs=(P("grp", "dev", None), P("grp", "dev", None)),
        check_vma=False,
    )
```

time: 61.6 us -> 46 us (0.75)
  the two profiles are of different devices: /device:TPU:223 before, /device:TPU:225 now
where the time goes in v2:
time: 46 us; the launch traced here: 45.7 us
  starting transfers between devices  22 us (48%)
  Pallas kernels  13 us (28%)
  waiting for transfers between devices  9.24 us (20%)
  between operations  0.77 us (2%)
  local copies, waits for them, and re-layouts  0.68 us (1%)
    pallas_call x8, Pallas kernels, call(): pl.pallas_call(body, out_shape=[jax.ShapeDtypeStruct(shape, F32) for shap...  13 us
    ppermute x1, waiting for transfers between devices, per_device(): y_before = lax.ppermute(y_up, 'dev', y_ways[0])  5.58 us
    ppermute x1, starting transfers between devices, per_device(): x_before = lax.ppermute(x_up, 'grp', x_ways[0])  5.11 us
    ppermute x1, starting transfers between devices, per_device(): x_after = lax.ppermute(x_down, 'grp', x_ways[1])  5.1 us
    ppermute x1, starting transfers between devices, per_device(): core = lax.ppermute(core, ('grp', 'dev'), chain)  3.38 us
    ppermute x1, starting transfers between devices, per_device(): shell = lax.ppermute(shell, ('grp', 'dev'), chain)  3.12 us
    ppermute x1, waiting for transfers between devices, per_device(): shell = lax.ppermute(shell, ('grp', 'dev'), chain)  2.95 us
    ppermute x1, starting transfers between devices, per_device(): y_before = lax.ppermute(y_up, 'dev', y_ways[0])  2.74 us
  transfers between devices with their start and end apart: 6, of which 3 were waited for; matrix products, arithmetic and copies ran while one was open for 0% of the time, Pallas kernels for 14%

profile of v2, /device:TPU:225, one launch (start us, length us, event | category | flops | bytes accessed | tf_op | source)
XLA Modules:
  0.0 45.7 jit_solution(10296859610329165901)
XLA Ops:
  0.6 0.0 copy-start.1
  0.6 0.7 %copy-done.1 = s32[512]{0:T(512)S(1)} copy-done((s32[512]{0:T(512)S(1)}, s32[512]{0:T(512)}, u32[]{:S(2)}) %copy-start.1) | copy-done | bytes 2072
  1.3 1.5 %pack_shell.1 = f32[5,14,8,128]{3,2,1,0:T(8,128)S(1)} custom-call(s32[4,128]{1,0:T(4,128)S(1)} %bitcast.3, f32[3,8,32,1024]{3,2,1,0:T(8,128)} %old_ref.7), custom_call_target="tpu_custom_call" | custom-call | flops 1000000 | bytes 2000000 | tf_op jit(solution)/shard_map/pack_shell/pallas_call | solution.py:411
  2.8 3.1 %collective-permute-start = (f32[5,14,8,128]{3,2,1,0:T(8,128)S(1)}, f32[5,14,8,128]{3,2,1,0:T(8,128)S(1)}, u32[]{:S(2)}, u32[]{:S(2)}) collective-permute-start(f32[5,14,8,128]{3,2,1,0:T(8,128)S(1)} %pack_shell.1), channel_id=1, source_target_pairs={{0,1},{1,2},{2,3},{3,4},{4,5},{5,6},{6,7},{7,8},{8,9},{9,10},{10,1... | collective-permute-start | bytes 860168 | tf_op jit(solution)/shard_map/ppermute | solution.py:448
  6.0 1.5 %pack_core.1 = f32[5,18,8,128]{3,2,1,0:T(8,128)S(1)} custom-call(s32[4,128]{1,0:T(4,128)S(1)} %bitcast.4, f32[3,8,32,1024]{3,2,1,0:T(8,128)} %old_ref.7), custom_call_target="tpu_custom_call" | custom-call | flops 1000000 | bytes 2000000 | tf_op jit(solution)/shard_map/pack_core/pallas_call | solution.py:411
  7.5 0.0 copy-start
  7.5 3.4 %collective-permute-start.3 = (f32[5,18,8,128]{3,2,1,0:T(8,128)S(1)}, f32[5,18,8,128]{3,2,1,0:T(8,128)S(1)}, u32[]{:S(2)}, u32[]{:S(2)}) collective-permute-start(f32[5,18,8,128]{3,2,1,0:T(8,128)S(1)} %pack_core.1), channel_id=1, source_target_pairs={{0,1},{1,2},{2,3},{3,4},{4,5},{5,6},{6,7},{7,8},{8,9},{9,10},{10,1... | collective-permute-start | bytes 1105928 | tf_op jit(solution)/shard_map/ppermute | solution.py:450
  10.9 1.9 %relayout_edges.1 = (f32[3,32,8,128]{3,2,1,0:T(8,128)S(1)}, f32[3,2,4,32,128]{4,3,2,1,0:T(8,128)S(1)}) custom-call(s32[4,128]{1,0:T(4,128)S(1)} %bitcast.5, f32[3,8,32,1024]{3,2,1,0:T(8,128)} %old_ref.7), custom_call_target="tpu_custom_call" | custom-call | flops 1000000 | bytes 2000000 | tf_op jit(solution)/shard_map/relayout_edges/pallas_call | solution.py:411
  12.8 3.0 %collective-permute-done.shell = f32[5,14,8,128]{3,2,1,0:T(8,128)S(1)} collective-permute-done((f32[5,14,8,128]{3,2,1,0:T(8,128)S(1)}, f32[5,14,8,128]{3,2,1,0:T(8,128)S(1)}, u32[]{:S(2)}, u32[]{:S(2)}) %collective-permute-start) | collective-permute-done | bytes 286752 | tf_op jit(solution)/shard_map/ppermute | solution.py:448
  15.8 0.2 make_faces.1
  16.0 2.5 %collective-permute-start.2 = (f32[8,32,128]{2,1,0:T(8,128)S(1)}, f32[8,32,128]{2,1,0:T(8,128)S(1)}, u32[]{:S(2)}, u32[]{:S(2)}) collective-permute-start(f32[8,32,128]{2,1,0:T(8,128)S(1)} %get-tuple-element.20), channel_id=1, source_target_pairs={{1,0},{2,1},{3,2},{4,3},{5,4},{6,5},{7,6},{8,7},{9,8},{10,9},{11,1... | collective-permute-start | bytes 393224 | tf_op jit(solution)/shard_map/ppermute | solution.py:457
  18.6 2.7 %collective-permute-start.1 = (f32[8,32,128]{2,1,0:T(8,128)S(1)}, f32[8,32,128]{2,1,0:T(8,128)S(1)}, u32[]{:S(2)}, u32[]{:S(2)}) collective-permute-start(f32[8,32,128]{2,1,0:T(8,128)S(1)} %get-tuple-element.19), channel_id=1, source_target_pairs={{0,1},{1,2},{2,3},{3,4},{4,5},{5,6},{6,7},{7,8},{8,9},{9,10},{10,1... | collective-permute-start | bytes 393224 | tf_op jit(solution)/shard_map/ppermute | solution.py:456
  21.3 0.7 %collective-permute-done.2.after.y_after = f32[8,32,128]{2,1,0:T(8,128)S(1)} collective-permute-done((f32[8,32,128]{2,1,0:T(8,128)S(1)}, f32[8,32,128]{2,1,0:T(8,128)S(1)}, u32[]{:S(2)}, u32[]{:S(2)}) %collective-permute-start.2) | collective-permute-done | bytes 131104 | tf_op jit(solution)/shard_map/ppermute | solution.py:457
  22.0 5.6 %collective-permute-done.1.before.y_before = f32[8,32,128]{2,1,0:T(8,128)S(1)} collective-permute-done((f32[8,32,128]{2,1,0:T(8,128)S(1)}, f32[8,32,128]{2,1,0:T(8,128)S(1)}, u32[]{:S(2)}, u32[]{:S(2)}) %collective-permute-start.1) | collective-permute-done | bytes 131104 | tf_op jit(solution)/shard_map/ppermute | solution.py:456
  27.6 0.1 add_corners.1
  27.7 5.1 %collective-permute-start.5 = (f32[36,8,128]{2,1,0:T(8,128)S(1)}, f32[36,8,128]{2,1,0:T(8,128)S(1)}, u32[]{:S(2)}, u32[]{:S(2)}) collective-permute-start(f32[36,8,128]{2,1,0:T(8,128)S(1)} %get-tuple-element.29), channel_id=1, source_target_pairs={{32,0},{64,32},{96,64},{128,96},{160,128},{192,160},{224,192},{256... | collective-permute-start | bytes 442376 | tf_op jit(solution)/shard_map/ppermute | solution.py:469
  32.8 5.1 %collective-permute-start.4 = (f32[36,8,128]{2,1,0:T(8,128)S(1)}, f32[36,8,128]{2,1,0:T(8,128)S(1)}, u32[]{:S(2)}, u32[]{:S(2)}) collective-permute-start(f32[36,8,128]{2,1,0:T(8,128)S(1)} %get-tuple-element.23), channel_id=1, source_target_pairs={{0,32},{32,64},{64,96},{96,128},{128,160},{160,192},{192,224},{224... | collective-permute-start | bytes 442376 | tf_op jit(solution)/shard_map/ppermute | solution.py:468
  37.9 0.0 copy-done
  37.9 2.3 %relayout.1.own = f32[3,32,32,128]{3,2,1,0:T(8,128)S(1)} custom-call(s32[4,128]{1,0:T(4,128)S(1)} %bitcast.7, f32[3,8,32,1024]{3,2,1,0:T(8,128)S(1)} %copy-done), custom_call_target="tpu_custom_call" | custom-call | flops 1000000 | bytes 2000000 | tf_op jit(solution)/shard_map/relayout/pallas_call | solution.py:411
  40.2 0.0 collective-permute-done.3.core
  40.3 0.4 assemble.1
  40.7 0.0 collective-permute-done.5.x_after
  40.7 0.0 collective-permute-done.4.x_before
  40.7 5.0 %sweep.1 = (f32[1024,128]{1,0:T(8,128)}, f32[1024,128]{1,0:T(8,128)}) custom-call(f32[32,32,128]{2,1,0:T(8,128)S(1)} %get-tuple-element.26.half_in, f32[32,32,128]{2,1,0:T(8,128)S(1)} %get-tuple-element.27.mix_in, f32[32,32,128]{2,1,0:T(8,128)S(1)} %get-tuple-element.28.rhs_in, f32[8,32,128]{2,1,0:T(8,128)S(1)} %collective-permute-done.1.before.y_before, ...), custom_call_target="tpu_custom_call" | custom-call | flops 100000000 | bytes 5000000 | tf_op jit(solution)/shard_map/sweep/pallas_call | solution.py:411
Async XLA Ops:
  0.6 0.7 %copy-start.1 = (s32[512]{0:T(512)S(1)}, s32[512]{0:T(512)}, u32[]{:S(2)}) copy-start(s32[512]{0:T(512)} %param.3) | copy-start | bytes 6148
  2.8 12.9 %collective-permute-start = (f32[5,14,8,128]{3,2,1,0:T(8,128)S(1)}, f32[5,14,8,128]{3,2,1,0:T(8,128)S(1)}, u32[]{:S(2)}, u32[]{:S(2)}) collective-permute-start(f32[5,14,8,128]{3,2,1,0:T(8,128)S(1)} %pack_shell.1), channel_id=1, source_target_pairs={{0,1},{1,2},{2,3},{3,4},{4,5},{5,6},{6,7},{7,8},{8,9},{9,10},{10,1... | collective-permute-start | bytes 860168 | tf_op jit(solution)/shard_map/ppermute | solution.py:448
  7.5 30.4 %copy-start = (f32[3,8,32,1024]{3,2,1,0:T(8,128)S(1)}, f32[3,8,32,1024]{3,2,1,0:T(8,128)}, u32[]{:S(2)}) copy-start(f32[3,8,32,1024]{3,2,1,0:T(8,128)} %old_ref.7) | copy-start | bytes 9437188
  7.5 32.8 %collective-permute-start.3 = (f32[5,18,8,128]{3,2,1,0:T(8,128)S(1)}, f32[5,18,8,128]{3,2,1,0:T(8,128)S(1)}, u32[]{:S(2)}, u32[]{:S(2)}) collective-permute-start(f32[5,18,8,128]{3,2,1,0:T(8,128)S(1)} %pack_core.1), channel_id=1, source_target_pairs={{0,1},{1,2},{2,3},{3,4},{4,5},{5,6},{6,7},{7,8},{8,9},{9,10},{10,1... | collective-permute-start | bytes 1105928 | tf_op jit(solution)/shard_map/ppermute | solution.py:450
  16.0 6.0 %collective-permute-start.2 = (f32[8,32,128]{2,1,0:T(8,128)S(1)}, f32[8,32,128]{2,1,0:T(8,128)S(1)}, u32[]{:S(2)}, u32[]{:S(2)}) collective-permute-start(f32[8,32,128]{2,1,0:T(8,128)S(1)} %get-tuple-element.20), channel_id=1, source_target_pairs={{1,0},{2,1},{3,2},{4,3},{5,4},{6,5},{7,6},{8,7},{9,8},{10,9},{11,1... | collective-permute-start | bytes 393224 | tf_op jit(solution)/shard_map/ppermute | solution.py:457
  18.6 9.0 %collective-permute-start.1 = (f32[8,32,128]{2,1,0:T(8,128)S(1)}, f32[8,32,128]{2,1,0:T(8,128)S(1)}, u32[]{:S(2)}, u32[]{:S(2)}) collective-permute-start(f32[8,32,128]{2,1,0:T(8,128)S(1)} %get-tuple-element.19), channel_id=1, source_target_pairs={{0,1},{1,2},{2,3},{3,4},{4,5},{5,6},{6,7},{7,8},{8,9},{9,10},{10,1... | collective-permute-start | bytes 393224 | tf_op jit(solution)/shard_map/ppermute | solution.py:456
  27.7 13.0 %collective-permute-start.5 = (f32[36,8,128]{2,1,0:T(8,128)S(1)}, f32[36,8,128]{2,1,0:T(8,128)S(1)}, u32[]{:S(2)}, u32[]{:S(2)}) collective-permute-start(f32[36,8,128]{2,1,0:T(8,128)S(1)} %get-tuple-element.29), channel_id=1, source_target_pairs={{32,0},{64,32},{96,64},{128,96},{160,128},{192,160},{224,192},{256... | collective-permute-start | bytes 442376 | tf_op jit(solution)/shard_map/ppermute | solution.py:469
  32.8 7.9 %collective-permute-start.4 = (f32[36,8,128]{2,1,0:T(8,128)S(1)}, f32[36,8,128]{2,1,0:T(8,128)S(1)}, u32[]{:S(2)}, u32[]{:S(2)}) collective-permute-start(f32[36,8,128]{2,1,0:T(8,128)S(1)} %get-tuple-element.23), channel_id=1, source_target_pairs={{0,32},{32,64},{64,96},{96,128},{128,160},{160,192},{192,224},{224... | collective-permute-start | bytes 442376 | tf_op jit(solution)/shard_map/ppermute | solution.py:468

commit v3 on v2

--- a/solution.py
+++ b/solution.py
@@ -4,6 +4,7 @@
 from jax.experimental import pallas as pl
 from jax.experimental.pallas import tpu as pltpu
 from jax.sharding import PartitionSpec as P
+
 
 EDGE = 32
 LANES = 128
@@ -12,11 +13,10 @@
 FIELDS = 3
 MOVED = 2
 KINDS = 5
-SHELL = GROUPS + 6
-CORE = 3 * (GROUPS - 2)
+CORE = 3 * GROUPS
 ROWS = EDGE + 16
 DEEP = EDGE + 8
-XMSG = EDGE + 4
+YMSG = 8 * EDGE + 32
 F32 = jnp.float32
 VMEM = pltpu.VMEM
 
@@ -78,18 +78,15 @@
         copy.wait()
     for g in range(GROUPS):
         pack(boxes, moved, out, g, g, "edge")
-    for side, g in enumerate((0, GROUPS - 1)):
-        for which in range(3):
-            pack(boxes, moved, out, GROUPS + 3 * side + which, g, which)
 
 
 def pack_core(counts_ref, old_ref, out, counts, boxes, sems):
     copies, moved = fetch(counts_ref, old_ref, counts, boxes, sems, MOVED)
     for copy in copies:
         copy.wait()
-    for g in range(1, GROUPS - 1):
+    for g in range(GROUPS):
         for which in range(3):
-            pack(boxes, moved, out, 3 * (g - 1) + which, g, which)
+            pack(boxes, moved, out, 3 * g + which, g, which)
 
 
 def interleave(v):
@@ -106,7 +103,7 @@
     return rows
 
 
-def relayout_edges(counts_ref, old_ref, edges, slabs, counts, boxes, sems):
+def relayout_edges(counts_ref, old_ref, edges, counts, boxes, sems):
     copies, moved = fetch(counts_ref, old_ref, counts, boxes, sems, 0)
     slots = [jnp.maximum(c - moved, 0) for c in range(COLUMN)]
     for f in range(FIELDS):
@@ -114,9 +111,6 @@
         for g in range(GROUPS):
             for r, row in enumerate(interleave([box_tiles(boxes, f, slot, g, "edge") for slot in slots])):
                 edges[f, 4 * g + r] = row
-        for side, g in enumerate((0, GROUPS - 1)):
-            for r, row in enumerate(interleave([boxes[f, slot, :, lane_group(g)] for slot in slots])):
-                slabs[f, side, r] = row
 
 
 def relayout(counts_ref, old_ref, out, counts, boxes, sems):
@@ -140,11 +134,7 @@
 def wire_rows(shell, core, k, g):
     low = iota((8, LANES), 0) < 4
     edge = shell[k, g]
-    if g in (0, GROUPS - 1):
-        base = GROUPS + (3 if g else 0)
-        mid = [shell[k, base + which] for which in range(3)]
-    else:
-        mid = [core[k, 3 * (g - 1) + which] for which in range(3)]
+    mid = [core[k, 3 * g + which] for which in range(3)]
     return jnp.concatenate([jnp.where(low, edge, mid[0]), mid[1], mid[2], jnp.where(low, mid[0], edge)], axis=0)
 
 
@@ -159,17 +149,8 @@
     return high, low
 
 
-def make_faces(counts_ref, shell, edges, slabs, y_up, y_down, x_up, x_down):
+def make_faces(counts_ref, shell, edges, x_up, x_down):
     limit = moved_boxes(counts_ref) * EDGE
-    taken = iota((EDGE, LANES), 1) < limit
-    for side, g in enumerate((0, GROUPS - 1)):
-        out = y_up if side else y_down
-        kinds = [wire_rows(shell, None, k, g) for k in range(KINDS)]
-        for f, at, depth in ((2, 0, 3), (0, 3, 3), (1, 6, 2)):
-            rows = unmix(kinds, f)
-            for j in range(depth):
-                r = 4 - depth + j if side else j
-                out[at + j] = jnp.where(taken, rows[r], slabs[f, side, r])
     taken = iota((8, LANES), 1) < limit
     for g in range(GROUPS):
         kinds = [shell[k, g] for k in range(KINDS)]
@@ -177,24 +158,17 @@
         for r in range(4):
             y = 4 * g + r
             edge = [jnp.where(taken, rows[f][r], edges[f, y]) for f in range(FIELDS)]
-            x_up[y + 2], x_down[y + 2] = pack_x(*edge)
-
-
-def add_corners(before, after, x_up_in, x_down_in, x_up, x_down, tiles, sems):
-    del x_up_in, x_down_in
-    low = iota((8, LANES), 0) < 4
-    places = ((before, 1, 4, 6), (before, 2, 5, 7), (after, 0, 3, 6), (after, 1, 4, 7))
-    for at, (ref, b, p, f) in enumerate(places):
-        edge = [jnp.where(low, ref[i, 0:8], ref[i, 24:32]) for i in (p, f, b)]
-        tiles[0, at], tiles[1, at] = pack_x(*edge)
+            x_up[y], x_down[y] = pack_x(*edge)
+
+
+def add_corners(before, after, y_up_in, y_down_in, y_up, y_down, sems):
+    del y_up_in, y_down_in
     copies = []
-    for way, out in enumerate((x_up, x_down)):
-        for side in range(2):
-            copies.append(
-                pltpu.make_async_copy(
-                    tiles.at[way, pl.ds(2 * side, 2)], out.at[pl.ds((XMSG - 2) * side, 2)], sems.at[way, side]
-                )
-            )
+    for way, (out, first) in enumerate(((y_up, EDGE - 2), (y_down, 0))):
+        for d in range(2):
+            for side, ref in enumerate((before, after)):
+                at = 8 * EDGE + 8 * (2 * d + side)
+                copies.append(pltpu.make_async_copy(ref.at[first + d], out.at[pl.ds(at, 8)], sems.at[way, d, side]))
     for copy in copies:
         copy.start()
     for copy in copies:
@@ -205,7 +179,7 @@
     return (iota(shape, 0) + iota(shape, 1) + shift) & 1 == 0
 
 
-def assemble(counts_ref, own, shell, core, half, mix, rhs):
+def assemble(counts_ref, own, shell, core, half, mix, rhs, y_up, y_down):
     limit = moved_boxes(counts_ref) * EDGE
     taken = iota((EDGE, LANES), 1) < limit
     reds = [is_red((EDGE, LANES), y) for y in range(2)]
@@ -223,6 +197,12 @@
                 mix[y - 1] = jnp.where(reds[(y - 1) % 2], h * p, before)
             before = p
     mix[EDGE - 1] = before
+    for out, first, thin in ((y_up, EDGE - 3, EDGE - 2), (y_down, 0, 0)):
+        for i in range(3):
+            out[EDGE * i : EDGE * (i + 1)] = half[first + i]
+            out[EDGE * (3 + i) : EDGE * (4 + i)] = mix[first + i]
+        for i in range(2):
+            out[EDGE * (6 + i) : EDGE * (7 + i)] = rhs[thin + i]
 
 
 def tile(row):
@@ -257,13 +237,13 @@
     pressures, flux = {}, {}
     for y in (-3, -2, -1, 32, 33, 34):
         ref, k = (y_before, y + 3) if y < 0 else (y_after, y - 32)
-        h = 0.5 * ref[k]
+        h, p = [ref[EDGE * i : EDGE * (i + 1)] for i in (k, 3 + k)]
         half[y + 4, inner] = h
-        pressures[y] = ref[3 + k]
-        flux[y] = h * ref[3 + k]
+        pressures[y] = p
+        flux[y] = h * p
         k = k - 1 if y < 0 else k
         if 0 <= k < 2:
-            rhs[y + 4, inner] = ref[6 + k]
+            rhs[y + 4, inner] = ref[EDGE * (6 + k) : EDGE * (7 + k)]
     flux[0] = half_in[0] * mix_in[0]
     pressures[EDGE - 1] = mix_in[EDGE - 1]
 
@@ -280,27 +260,33 @@
     for y in (-4, -3, -2, -1, 31, 32, 33, 34):
         mix[y + 4, inner] = jnp.where(red_rows[y % 2], flux.get(y + 1, zero), pressures.get(y, zero))
 
-    def strip(i, odd, last):
-        j = i + 2
+    def strip(j, odd, values, last):
         rows = []
-        for ref, at, turn_p, turn_f, kept in ((x_before, 0, 3, 6, last[0]), (x_after, ROWS - 8, 5, 2, last[1])):
-            v = ref[i]
+        for v, at, turn_p, turn_f, kept in zip(values, (0, ROWS - 8), (3, 5), (6, 2), last):
             h = 0.5 * v
             p = pltpu.roll(v, turn_p, 0)
             half[j, tile(at)] = h
             rhs[j, tile(at)] = pltpu.roll(v, turn_f, 0)
             mix[j, tile(at)] = jnp.where(reds[odd], kept, p)
             rows.append(h * p)
-        return rows
+        return tuple(rows)
 
     def strips(k, carry):
-        i = XMSG - 1 - 4 * k
         for d in range(4):
-            carry = strip(i - d, (1 + d) % 2, carry)
-        return tuple(carry)
+            y = EDGE - 1 - 4 * k - d
+            carry = strip(y + 4, (1 + d) % 2, (x_before[y], x_after[y]), carry)
+        return carry
+
+    def corners(ref, d):
+        return [ref[pl.ds(8 * EDGE + 8 * (2 * d + side), 8)] for side in range(2)]
 
     nothing = jnp.zeros((8, LANES), F32)
-    last = lax.fori_loop(0, XMSG // 4, strips, (nothing, nothing))
+    last = (nothing, nothing)
+    for d in (1, 0):
+        last = strip(EDGE + 4 + d, d, corners(y_after, d), last)
+    last = lax.fori_loop(0, EDGE // 4, strips, last)
+    for d in (1, 0):
+        last = strip(2 + d, d, corners(y_before, d), last)
     mix[1, tile(0)], mix[1, tile(ROWS - 8)] = last
 
     lane = iota((8, LANES), 1)
@@ -407,7 +393,7 @@
 
 def call(body, inputs, outputs, scratch, flops, moved, aliases=None, hbm=(), anywhere=False, limit=40 * 2**20):
     vmem, place, far = [pl.BlockSpec(memory_space=m) for m in (pltpu.VMEM, pl.ANY, pltpu.HBM)]
-    kept = set(aliases or {}) if anywhere else ()
+    kept = range(len(inputs)) if anywhere else ()
     return pl.pallas_call(
         body,
         out_shape=[jax.ShapeDtypeStruct(shape, F32) for shape in outputs],
@@ -417,7 +403,6 @@
         input_output_aliases=aliases or {},
         cost_estimate=pl.CostEstimate(flops=flops, bytes_accessed=moved, transcendentals=0),
         compiler_params=pltpu.CompilerParams(vmem_limit_bytes=limit),
-        name=body.__name__,
     )(*inputs)
 
 
@@ -433,42 +418,41 @@
 
     y_ways, x_ways = ends(columns), ends(groups)
 
-    def read(body, outputs, after=None):
+    def read(body, outputs, after=None, limit=54400000):
         table = counts if after is None else lax.optimization_barrier((counts, after))[0]
         scratch = [
             VMEM(counts.shape, jnp.int32),
             VMEM((FIELDS, COLUMN, EDGE, EDGE * EDGE), F32),
             pltpu.SemaphoreType.DMA((FIELDS + 1,)),
         ]
-        return call(body, (table, old_fields), outputs, scratch, 10**6, 2 * 10**6, hbm=(0, 1), limit=40 * 2**20 if after is not None else 54400000)
-
-    face, strip = (8, EDGE, LANES), (XMSG, 8, LANES)
-    deep = (DEEP, ROWS, LANES)
-    (shell,) = read(pack_shell, [(KINDS, SHELL, 8, LANES)])
+        return call(body, (table, old_fields), outputs, scratch, 10**6, 2 * 10**6, hbm=(0, 1), limit=limit)
+
+    strip, message = (EDGE, 8, LANES), (YMSG, LANES)
+    deep, block = (DEEP, ROWS, LANES), (EDGE, EDGE, LANES)
+    (shell,) = read(pack_shell, [(KINDS, GROUPS, 8, LANES)])
+    (core,) = read(pack_core, [(KINDS, CORE, 8, LANES)], shell)
     shell = lax.ppermute(shell, ("grp", "dev"), chain)
-    (core,) = read(pack_core, [(KINDS, CORE, 8, LANES)])
     core = lax.ppermute(core, ("grp", "dev"), chain)
-    edges, slabs = read(relayout_edges, [(FIELDS, EDGE, 8, LANES), (FIELDS, 2, 4, EDGE, LANES)])
-    y_up, y_down, x_up, x_down = call(
-        make_faces, (counts, shell, edges, slabs), [face, face, strip, strip], [], 10**6, 10**6
-    )
-    (own,) = read(relayout, [(FIELDS, EDGE, EDGE, LANES)], y_up)
-    y_before = lax.ppermute(y_up, "dev", y_ways[0])
-    y_after = lax.ppermute(y_down, "dev", y_ways[1])
-    x_up, x_down = call(
+    (edges,) = read(relayout_edges, [(FIELDS, EDGE, 8, LANES)])
+    x_up, x_down = call(make_faces, (counts, shell, edges), [strip, strip], [], 10**6, 10**6)
+    x_before = lax.ppermute(x_up, "grp", x_ways[0])
+    x_after = lax.ppermute(x_down, "grp", x_ways[1])
+    (own,) = read(relayout, [(FIELDS, EDGE, EDGE, LANES)], x_up, 40 * 2**20)
+    half, mix, rhs, y_up, y_down = call(
+        assemble, (counts, own, shell, core), [block, block, block, message, message], [], 10**6, 10**6
+    )
+    y_up, y_down = call(
         add_corners,
-        (y_before, y_after, x_up, x_down),
-        [strip, strip],
-        [VMEM((2, 4, 8, LANES), F32), pltpu.SemaphoreType.DMA((2, 2))],
+        (x_before, x_after, y_up, y_down),
+        [message, message],
+        [pltpu.SemaphoreType.DMA((2, 2, 2))],
         10**4,
         10**5,
         aliases={2: 0, 3: 1},
         anywhere=True,
     )
-    x_before = lax.ppermute(x_up, "grp", x_ways[0])
-    x_after = lax.ppermute(x_down, "grp", x_ways[1])
-    table = lax.optimization_barrier((counts, x_up))[0]
-    half, mix, rhs = call(assemble, (table, own, shell, core), [(EDGE, EDGE, LANES)] * 3, [], 10**6, 10**6)
+    y_before = lax.ppermute(y_up, "dev", y_ways[0])
+    y_after = lax.ppermute(y_down, "dev", y_ways[1])
     flat = (EDGE * EDGE, LANES)
     outs = call(
         sweep,

time: 46 us -> 56.5 us (1.23)
  the two profiles are of different devices: /device:TPU:225 before, /device:TPU:223 now
where the time goes in v3:
time: 56.5 us; the launch traced here: 56.2 us
  starting transfers between devices  25.3 us (45%)
  waiting for transfers between devices  16.6 us (29%)
  Pallas kernels  12.8 us (23%)
  between operations  0.78 us (1%)
  local copies, waits for them, and re-layouts  0.68 us (1%)
    pallas_call x8, Pallas kernels, call(): pl.pallas_call(body, out_shape=[jax.ShapeDtypeStruct(shape, F32) for shap...  12.8 us
    ppermute x1, waiting for transfers between devices, per_device(): shell = lax.ppermute(shell, ('grp', 'dev'), chain)  8.66 us
    ppermute x1, starting transfers between devices, per_device(): y_before = lax.ppermute(y_up, 'dev', y_ways[0])  7.43 us
    ppermute x1, waiting for transfers between devices, per_device(): y_after = lax.ppermute(y_down, 'dev', y_ways[1])  7.42 us
    ppermute x1, starting transfers between devices, per_device(): x_before = lax.ppermute(x_up, 'grp', x_ways[0])  5.11 us
    ppermute x1, starting transfers between devices, per_device(): core = lax.ppermute(core, ('grp', 'dev'), chain)  4.33 us
    ppermute x1, starting transfers between devices, per_device(): x_after = lax.ppermute(x_down, 'grp', x_ways[1])  3.44 us
    ppermute x1, starting transfers between devices, per_device(): shell = lax.ppermute(shell, ('grp', 'dev'), chain)  3.12 us
  transfers between devices with their start and end apart: 6, of which 3 were waited for; matrix products, arithmetic and copies ran while one was open for 0% of the time, Pallas kernels for 8%

profile of v3, /device:TPU:223, one launch (start us, length us, event | category | flops | bytes accessed | tf_op | source)
XLA Modules:
  0.0 56.2 jit_solution(7412684346619155252)
XLA Ops:
  0.6 0.0 copy-start.1
  0.6 0.7 %copy-done.1 = s32[512]{0:T(512)S(1)} copy-done((s32[512]{0:T(512)S(1)}, s32[512]{0:T(512)}, u32[]{:S(2)}) %copy-start.1) | copy-done | bytes 2072
  1.3 1.5 %shard_map.41 = f32[5,8,8,128]{3,2,1,0:T(8,128)S(1)} custom-call(s32[4,128]{1,0:T(4,128)S(1)} %bitcast.3, f32[3,8,32,1024]{3,2,1,0:T(8,128)} %old_ref.7), custom_call_target="tpu_custom_call" | custom-call | flops 1000000 | bytes 2000000 | tf_op jit(solution)/shard_map/pallas_call | solution.py:397
  2.8 0.0 copy-start
  2.8 1.7 %shard_map.45 = f32[5,24,8,128]{3,2,1,0:T(8,128)S(1)} custom-call(s32[4,128]{1,0:T(4,128)S(1)} %bitcast.4, f32[3,8,32,1024]{3,2,1,0:T(8,128)} %old_ref.7), custom_call_target="tpu_custom_call" | custom-call | flops 1000000 | bytes 2000000 | tf_op jit(solution)/shard_map/pallas_call | solution.py:397
  4.5 4.3 %collective-permute-start.1 = (f32[5,24,8,128]{3,2,1,0:T(8,128)S(1)}, f32[5,24,8,128]{3,2,1,0:T(8,128)S(1)}, u32[]{:S(2)}, u32[]{:S(2)}) collective-permute-start(f32[5,24,8,128]{3,2,1,0:T(8,128)S(1)} %shard_map.45), channel_id=1, source_target_pairs={{0,1},{1,2},{2,3},{3,4},{4,5},{5,6},{6,7},{7,8},{8,9},{9,10},{10,1... | collective-permute-start | bytes 1474568 | tf_op jit(solution)/shard_map/ppermute | solution.py:435
  8.9 3.1 %collective-permute-start = (f32[5,8,8,128]{3,2,1,0:T(8,128)S(1)}, f32[5,8,8,128]{3,2,1,0:T(8,128)S(1)}, u32[]{:S(2)}, u32[]{:S(2)}) collective-permute-start(f32[5,8,8,128]{3,2,1,0:T(8,128)S(1)} %shard_map.41), channel_id=1, source_target_pairs={{0,1},{1,2},{2,3},{3,4},{4,5},{5,6},{6,7},{7,8},{8,9},{9,10},{10,1... | collective-permute-start | bytes 491528 | tf_op jit(solution)/shard_map/ppermute | solution.py:434
  12.0 1.6 %shard_map.42.edges = f32[3,32,8,128]{3,2,1,0:T(8,128)S(1)} custom-call(s32[4,128]{1,0:T(4,128)S(1)} %bitcast.5, f32[3,8,32,1024]{3,2,1,0:T(8,128)} %old_ref.7), custom_call_target="tpu_custom_call" | custom-call | flops 1000000 | bytes 2000000 | tf_op jit(solution)/shard_map/pallas_call | solution.py:397
  13.6 8.7 %collective-permute-done.shell = f32[5,8,8,128]{3,2,1,0:T(8,128)S(1)} collective-permute-done((f32[5,8,8,128]{3,2,1,0:T(8,128)S(1)}, f32[5,8,8,128]{3,2,1,0:T(8,128)S(1)}, u32[]{:S(2)}, u32[]{:S(2)}) %collective-permute-start) | collective-permute-done | bytes 163872 | tf_op jit(solution)/shard_map/ppermute | solution.py:434
  22.2 0.2 shard_map.43
  22.4 3.4 %collective-permute-start.3 = (f32[32,8,128]{2,1,0:T(8,128)S(1)}, f32[32,8,128]{2,1,0:T(8,128)S(1)}, u32[]{:S(2)}, u32[]{:S(2)}) collective-permute-start(f32[32,8,128]{2,1,0:T(8,128)S(1)} %get-tuple-element.21), channel_id=1, source_target_pairs={{32,0},{64,32},{96,64},{128,96},{160,128},{192,160},{224,192},{256... | collective-permute-start | bytes 393224 | tf_op jit(solution)/shard_map/ppermute | solution.py:439
  25.9 5.1 %collective-permute-start.2 = (f32[32,8,128]{2,1,0:T(8,128)S(1)}, f32[32,8,128]{2,1,0:T(8,128)S(1)}, u32[]{:S(2)}, u32[]{:S(2)}) collective-permute-start(f32[32,8,128]{2,1,0:T(8,128)S(1)} %get-tuple-element.15), channel_id=1, source_target_pairs={{0,32},{32,64},{64,96},{96,128},{128,160},{160,192},{192,224},{224... | collective-permute-start | bytes 393224 | tf_op jit(solution)/shard_map/ppermute | solution.py:438
  31.0 0.0 copy-done
  31.0 2.3 %shard_map.44.own = f32[3,32,32,128]{3,2,1,0:T(8,128)S(1)} custom-call(s32[4,128]{1,0:T(4,128)S(1)} %bitcast.7, f32[3,8,32,1024]{3,2,1,0:T(8,128)S(1)} %copy-done), custom_call_target="tpu_custom_call" | custom-call | flops 1000000 | bytes 2000000 | tf_op jit(solution)/shard_map/pallas_call | solution.py:397
  33.3 0.0 collective-permute-done.1.core
  33.4 0.4 shard_map.46
  33.8 0.0 collective-permute-done.3.after.x_after
  33.8 0.0 collective-permute-done.2.before.x_before
  33.8 0.1 shard_map.47
  34.0 7.4 %collective-permute-start.4 = (f32[288,128]{1,0:T(8,128)S(1)}, f32[288,128]{1,0:T(8,128)S(1)}, u32[]{:S(2)}, u32[]{:S(2)}) collective-permute-start(f32[288,128]{1,0:T(8,128)S(1)} %get-tuple-element.24), channel_id=1, source_target_pairs={{0,1},{1,2},{2,3},{3,4},{4,5},{5,6},{6,7},{7,8},{8,9},{9,10},{10,1... | collective-permute-start | bytes 442376 | tf_op jit(solution)/shard_map/ppermute | solution.py:454
  41.4 1.9 %collective-permute-start.5 = (f32[288,128]{1,0:T(8,128)S(1)}, f32[288,128]{1,0:T(8,128)S(1)}, u32[]{:S(2)}, u32[]{:S(2)}) collective-permute-start(f32[288,128]{1,0:T(8,128)S(1)} %get-tuple-element.25), channel_id=1, source_target_pairs={{1,0},{2,1},{3,2},{4,3},{5,4},{6,5},{7,6},{8,7},{9,8},{10,9},{11,1... | collective-permute-start | bytes 442376 | tf_op jit(solution)/shard_map/ppermute | solution.py:455
  43.3 0.5 collective-permute-done.4.y_before
  43.9 7.4 %collective-permute-done.5.y_after = f32[288,128]{1,0:T(8,128)S(1)} collective-permute-done((f32[288,128]{1,0:T(8,128)S(1)}, f32[288,128]{1,0:T(8,128)S(1)}, u32[]{:S(2)}, u32[]{:S(2)}) %collective-permute-start.5) | collective-permute-done | bytes 147488 | tf_op jit(solution)/shard_map/ppermute | solution.py:455
  51.3 5.0 %shard_map.48 = (f32[1024,128]{1,0:T(8,128)}, f32[1024,128]{1,0:T(8,128)}) custom-call(f32[32,32,128]{2,1,0:T(8,128)S(1)} %get-tuple-element.18.half_in, f32[32,32,128]{2,1,0:T(8,128)S(1)} %get-tuple-element.19.mix_in, f32[32,32,128]{2,1,0:T(8,128)S(1)} %get-tuple-element.20.rhs_in, f32[288,128]{1,0:T(8,128)S(1)} %collective-permute-done.4.y_before, ...), custom_call_target="tpu_custom_call" | custom-call | flops 100000000 | bytes 5000000 | tf_op jit(solution)/shard_map/pallas_call | solution.py:397
Async XLA Ops:
  0.6 0.7 %copy-start.1 = (s32[512]{0:T(512)S(1)}, s32[512]{0:T(512)}, u32[]{:S(2)}) copy-start(s32[512]{0:T(512)} %param.3) | copy-start | bytes 6148
  2.8 28.2 %copy-start = (f32[3,8,32,1024]{3,2,1,0:T(8,128)S(1)}, f32[3,8,32,1024]{3,2,1,0:T(8,128)}, u32[]{:S(2)}) copy-start(f32[3,8,32,1024]{3,2,1,0:T(8,128)} %old_ref.7) | copy-start | bytes 9437188
  4.5 28.8 %collective-permute-start.1 = (f32[5,24,8,128]{3,2,1,0:T(8,128)S(1)}, f32[5,24,8,128]{3,2,1,0:T(8,128)S(1)}, u32[]{:S(2)}, u32[]{:S(2)}) collective-permute-start(f32[5,24,8,128]{3,2,1,0:T(8,128)S(1)} %shard_map.45), channel_id=1, source_target_pairs={{0,1},{1,2},{2,3},{3,4},{4,5},{5,6},{6,7},{7,8},{8,9},{9,10},{10,1... | collective-permute-start | bytes 1474568 | tf_op jit(solution)/shard_map/ppermute | solution.py:435
  8.9 13.4 %collective-permute-start = (f32[5,8,8,128]{3,2,1,0:T(8,128)S(1)}, f32[5,8,8,128]{3,2,1,0:T(8,128)S(1)}, u32[]{:S(2)}, u32[]{:S(2)}) collective-permute-start(f32[5,8,8,128]{3,2,1,0:T(8,128)S(1)} %shard_map.41), channel_id=1, source_target_pairs={{0,1},{1,2},{2,3},{3,4},{4,5},{5,6},{6,7},{7,8},{8,9},{9,10},{10,1... | collective-permute-start | bytes 491528 | tf_op jit(solution)/shard_map/ppermute | solution.py:434
  22.4 11.4 %collective-permute-start.3 = (f32[32,8,128]{2,1,0:T(8,128)S(1)}, f32[32,8,128]{2,1,0:T(8,128)S(1)}, u32[]{:S(2)}, u32[]{:S(2)}) collective-permute-start(f32[32,8,128]{2,1,0:T(8,128)S(1)} %get-tuple-element.21), channel_id=1, source_target_pairs={{32,0},{64,32},{96,64},{128,96},{160,128},{192,160},{224,192},{256... | collective-permute-start | bytes 393224 | tf_op jit(solution)/shard_map/ppermute | solution.py:439
  25.9 7.9 %collective-permute-start.2 = (f32[32,8,128]{2,1,0:T(8,128)S(1)}, f32[32,8,128]{2,1,0:T(8,128)S(1)}, u32[]{:S(2)}, u32[]{:S(2)}) collective-permute-start(f32[32,8,128]{2,1,0:T(8,128)S(1)} %get-tuple-element.15), channel_id=1, source_target_pairs={{0,32},{32,64},{64,96},{96,128},{128,160},{160,192},{192,224},{224... | collective-permute-start | bytes 393224 | tf_op jit(solution)/shard_map/ppermute | solution.py:438
  34.0 9.9 %collective-permute-start.4 = (f32[288,128]{1,0:T(8,128)S(1)}, f32[288,128]{1,0:T(8,128)S(1)}, u32[]{:S(2)}, u32[]{:S(2)}) collective-permute-start(f32[288,128]{1,0:T(8,128)S(1)} %get-tuple-element.24), channel_id=1, source_target_pairs={{0,1},{1,2},{2,3},{3,4},{4,5},{5,6},{6,7},{7,8},{8,9},{9,10},{10,1... | collective-permute-start | bytes 442376 | tf_op jit(solution)/shard_map/ppermute | solution.py:454
  41.4 9.9 %collective-permute-start.5 = (f32[288,128]{1,0:T(8,128)S(1)}, f32[288,128]{1,0:T(8,128)S(1)}, u32[]{:S(2)}, u32[]{:S(2)}) collective-permute-start(f32[288,128]{1,0:T(8,128)S(1)} %get-tuple-element.25), channel_id=1, source_target_pairs={{1,0},{2,1},{3,2},{4,3},{5,4},{6,5},{7,6},{8,7},{9,8},{10,9},{11,1... | collective-permute-start | bytes 442376 | tf_op jit(solution)/shard_map/ppermute | solution.py:455

commit v4 on v3

v4 whole, which is shorter than its diff:
```python
import jax
import jax.numpy as jnp
from jax import lax
from jax.experimental import pallas as pl
from jax.experimental.pallas import tpu as pltpu
from jax.sharding import PartitionSpec as P


EDGE = 32
LANES = 128
GROUPS = EDGE * EDGE // LANES
COLUMN = 4
FIELDS = 3
MOVED = 2
KINDS = 5
RIM = 6
CORE = 3 * (GROUPS - 2)
ROWS = EDGE + 16
DEEP = EDGE + 8
YMSG = 8 * EDGE + 32
F32 = jnp.float32
VMEM = pltpu.VMEM


def iota(shape, dim):
    return lax.broadcasted_iota(jnp.int32, shape, dim)


def moved_boxes(counts_ref):
    device = lax.axis_index("grp") * lax.axis_size("dev") + lax.axis_index("dev")
    counts = counts_ref[...]
    index = iota(counts.shape, 0) * LANES + iota(counts.shape, 1)
    start = jnp.sum(jnp.where(index < device, counts, 0))
    return jnp.clip(start - device * COLUMN, 0, MOVED)


def lane_group(g):
    return pl.ds(g * LANES, LANES)


def fetch(counts_ref, old_ref, counts, boxes, sems, first):
    copies = [pltpu.make_async_copy(counts_ref, counts, sems.at[FIELDS])]
    for f in range(FIELDS):
        copies.append(pltpu.make_async_copy(old_ref.at[f, pl.ds(first, COLUMN)], boxes.at[f], sems.at[f]))
    for copy in copies:
        copy.start()
    copies[0].wait()
    return copies[1:], moved_boxes(counts)


def box_tiles(boxes, f, c, g, which):
    low = iota((8, LANES), 0) < 4
    if which == "edge":
        return jnp.where(low, boxes[f, c, 0:8, lane_group(g)], boxes[f, c, 24:32, lane_group(g)])
    if which == 0:
        return jnp.where(low, boxes[f, c, 24:32, lane_group(g)], boxes[f, c, 0:8, lane_group(g)])
    return boxes[f, c, 8 * which : 8 * which + 8, lane_group(g)]


def pack(boxes, moved, out, at, g, which):
    shape = (8, LANES)
    lane = iota(shape, 1)
    block = lane // EDGE
    black = (iota(shape, 0) + block + lane) % 2 == 1
    even = block % 2 == 0
    first, second = [
        [box_tiles(boxes, f, MOVED + c - moved, g, which) for f in range(FIELDS)] for c in range(MOVED)
    ]
    turned = [pltpu.roll(v, EDGE, 1) for v in second]
    out[0, at] = jnp.where(black, first[0], turned[0])
    for f in (1, 2):
        out[2 * f - 1, at] = jnp.where(even, first[f], turned[f])
        out[2 * f, at] = jnp.where(even, turned[f], first[f])


def pack_shell(counts_ref, old_ref, out, counts, boxes, sems):
    copies, moved = fetch(counts_ref, old_ref, counts, boxes, sems, MOVED)
    for copy in copies:
        copy.wait()
    for g in range(GROUPS):
        pack(boxes, moved, out, g, g, "edge")


def pack_rest(counts_ref, old_ref, rim, core, counts, boxes, sems):
    copies, moved = fetch(counts_ref, old_ref, counts, boxes, sems, MOVED)
    for copy in copies:
        copy.wait()
    for g in range(GROUPS):
        for which in range(3):
            if g in (0, GROUPS - 1):
                pack(boxes, moved, rim, (3 if g else 0) + which, g, which)
            else:
                pack(boxes, moved, core, 3 * (g - 1) + which, g, which)


def interleave(v):
    lane = iota(v[0].shape, 1)
    half = lane < 2 * EDGE
    even = (lane // EDGE) % 2 == 0
    w = [pltpu.roll(a, 2 * EDGE, 1) for a in v]
    a0, a1 = jnp.where(half, v[0], w[2]), jnp.where(half, v[1], w[3])
    a2, a3 = jnp.where(half, w[0], v[2]), jnp.where(half, w[1], v[3])
    rows = []
    for a, b in ((a0, a1), (a2, a3)):
        rows.append(jnp.where(even, a, pltpu.roll(b, EDGE, 1)))
        rows.append(jnp.where(even, pltpu.roll(a, LANES - EDGE, 1), b))
    return rows


def relayout_edges(counts_ref, old_ref, edges, slabs, counts, boxes, sems):
    copies, moved = fetch(counts_ref, old_ref, counts, boxes, sems, 0)
    slots = [jnp.maximum(c - moved, 0) for c in range(COLUMN)]
    for f in range(FIELDS):
        copies[f].wait()
        for g in range(GROUPS):
            for r, row in enumerate(interleave([box_tiles(boxes, f, slot, g, "edge") for slot in slots])):
                edges[f, 4 * g + r] = row
        for side, g in enumerate((0, GROUPS - 1)):
            for r, row in enumerate(interleave([boxes[f, slot, :, lane_group(g)] for slot in slots])):
                slabs[f, side, r] = row


def relayout(counts_ref, old_ref, out, counts, boxes, sems):
    copies, moved = fetch(counts_ref, old_ref, counts, boxes, sems, 0)
    slots = [jnp.maximum(c - moved, 0) for c in range(COLUMN)]
    for f in range(FIELDS):
        copies[f].wait()
        for g in range(GROUPS):
            for r, row in enumerate(interleave([boxes[f, slot, :, lane_group(g)] for slot in slots])):
                out[f, 4 * g + r] = row


def unmix(kinds, f):
    if f == 0:
        a = b = kinds[0]
    else:
        a, b = kinds[2 * f - 1], kinds[2 * f]
    return [a, pltpu.roll(b, LANES - EDGE, 1), pltpu.roll(a, 2 * EDGE, 1), pltpu.roll(b, EDGE, 1)]


def wire_rows(shell, rim, core, k, g):
    low = iota((8, LANES), 0) < 4
    edge = shell[k, g]
    if g in (0, GROUPS - 1):
        mid = [rim[k, (3 if g else 0) + which] for which in range(3)]
    else:
        mid = [core[k, 3 * (g - 1) + which] for which in range(3)]
    return jnp.concatenate([jnp.where(low, edge, mid[0]), mid[1], mid[2], jnp.where(low, mid[0], edge)], axis=0)


def pack_x(pressure, right_side, coefficient):
    row = iota((8, LANES), 0)
    high = jnp.where(
        row >= 5, coefficient, jnp.where(row >= 2, pltpu.roll(pressure, 5, 0), pltpu.roll(right_side, 2, 0))
    )
    low = jnp.where(
        row < 3, coefficient, jnp.where(row < 6, pltpu.roll(pressure, 3, 0), pltpu.roll(right_side, 6, 0))
    )
    return high, low


def make_faces(counts_ref, shell, edges, x_up, x_down):
    limit = moved_boxes(counts_ref) * EDGE
    taken = iota((8, LANES), 1) < limit
    for g in range(GROUPS):
        kinds = [shell[k, g] for k in range(KINDS)]
        rows = [unmix(kinds, f) for f in range(FIELDS)]
        for r in range(4):
            y = 4 * g + r
            edge = [jnp.where(taken, rows[f][r], edges[f, y]) for f in range(FIELDS)]
            x_up[y], x_down[y] = pack_x(*edge)


def make_slabs(counts_ref, shell, rim, slabs, y_up, y_down):
    taken = iota((EDGE, LANES), 1) < moved_boxes(counts_ref) * EDGE
    for side, g in enumerate((0, GROUPS - 1)):
        out = y_up if side else y_down
        kinds = [wire_rows(shell, rim, None, k, g) for k in range(KINDS)]
        for f, at, depth in ((2, 0, 3), (0, 3, 3), (1, 6, 2)):
            rows = unmix(kinds, f)
            for j in range(depth):
                r = 4 - depth + j if side else j
                slab = jnp.where(taken, rows[r], slabs[f, side, r])
                out[EDGE * (at + j) : EDGE * (at + j + 1)] = 0.5 * slab if f == 2 else slab


def add_corners(before, after, y_up_in, y_down_in, y_up, y_down, sems):
    del y_up_in, y_down_in
    copies = []
    for way, (out, first) in enumerate(((y_up, EDGE - 2), (y_down, 0))):
        for d in range(2):
            for side, ref in enumerate((before, after)):
                at = 8 * EDGE + 8 * (2 * d + side)
                copies.append(pltpu.make_async_copy(ref.at[first + d], out.at[pl.ds(at, 8)], sems.at[way, d, side]))
    for copy in copies:
        copy.start()
    for copy in copies:
        copy.wait()


def is_red(shape, shift):
    return (iota(shape, 0) + iota(shape, 1) + shift) & 1 == 0


def assemble(counts_ref, own, shell, rim, core, half, mix, rhs):
    limit = moved_boxes(counts_ref) * EDGE
    taken = iota((EDGE, LANES), 1) < limit
    reds = [is_red((EDGE, LANES), y) for y in range(2)]
    before = None
    for g in range(GROUPS):
        kinds = [wire_rows(shell, rim, core, k, g) for k in range(KINDS)]
        parts = [unmix(kinds, f) for f in range(FIELDS)]
        for r in range(4):
            y = 4 * g + r
            p, f, b = [jnp.where(taken, parts[i][r], own[i, y]) for i in range(FIELDS)]
            h = 0.5 * b
            half[y] = h
            rhs[y] = f
            if y:
                mix[y - 1] = jnp.where(reds[(y - 1) % 2], h * p, before)
            before = p
    mix[EDGE - 1] = before


def tile(row):
    return pl.ds(row, 8)


class Sweep:
    def __init__(self, shift, out_p, out_r, half, mix, rhs, mix2, mix3, new1, new2, inv, tot, rest):
        self.shift, self.out_p, self.out_r = shift, out_p, out_r
        self.half, self.mix, self.rhs, self.mix2, self.mix3 = half, mix, rhs, mix2, mix3
        self.new1, self.new2, self.inv, self.tot, self.rest = new1, new2, inv, tot, rest
        shape = (8, LANES)
        lane, self.row = iota(shape, 1), iota(shape, 0)
        self.first_lane, self.last_lane = lane == 0, lane == LANES - 1
        self.reds = [is_red(shape, y) for y in range(2)]
        self.nothing = jnp.zeros(shape, F32)
        grp = lax.axis_index("grp")
        low = self.row >= 2 * (grp == 0).astype(jnp.int32)
        high = self.row < 8 - 6 * (grp == lax.axis_size("grp") - 1).astype(jnp.int32)
        self.open_x = [low, None, None, None, high]

    def six(self, ref, y, top, count):
        j = y + self.shift
        sums = []
        for t in range(count):
            r = top + 8 * t
            v = ref[j, tile(r)]
            below = jnp.where(self.first_lane, 0.0, pltpu.roll(v, 1, 1))
            above = jnp.where(self.last_lane, 0.0, pltpu.roll(v, LANES - 1, 1))
            x = ref[j, tile(r - 1)] + ref[j, tile(r + 1)]
            sums.append(((below + above) + x) + (ref[j - 1, tile(r)] + ref[j + 1, tile(r)]))
        return sums

    def red(self, y, odd, carry, shut=None):
        flow_before, new_before = carry
        around = self.six(self.half, y, 6, 5)
        flow = self.six(self.mix, y, 6, 5)
        news = []
        j = y + self.shift
        for t in range(5):
            r = tile(6 + 8 * t)
            h = self.half[j, r]
            total = 6.0 * h + around[t]
            inverse = 1.0 / total
            if self.open_x[t] is not None:
                inverse = jnp.where(self.open_x[t], inverse, 0.0)
            if shut is not None:
                inverse = jnp.where(self.row >= 8 * shut, inverse, 0.0)
            new = (self.rhs[j, r] + (h * flow[t] + flow_before[t])) * inverse
            self.new1[j, r] = new
            self.inv[j, r] = inverse
            self.tot[j, r] = total
            self.mix2[j - 1, r] = jnp.where(self.reds[1 - odd], new_before[t], h * new)
            news.append(new)
        return flow, news

    def black(self, y, odd, carry):
        flow_before, new_before = carry
        flow = self.six(self.mix2, y, 7, 5)
        news = []
        j = y + self.shift
        for t in range(5):
            r = tile(7 + 8 * t)
            h = self.half[j, r]
            full = self.rhs[j, r] + (h * flow[t] + flow_before[t])
            new = full * self.inv[j, r]
            self.new2[j, r] = new
            self.rest[j, r] = full - self.tot[j, r] * new
            self.mix3[j - 1, r] = jnp.where(self.reds[1 - odd], new_before[t], h * new)
            news.append(new)
        return flow, news

    def finish(self, y, odd, flow_before):
        flow = self.six(self.mix3, y, 8, 4)
        j = y + self.shift
        for t in range(4):
            r = tile(8 + 8 * t)
            mine = self.new1[j, r]
            left = (self.rhs[j, r] + (self.half[j, r] * flow[t] + flow_before[t])) - self.tot[j, r] * mine
            rows = pl.ds(y + 8 * t * EDGE, 8, stride=EDGE)
            self.out_p[rows, :] = jnp.where(self.reds[odd], mine, self.new2[j, r])
            self.out_r[rows, :] = jnp.where(self.reds[odd], left, self.rest[j, r])
        return flow

    def strip(self, y, odd, values, last):
        rows = []
        j = y + self.shift
        for v, at, turn_p, turn_f, kept in zip(values, (0, ROWS - 8), (3, 5), (6, 2), last):
            h = 0.5 * v
            p = pltpu.roll(v, turn_p, 0)
            self.half[j, tile(at)] = h
            self.rhs[j, tile(at)] = pltpu.roll(v, turn_f, 0)
            self.mix[j, tile(at)] = jnp.where(self.reds[odd], kept, p)
            rows.append(h * p)
        return tuple(rows)


def fours(first, count, step, carry):
    def body(k, carry):
        for d in range(4):
            carry = step(first + 4 * k + d, (first + d) % 2, carry)
        return carry

    return lax.fori_loop(0, count // 4, body, carry)


INNER = pl.ds(8, EDGE)


def sweep_inner(half_in, mix_in, rhs_in, x_before, x_after, *refs):
    w = Sweep(4, *refs)
    w.mix[3, INNER] = half_in[0] * mix_in[0]

    def take_in(y, odd, carry):
        w.half[y + 4, INNER] = half_in[y]
        w.mix[y + 4, INNER] = mix_in[y]
        w.rhs[y + 4, INNER] = rhs_in[y]
        return carry

    fours(0, EDGE, take_in, 0)

    def strips(k, odd, carry):
        y = EDGE - 1 - k
        return w.strip(y, 1 - odd, (x_before[y], x_after[y]), carry)

    last = fours(0, EDGE, strips, (w.nothing, w.nothing))
    w.mix[3, tile(0)], w.mix[3, tile(ROWS - 8)] = last
    carry = w.red(1, 1, (w.six(w.mix, 0, 6, 5), [w.nothing] * 5))
    carry = fours(2, EDGE - 4, w.red, carry)
    carry = w.red(EDGE - 2, 0, carry)
    for t in range(5):
        w.mix2[EDGE + 2, tile(6 + 8 * t)] = carry[1][t]
    carry = fours(2, EDGE - 4, w.black, (w.six(w.mix2, 1, 7, 5), [w.nothing] * 5))
    for t in range(5):
        w.mix3[EDGE + 1, tile(7 + 8 * t)] = carry[1][t]
    flow = w.finish(3, 1, w.six(w.mix3, 2, 8, 4))
    flow = fours(4, EDGE - 8, w.finish, flow)
    w.finish(EDGE - 4, 0, flow)


KEPT = ("half", "mix", "rhs", "mix2", "mix3", "new1", "new2", "inv", "tot", "rest")
NEAR = (
    ((0, 3), (0, 2), (0, 3), (1, 3), (2, 4), (1, 3), (2, 3), (1, 2), (1, 3), (2, 3)),
    ((29, 32), (29, 32), (29, 32), (28, 30), (27, 29), (29, 31), (29, 30), (30, 31), (29, 31), (29, 30)),
)


def sweep_outer(y_before, y_after, x_before, x_after, part_p, part_r, *refs):
    n = len(KEPT)
    old, (out_p, out_r), new = refs[:n], refs[n : n + 2], refs[n + 2 :]
    out_p[...] = part_p[...]
    out_r[...] = part_r[...]
    dev = lax.axis_index("dev")
    red_rows = [is_red((EDGE, LANES), y) for y in range(2)]
    zero = jnp.zeros((EDGE, LANES), F32)
    sides = [Sweep(shift, out_p, out_r, *[ref.at[i] for ref in new]) for i, shift in enumerate((4, -26))]
    for side, (w, spans) in enumerate(zip(sides, NEAR)):
        for name, ref, (first, end) in zip(KEPT, old, spans):
            for y in range(first, end):
                getattr(w, name)[y + w.shift] = ref[y + 4]
        source = y_after if side else y_before
        pressures, flux = {}, {}
        for k, y in enumerate(range(EDGE, EDGE + 3) if side else range(-3, 0)):
            h, p = [source[EDGE * i : EDGE * (i + 1)] for i in (k, 3 + k)]
            w.half[y + w.shift, INNER] = h
            pressures[y] = p
            flux[y] = h * p
            k = k if side else k - 1
            if 0 <= k < 2:
                w.rhs[y + w.shift, INNER] = source[EDGE * (6 + k) : EDGE * (7 + k)]
        edge = (EDGE - 1 if side else 0) + w.shift
        if side:
            pressures[EDGE - 1] = w.mix[edge, INNER]
        else:
            flux[0] = w.half[edge, INNER] * w.mix[edge, INNER]
        for y in range(EDGE - 1, EDGE + 3) if side else range(-4, 0):
            w.mix[y + w.shift, INNER] = jnp.where(red_rows[y % 2], flux.get(y + 1, zero), pressures.get(y, zero))

    def corners(ref, d):
        return [ref[pl.ds(8 * EDGE + 8 * (2 * d + side), 8)] for side in range(2)]

    low, high = sides
    last = (low.nothing, low.nothing)
    for d in (1, 0):
        last = high.strip(EDGE + d, d, corners(y_after, d), last)
    high.strip(EDGE - 1, 1, (x_before[EDGE - 1], x_after[EDGE - 1]), last)
    v = (x_before[0], x_after[0])
    last = tuple(0.5 * a * pltpu.roll(a, turn, 0) for a, turn in zip(v, (3, 5)))
    for d in (1, 0):
        last = low.strip(d - 2, d, corners(y_before, d), last)
    low.mix[1, tile(0)], low.mix[1, tile(ROWS - 8)] = last

    low_shut = (dev == 0).astype(jnp.int32)
    high_shut = (dev == lax.axis_size("dev") - 1).astype(jnp.int32)
    carry = (low.six(low.mix, -3, 6, 5), [low.nothing] * 5)
    carry = low.red(-2, 0, carry, low_shut)
    carry = low.red(-1, 1, carry, low_shut)
    carry = low.red(0, 0, carry)
    for t in range(5):
        r = tile(6 + 8 * t)
        low.mix2[4, r] = jnp.where(low.reds[0], carry[1][t], low.half[5, r] * low.new1[5, r])
    top = EDGE - 2
    carry = (high.six(high.mix, top, 6, 5), [high.new1[top + high.shift, tile(6 + 8 * t)] for t in range(5)])
    carry = high.red(top + 1, 1, carry)
    carry = high.red(top + 2, 0, carry, high_shut)
    carry = high.red(top + 3, 1, carry, high_shut)
    for t in range(5):
        high.mix2[top + 3 + high.shift, tile(6 + 8 * t)] = carry[1][t]

    carry = (low.six(low.mix2, -2, 7, 5), [low.nothing] * 5)
    for y in (-1, 0, 1):
        carry = low.black(y, y % 2, carry)
    for t in range(5):
        r = tile(7 + 8 * t)
        low.mix3[5, r] = jnp.where(low.reds[1], carry[1][t], low.half[6, r] * low.new2[6, r])
    top = EDGE - 3
    carry = (high.six(high.mix2, top, 7, 5), [high.new2[top + high.shift, tile(7 + 8 * t)] for t in range(5)])
    for y in range(top + 1, top + 4):
        carry = high.black(y, y % 2, carry)
    for t in range(5):
        high.mix3[top + 3 + high.shift, tile(7 + 8 * t)] = carry[1][t]

    flow = low.six(low.mix3, -1, 8, 4)
    for y in (0, 1, 2):
        flow = low.finish(y, y % 2, flow)
    flow = high.six(high.mix3, EDGE - 4, 8, 4)
    for y in range(EDGE - 3, EDGE):
        flow = high.finish(y, y % 2, flow)


def call(body, inputs, outputs, scratch, flops, moved, aliases=None, hbm=(), anywhere=False, limit=40 * 2**20):
    vmem, place, far = [pl.BlockSpec(memory_space=m) for m in (pltpu.VMEM, pl.ANY, pltpu.HBM)]
    kept = range(len(inputs)) if anywhere else ()
    return pl.pallas_call(
        body,
        out_shape=[jax.ShapeDtypeStruct(shape, F32) for shape in outputs],
        in_specs=[far if i in hbm else place if i in kept else vmem for i in range(len(inputs))],
        out_specs=[place if anywhere else vmem for _ in outputs],
        scratch_shapes=scratch,
        input_output_aliases=aliases or {},
        cost_estimate=pl.CostEstimate(flops=flops, bytes_accessed=moved, transcendentals=0),
        compiler_params=pltpu.CompilerParams(vmem_limit_bytes=limit),
    )(*inputs)


def per_device(old_fields, old_counts):
    groups, columns = lax.axis_size("grp"), lax.axis_size("dev")
    devices = groups * columns
    counts = jnp.pad(old_counts, (0, -devices % LANES)).reshape(-1, LANES)
    chain = [(i, i + 1) for i in range(devices - 1)]

    def ends(count):
        up = [(i, i + 1) for i in range(count - 1)]
        return up, [(j, i) for i, j in up]

    y_ways, x_ways = ends(columns), ends(groups)

    def read(body, outputs, after=None, limit=54400000):
        table = counts if after is None else lax.optimization_barrier((counts, after))[0]
        scratch = [
            VMEM(counts.shape, jnp.int32),
            VMEM((FIELDS, COLUMN, EDGE, EDGE * EDGE), F32),
            pltpu.SemaphoreType.DMA((FIELDS + 1,)),
        ]
        return call(body, (table, old_fields), outputs, scratch, 10**6, 2 * 10**6, hbm=(0, 1), limit=limit)

    strip, message = (EDGE, 8, LANES), (YMSG, LANES)
    deep, block = (DEEP, ROWS, LANES), (EDGE, EDGE, LANES)
    (shell,) = read(pack_shell, [(KINDS, GROUPS, 8, LANES)])
    rim, core = read(pack_rest, [(KINDS, RIM, 8, LANES), (KINDS, CORE, 8, LANES)], shell)
    shell = lax.ppermute(shell, ("grp", "dev"), chain)
    rim = lax.ppermute(rim, ("grp", "dev"), chain)
    core = lax.ppermute(core, ("grp", "dev"), chain)
    edges, slabs = read(relayout_edges, [(FIELDS, EDGE, 8, LANES), (FIELDS, 2, 4, EDGE, LANES)])
    x_up, x_down = call(make_faces, (counts, shell, edges), [strip, strip], [], 10**6, 10**6)
    x_before = lax.ppermute(x_up, "grp", x_ways[0])
    x_after = lax.ppermute(x_down, "grp", x_ways[1])
    table = lax.optimization_barrier((counts, x_up))[0]
    y_up, y_down = call(make_slabs, (table, shell, rim, slabs), [message, message], [], 10**6, 10**6)
    y_up, y_down = call(
        add_corners,
        (x_before, x_after, y_up, y_down),
        [message, message],
        [pltpu.SemaphoreType.DMA((2, 2, 2))],
        10**4,
        10**5,
        aliases={2: 0, 3: 1},
        anywhere=True,
    )
    y_before = lax.ppermute(y_up, "dev", y_ways[0])
    y_after = lax.ppermute(y_down, "dev", y_ways[1])
    (own,) = read(relayout, [(FIELDS, EDGE, EDGE, LANES)], y_up, 40 * 2**20)
    half, mix, rhs = call(assemble, (counts, own, shell, rim, core), [block] * 3, [], 10**6, 10**6)
    flat = (EDGE * EDGE, LANES)
    part_p, part_r, *kept = call(
        sweep_inner,
        (half, mix, rhs, x_before, x_after),
        [flat, flat] + [deep] * len(KEPT),
        [],
        10**8,
        5 * 10**6,
    )
    outs = call(
        sweep_outer,
        (y_before, y_after, x_before, x_after, part_p, part_r, *kept),
        [flat, flat],
        [VMEM((2, 10, ROWS, LANES), F32)] * len(KEPT),
        10**7,
        10**6,
    )
    return tuple(out.reshape(EDGE, EDGE, LANES) for out in outs)


def solution(mesh):
    placed = (P(None, ("grp", "dev"), None, None), P())
    return jax.shard_map(
        per_device,
        mesh=mesh,
        in_specs=placed,
        out_specs=(P("grp", "dev", None), P("grp", "dev", None)),
        check_vma=False,
    )
```

time: 56.5 us -> 48 us (0.85)
  the two profiles are of different devices: /device:TPU:223 before, /device:TPU:193 now
where the time goes in v4:
time: 48 us; the launch traced here: 47.6 us
  starting transfers between devices  22.6 us (47%)
  Pallas kernels  13.2 us (28%)
  waiting for transfers between devices  10.3 us (21%)
  between operations  0.82 us (2%)
  local copies, waits for them, and re-layouts  0.69 us (1%)
    pallas_call x10, Pallas kernels, call(): pl.pallas_call(body, out_shape=[jax.ShapeDtypeStruct(shape, F32) for shap...  13.2 us
    ppermute x1, waiting for transfers between devices, per_device(): rim = lax.ppermute(rim, ('grp', 'dev'), chain)  8.55 us
    ppermute x1, starting transfers between devices, per_device(): x_before = lax.ppermute(x_up, 'grp', x_ways[0])  5.44 us
    ppermute x1, starting transfers between devices, per_device(): y_before = lax.ppermute(y_up, 'dev', y_ways[0])  3.99 us
    ppermute x1, starting transfers between devices, per_device(): x_after = lax.ppermute(x_down, 'grp', x_ways[1])  3.45 us
    ppermute x1, starting transfers between devices, per_device(): core = lax.ppermute(core, ('grp', 'dev'), chain)  3.38 us
    ppermute x1, starting transfers between devices, per_device(): shell = lax.ppermute(shell, ('grp', 'dev'), chain)  3.12 us
    ppermute x1, starting transfers between devices, per_device(): rim = lax.ppermute(rim, ('grp', 'dev'), chain)  1.92 us
  transfers between devices with their start and end apart: 7, of which 2 were waited for; matrix products, arithmetic and copies ran while one was open for 0% of the time, Pallas kernels for 21%

profile of v4, /device:TPU:193, one launch (start us, length us, event | category | flops | bytes accessed | tf_op | source)
XLA Modules:
  0.0 47.6 jit_solution(12204989832473986637)
XLA Ops:
  0.6 0.0 copy-start.1
  0.6 0.7 %copy-done.1 = s32[512]{0:T(512)S(1)} copy-done((s32[512]{0:T(512)S(1)}, s32[512]{0:T(512)}, u32[]{:S(2)}) %copy-start.1) | copy-done | bytes 2072
  1.3 1.5 %shard_map.41 = f32[5,8,8,128]{3,2,1,0:T(8,128)S(1)} custom-call(s32[4,128]{1,0:T(4,128)S(1)} %bitcast.3, f32[3,8,32,1024]{3,2,1,0:T(8,128)} %old_ref.7), custom_call_target="tpu_custom_call" | custom-call | flops 1000000 | bytes 2000000 | tf_op jit(solution)/shard_map/pallas_call | solution.py:456
  2.8 0.0 copy-start.2
  2.8 3.1 %collective-permute-start = (f32[5,8,8,128]{3,2,1,0:T(8,128)S(1)}, f32[5,8,8,128]{3,2,1,0:T(8,128)S(1)}, u32[]{:S(2)}, u32[]{:S(2)}) collective-permute-start(f32[5,8,8,128]{3,2,1,0:T(8,128)S(1)} %shard_map.41), channel_id=1, source_target_pairs={{0,1},{1,2},{2,3},{3,4},{4,5},{5,6},{6,7},{7,8},{8,9},{9,10},{10,1... | collective-permute-start | bytes 491528 | tf_op jit(solution)/shard_map/ppermute | solution.py:493
  5.9 1.5 %shard_map.44 = (f32[5,6,8,128]{3,2,1,0:T(8,128)S(1)}, f32[5,18,8,128]{3,2,1,0:T(8,128)S(1)}) custom-call(s32[4,128]{1,0:T(4,128)S(1)} %bitcast.4, f32[3,8,32,1024]{3,2,1,0:T(8,128)} %old_ref.7), custom_call_target="tpu_custom_call" | custom-call | flops 1000000 | bytes 2000000 | tf_op jit(solution)/shard_map/pallas_call | solution.py:456
  7.5 0.0 copy-start
  7.5 3.4 %collective-permute-start.6 = (f32[5,18,8,128]{3,2,1,0:T(8,128)S(1)}, f32[5,18,8,128]{3,2,1,0:T(8,128)S(1)}, u32[]{:S(2)}, u32[]{:S(2)}) collective-permute-start(f32[5,18,8,128]{3,2,1,0:T(8,128)S(1)} %get-tuple-element.44), channel_id=1, source_target_pairs={{0,1},{1,2},{2,3},{3,4},{4,5},{5,6},{6,7},{7,8},{8,9},{9,10},{10,1... | collective-permute-start | bytes 1105928 | tf_op jit(solution)/shard_map/ppermute | solution.py:495
  10.9 1.9 %shard_map.42 = (f32[3,32,8,128]{3,2,1,0:T(8,128)S(1)}, f32[3,2,4,32,128]{4,3,2,1,0:T(8,128)S(1)}) custom-call(s32[4,128]{1,0:T(4,128)S(1)} %bitcast.5, f32[3,8,32,1024]{3,2,1,0:T(8,128)} %old_ref.7), custom_call_target="tpu_custom_call" | custom-call | flops 1000000 | bytes 2000000 | tf_op jit(solution)/shard_map/pallas_call | solution.py:456
  12.8 1.8 %collective-permute-done.shell = f32[5,8,8,128]{3,2,1,0:T(8,128)S(1)} collective-permute-done((f32[5,8,8,128]{3,2,1,0:T(8,128)S(1)}, f32[5,8,8,128]{3,2,1,0:T(8,128)S(1)}, u32[]{:S(2)}, u32[]{:S(2)}) %collective-permute-start) | collective-permute-done | bytes 163872 | tf_op jit(solution)/shard_map/ppermute | solution.py:493
  14.6 0.2 shard_map.43
  14.8 3.4 %collective-permute-start.2 = (f32[32,8,128]{2,1,0:T(8,128)S(1)}, f32[32,8,128]{2,1,0:T(8,128)S(1)}, u32[]{:S(2)}, u32[]{:S(2)}) collective-permute-start(f32[32,8,128]{2,1,0:T(8,128)S(1)} %get-tuple-element.34), channel_id=1, source_target_pairs={{32,0},{64,32},{96,64},{128,96},{160,128},{192,160},{224,192},{256... | collective-permute-start | bytes 393224 | tf_op jit(solution)/shard_map/ppermute | solution.py:499
  18.2 5.4 %collective-permute-start.1 = (f32[32,8,128]{2,1,0:T(8,128)S(1)}, f32[32,8,128]{2,1,0:T(8,128)S(1)}, u32[]{:S(2)}, u32[]{:S(2)}) collective-permute-start(f32[32,8,128]{2,1,0:T(8,128)S(1)} %get-tuple-element.33), channel_id=1, source_target_pairs={{0,32},{32,64},{64,96},{96,128},{128,160},{160,192},{192,224},{224... | collective-permute-start | bytes 393224 | tf_op jit(solution)/shard_map/ppermute | solution.py:498
  23.7 1.9 %collective-permute-start.3 = (f32[5,6,8,128]{3,2,1,0:T(8,128)S(1)}, f32[5,6,8,128]{3,2,1,0:T(8,128)S(1)}, u32[]{:S(2)}, u32[]{:S(2)}) collective-permute-start(f32[5,6,8,128]{3,2,1,0:T(8,128)S(1)} %get-tuple-element.37), channel_id=1, source_target_pairs={{0,1},{1,2},{2,3},{3,4},{4,5},{5,6},{6,7},{7,8},{8,9},{9,10},{10,1... | collective-permute-start | bytes 368648 | tf_op jit(solution)/shard_map/ppermute | solution.py:494
  25.6 8.5 %collective-permute-done.3.rim = f32[5,6,8,128]{3,2,1,0:T(8,128)S(1)} collective-permute-done((f32[5,6,8,128]{3,2,1,0:T(8,128)S(1)}, f32[5,6,8,128]{3,2,1,0:T(8,128)S(1)}, u32[]{:S(2)}, u32[]{:S(2)}) %collective-permute-start.3) | collective-permute-done | bytes 122912 | tf_op jit(solution)/shard_map/ppermute | solution.py:494
  34.2 0.2 shard_map.45
  34.3 0.1 shard_map.46
  34.5 1.3 %collective-permute-start.5 = (f32[288,128]{1,0:T(8,128)S(1)}, f32[288,128]{1,0:T(8,128)S(1)}, u32[]{:S(2)}, u32[]{:S(2)}) collective-permute-start(f32[288,128]{1,0:T(8,128)S(1)} %get-tuple-element.42), channel_id=1, source_target_pairs={{1,0},{2,1},{3,2},{4,3},{5,4},{6,5},{7,6},{8,7},{9,8},{10,9},{11,1... | collective-permute-start | bytes 442376 | tf_op jit(solution)/shard_map/ppermute | solution.py:513
  35.8 4.0 %collective-permute-start.4 = (f32[288,128]{1,0:T(8,128)S(1)}, f32[288,128]{1,0:T(8,128)S(1)}, u32[]{:S(2)}, u32[]{:S(2)}) collective-permute-start(f32[288,128]{1,0:T(8,128)S(1)} %get-tuple-element.41), channel_id=1, source_target_pairs={{0,1},{1,2},{2,3},{3,4},{4,5},{5,6},{6,7},{7,8},{8,9},{9,10},{10,1... | collective-permute-start | bytes 442376 | tf_op jit(solution)/shard_map/ppermute | solution.py:512
  39.8 2.3 %shard_map.47.own = f32[3,32,32,128]{3,2,1,0:T(8,128)S(1)} custom-call(s32[4,128]{1,0:T(4,128)S(1)} %bitcast.8, f32[3,8,32,1024]{3,2,1,0:T(8,128)S(1)} %copy-done), custom_call_target="tpu_custom_call" | custom-call | flops 1000000 | bytes 2000000 | tf_op jit(solution)/shard_map/pallas_call | solution.py:456
  42.1 0.0 collective-permute-done.6.core
  42.1 0.4 shard_map.48
  42.6 3.5 %shard_map.49 = (f32[1024,128]{1,0:T(8,128)S(1)}, f32[1024,128]{1,0:T(8,128)S(1)}, f32[40,48,128]{2,1,0:T(8,128)S(1)}, f32[40,48,128]{2,1,0:T(8,128)S(1)}, f32[4...) custom-call(f32[32,32,128]{2,1,0:T(8,128)S(1)} %get-tuple-element.45, ...), custom_call_target="tpu_custom_call" | custom-call | flops 100000000 | bytes 5000000 | tf_op jit(solution)/shard_map/pallas_call | solution.py:456
  46.1 1.5 %shard_map.50 = (f32[1024,128]{1,0:T(8,128)}, f32[1024,128]{1,0:T(8,128)}) custom-call(f32[288,128]{1,0:T(8,128)S(1)} %collective-permute-done.4.y_before, f32[288,128]{1,0:T(8,128)S(1)} %collective-permute-done.5.y_after, f32[32,8,128]{2,1,0:T(8,128)S(1)} %collective-permute-done.1.before.x_before, f32[32,8,128]{2,1,0:T(8,128)S(1)} %collective-permute-done.2.after.x_after, ...), custom_call_target="tpu_custom_call" | custom-call | flops 10000000 | bytes 1000000 | tf_op jit(solution)/shard_map/pallas_call | solution.py:456
  (6 shorter events, 0.0 us)
Async XLA Ops:
  0.6 0.7 %copy-start.1 = (s32[512]{0:T(512)S(1)}, s32[512]{0:T(512)}, u32[]{:S(2)}) copy-start(s32[512]{0:T(512)} %param.3) | copy-start | bytes 6148
  2.8 31.3 %copy-start.2 = (s32[512]{0:T(512)S(1)}, s32[512]{0:T(512)}, u32[]{:S(2)}) copy-start(s32[512]{0:T(512)} %param.3) | copy-start | bytes 6148
  2.8 11.7 %collective-permute-start = (f32[5,8,8,128]{3,2,1,0:T(8,128)S(1)}, f32[5,8,8,128]{3,2,1,0:T(8,128)S(1)}, u32[]{:S(2)}, u32[]{:S(2)}) collective-permute-start(f32[5,8,8,128]{3,2,1,0:T(8,128)S(1)} %shard_map.41), channel_id=1, source_target_pairs={{0,1},{1,2},{2,3},{3,4},{4,5},{5,6},{6,7},{7,8},{8,9},{9,10},{10,1... | collective-permute-start | bytes 491528 | tf_op jit(solution)/shard_map/ppermute | solution.py:493
  7.5 32.3 %copy-start = (f32[3,8,32,1024]{3,2,1,0:T(8,128)S(1)}, f32[3,8,32,1024]{3,2,1,0:T(8,128)}, u32[]{:S(2)}) copy-start(f32[3,8,32,1024]{3,2,1,0:T(8,128)} %old_ref.7) | copy-start | bytes 9437188
  7.5 34.6 %collective-permute-start.6 = (f32[5,18,8,128]{3,2,1,0:T(8,128)S(1)}, f32[5,18,8,128]{3,2,1,0:T(8,128)S(1)}, u32[]{:S(2)}, u32[]{:S(2)}) collective-permute-start(f32[5,18,8,128]{3,2,1,0:T(8,128)S(1)} %get-tuple-element.44), channel_id=1, source_target_pairs={{0,1},{1,2},{2,3},{3,4},{4,5},{5,6},{6,7},{7,8},{8,9},{9,10},{10,1... | collective-permute-start | bytes 1105928 | tf_op jit(solution)/shard_map/ppermute | solution.py:495
  14.8 19.6 %collective-permute-start.2 = (f32[32,8,128]{2,1,0:T(8,128)S(1)}, f32[32,8,128]{2,1,0:T(8,128)S(1)}, u32[]{:S(2)}, u32[]{:S(2)}) collective-permute-start(f32[32,8,128]{2,1,0:T(8,128)S(1)} %get-tuple-element.34), channel_id=1, source_target_pairs={{32,0},{64,32},{96,64},{128,96},{160,128},{192,160},{224,192},{256... | collective-permute-start | bytes 393224 | tf_op jit(solution)/shard_map/ppermute | solution.py:499
  18.2 16.1 %collective-permute-start.1 = (f32[32,8,128]{2,1,0:T(8,128)S(1)}, f32[32,8,128]{2,1,0:T(8,128)S(1)}, u32[]{:S(2)}, u32[]{:S(2)}) collective-permute-start(f32[32,8,128]{2,1,0:T(8,128)S(1)} %get-tuple-element.33), channel_id=1, source_target_pairs={{0,32},{32,64},{64,96},{96,128},{128,160},{160,192},{192,224},{224... | collective-permute-start | bytes 393224 | tf_op jit(solution)/shard_map/ppermute | solution.py:498
  23.7 10.5 %collective-permute-start.3 = (f32[5,6,8,128]{3,2,1,0:T(8,128)S(1)}, f32[5,6,8,128]{3,2,1,0:T(8,128)S(1)}, u32[]{:S(2)}, u32[]{:S(2)}) collective-permute-start(f32[5,6,8,128]{3,2,1,0:T(8,128)S(1)} %get-tuple-element.37), channel_id=1, source_target_pairs={{0,1},{1,2},{2,3},{3,4},{4,5},{5,6},{6,7},{7,8},{8,9},{9,10},{10,1... | collective-permute-start | bytes 368648 | tf_op jit(solution)/shard_map/ppermute | solution.py:494
  34.5 11.6 %collective-permute-start.5 = (f32[288,128]{1,0:T(8,128)S(1)}, f32[288,128]{1,0:T(8,128)S(1)}, u32[]{:S(2)}, u32[]{:S(2)}) collective-permute-start(f32[288,128]{1,0:T(8,128)S(1)} %get-tuple-element.42), channel_id=1, source_target_pairs={{1,0},{2,1},{3,2},{4,3},{5,4},{6,5},{7,6},{8,7},{9,8},{10,9},{11,1... | collective-permute-start | bytes 442376 | tf_op jit(solution)/shard_map/ppermute | solution.py:513
  35.8 10.3 %collective-permute-start.4 = (f32[288,128]{1,0:T(8,128)S(1)}, f32[288,128]{1,0:T(8,128)S(1)}, u32[]{:S(2)}, u32[]{:S(2)}) collective-permute-start(f32[288,128]{1,0:T(8,128)S(1)} %get-tuple-element.41), channel_id=1, source_target_pairs={{0,1},{1,2},{2,3},{3,4},{4,5},{5,6},{6,7},{7,8},{8,9},{9,10},{10,1... | collective-permute-start | bytes 442376 | tf_op jit(solution)/shard_map/ppermute | solution.py:512

commit v5 on v4

--- a/solution.py
+++ b/solution.py
@@ -13,11 +13,12 @@
 FIELDS = 3
 MOVED = 2
 KINDS = 5
-RIM = 6
+SHELL = GROUPS + 6
 CORE = 3 * (GROUPS - 2)
 ROWS = EDGE + 16
 DEEP = EDGE + 8
-YMSG = 8 * EDGE + 32
+CORNERS = 6 * EDGE
+YMSG = CORNERS + 32
 F32 = jnp.float32
 VMEM = pltpu.VMEM
 
@@ -79,18 +80,18 @@
         copy.wait()
     for g in range(GROUPS):
         pack(boxes, moved, out, g, g, "edge")
-
-
-def pack_rest(counts_ref, old_ref, rim, core, counts, boxes, sems):
+    for side, g in enumerate((0, GROUPS - 1)):
+        for which in range(3):
+            pack(boxes, moved, out, GROUPS + 3 * side + which, g, which)
+
+
+def pack_core(counts_ref, old_ref, out, counts, boxes, sems):
     copies, moved = fetch(counts_ref, old_ref, counts, boxes, sems, MOVED)
     for copy in copies:
         copy.wait()
-    for g in range(GROUPS):
+    for g in range(1, GROUPS - 1):
         for which in range(3):
-            if g in (0, GROUPS - 1):
-                pack(boxes, moved, rim, (3 if g else 0) + which, g, which)
-            else:
-                pack(boxes, moved, core, 3 * (g - 1) + which, g, which)
+            pack(boxes, moved, out, 3 * (g - 1) + which, g, which)
 
 
 def interleave(v):
@@ -138,11 +139,11 @@
     return [a, pltpu.roll(b, LANES - EDGE, 1), pltpu.roll(a, 2 * EDGE, 1), pltpu.roll(b, EDGE, 1)]
 
 
-def wire_rows(shell, rim, core, k, g):
+def wire_rows(shell, core, k, g):
     low = iota((8, LANES), 0) < 4
     edge = shell[k, g]
     if g in (0, GROUPS - 1):
-        mid = [rim[k, (3 if g else 0) + which] for which in range(3)]
+        mid = [shell[k, GROUPS + (3 if g else 0) + which] for which in range(3)]
     else:
         mid = [core[k, 3 * (g - 1) + which] for which in range(3)]
     return jnp.concatenate([jnp.where(low, edge, mid[0]), mid[1], mid[2], jnp.where(low, mid[0], edge)], axis=0)
@@ -159,39 +160,59 @@
     return high, low
 
 
-def make_faces(counts_ref, shell, edges, x_up, x_down):
+def is_odd(axis):
+    return lax.axis_index(axis) % 2 == 1
+
+
+def make_faces(counts_ref, shell, edges, first, second):
     limit = moved_boxes(counts_ref) * EDGE
     taken = iota((8, LANES), 1) < limit
+    odd = is_odd("grp")
     for g in range(GROUPS):
         kinds = [shell[k, g] for k in range(KINDS)]
         rows = [unmix(kinds, f) for f in range(FIELDS)]
         for r in range(4):
             y = 4 * g + r
             edge = [jnp.where(taken, rows[f][r], edges[f, y]) for f in range(FIELDS)]
-            x_up[y], x_down[y] = pack_x(*edge)
-
-
-def make_slabs(counts_ref, shell, rim, slabs, y_up, y_down):
+            up, down = pack_x(*edge)
+            first[y] = jnp.where(odd, down, up)
+            second[y] = jnp.where(odd, up, down)
+
+
+def make_slabs(counts_ref, shell, slabs, first, second):
     taken = iota((EDGE, LANES), 1) < moved_boxes(counts_ref) * EDGE
+    blacks = [~is_red((EDGE, LANES), y) for y in range(2)]
+    sides = []
     for side, g in enumerate((0, GROUPS - 1)):
-        out = y_up if side else y_down
-        kinds = [wire_rows(shell, rim, None, k, g) for k in range(KINDS)]
-        for f, at, depth in ((2, 0, 3), (0, 3, 3), (1, 6, 2)):
-            rows = unmix(kinds, f)
-            for j in range(depth):
-                r = 4 - depth + j if side else j
-                slab = jnp.where(taken, rows[r], slabs[f, side, r])
-                out[EDGE * (at + j) : EDGE * (at + j + 1)] = 0.5 * slab if f == 2 else slab
-
-
-def add_corners(before, after, y_up_in, y_down_in, y_up, y_down, sems):
-    del y_up_in, y_down_in
+        kinds = [wire_rows(shell, None, k, g) for k in range(KINDS)]
+        p, f, b = [[jnp.where(taken, row, slabs[i, side, r]) for r, row in enumerate(unmix(kinds, i))] for i in range(FIELDS)]
+        near, next_, far = (3, 2, 1) if side else (0, 1, 2)
+        sides.append(
+            [
+                0.5 * b[near],
+                0.5 * b[next_],
+                jnp.where(blacks[far % 2], 0.5 * b[far], pltpu.roll(p[far], 1, 1)),
+                jnp.where(blacks[near % 2], p[near], p[next_]),
+                f[near],
+                f[next_],
+            ]
+        )
+    odd = is_odd("dev")
+    for i, (down, up) in enumerate(zip(*sides)):
+        first[EDGE * i : EDGE * (i + 1)] = jnp.where(odd, down, up)
+        second[EDGE * i : EDGE * (i + 1)] = jnp.where(odd, up, down)
+
+
+def add_corners(x_first, x_second, first_in, second_in, first, second, sems):
+    del first_in, second_in
+    odd = lax.axis_index("dev") % 2
     copies = []
-    for way, (out, first) in enumerate(((y_up, EDGE - 2), (y_down, 0))):
+    for way, out in enumerate((first, second)):
+        top = (EDGE - 2) * (odd if way else 1 - odd)
         for d in range(2):
-            for side, ref in enumerate((before, after)):
-                at = 8 * EDGE + 8 * (2 * d + side)
-                copies.append(pltpu.make_async_copy(ref.at[first + d], out.at[pl.ds(at, 8)], sems.at[way, d, side]))
+            for side, ref in enumerate((x_first, x_second)):
+                at = CORNERS + 8 * (2 * d + side)
+                copies.append(pltpu.make_async_copy(ref.at[top + d], out.at[pl.ds(at, 8)], sems.at[way, d, side]))
     for copy in copies:
         copy.start()
     for copy in copies:
@@ -202,13 +223,13 @@
     return (iota(shape, 0) + iota(shape, 1) + shift) & 1 == 0
 
 
-def assemble(counts_ref, own, shell, rim, core, half, mix, rhs):
+def assemble(counts_ref, own, shell, core, half, mix, rhs):
     limit = moved_boxes(counts_ref) * EDGE
     taken = iota((EDGE, LANES), 1) < limit
     reds = [is_red((EDGE, LANES), y) for y in range(2)]
     before = None
     for g in range(GROUPS):
-        kinds = [wire_rows(shell, rim, core, k, g) for k in range(KINDS)]
+        kinds = [wire_rows(shell, core, k, g) for k in range(KINDS)]
         parts = [unmix(kinds, f) for f in range(FIELDS)]
         for r in range(4):
             y = 4 * g + r
@@ -329,7 +350,12 @@
 INNER = pl.ds(8, EDGE)
 
 
-def sweep_inner(half_in, mix_in, rhs_in, x_before, x_after, *refs):
+def order(axis, first, second):
+    odd = is_odd(axis)
+    return jnp.where(odd, first, second), jnp.where(odd, second, first)
+
+
+def sweep_inner(half_in, mix_in, rhs_in, x_first, x_second, *refs):
     w = Sweep(4, *refs)
     w.mix[3, INNER] = half_in[0] * mix_in[0]
 
@@ -343,7 +369,7 @@
 
     def strips(k, odd, carry):
         y = EDGE - 1 - k
-        return w.strip(y, 1 - odd, (x_before[y], x_after[y]), carry)
+        return w.strip(y, 1 - odd, order("grp", x_first[y], x_second[y]), carry)
 
     last = fours(0, EDGE, strips, (w.nothing, w.nothing))
     w.mix[3, tile(0)], w.mix[3, tile(ROWS - 8)] = last
@@ -367,7 +393,7 @@
 )
 
 
-def sweep_outer(y_before, y_after, x_before, x_after, part_p, part_r, *refs):
+def sweep_outer(y_first, y_second, x_first, x_second, part_p, part_r, *refs):
     n = len(KEPT)
     old, (out_p, out_r), new = refs[:n], refs[n : n + 2], refs[n + 2 :]
     out_p[...] = part_p[...]
@@ -375,21 +401,23 @@
     dev = lax.axis_index("dev")
     red_rows = [is_red((EDGE, LANES), y) for y in range(2)]
     zero = jnp.zeros((EDGE, LANES), F32)
+
+    def message(side, row, rows):
+        return order("dev", y_first[row : row + rows], y_second[row : row + rows])[side]
+
     sides = [Sweep(shift, out_p, out_r, *[ref.at[i] for ref in new]) for i, shift in enumerate((4, -26))]
     for side, (w, spans) in enumerate(zip(sides, NEAR)):
         for name, ref, (first, end) in zip(KEPT, old, spans):
             for y in range(first, end):
                 getattr(w, name)[y + w.shift] = ref[y + 4]
-        source = y_after if side else y_before
-        pressures, flux = {}, {}
-        for k, y in enumerate(range(EDGE, EDGE + 3) if side else range(-3, 0)):
-            h, p = [source[EDGE * i : EDGE * (i + 1)] for i in (k, 3 + k)]
+        h1, h2, far, mixed, f1, f2 = [message(side, EDGE * i, EDGE) for i in range(6)]
+        place = (EDGE, EDGE + 1, EDGE + 2) if side else (-1, -2, -3)
+        for y, h in zip(place, (h1, h2, far)):
             w.half[y + w.shift, INNER] = h
-            pressures[y] = p
-            flux[y] = h * p
-            k = k if side else k - 1
-            if 0 <= k < 2:
-                w.rhs[y + w.shift, INNER] = source[EDGE * (6 + k) : EDGE * (7 + k)]
+        for y, f in zip(place, (f1, f2)):
+            w.rhs[y + w.shift, INNER] = f
+        pressures = dict(zip(place, (mixed, mixed, pltpu.roll(far, LANES - 1, 1))))
+        flux = {y: h * pressures[y] for y, h in zip(place, (h1, h2, far))}
         edge = (EDGE - 1 if side else 0) + w.shift
         if side:
             pressures[EDGE - 1] = w.mix[edge, INNER]
@@ -398,18 +426,18 @@
         for y in range(EDGE - 1, EDGE + 3) if side else range(-4, 0):
             w.mix[y + w.shift, INNER] = jnp.where(red_rows[y % 2], flux.get(y + 1, zero), pressures.get(y, zero))
 
-    def corners(ref, d):
-        return [ref[pl.ds(8 * EDGE + 8 * (2 * d + side), 8)] for side in range(2)]
+    def corners(side, d):
+        return order("grp", *[message(side, CORNERS + 8 * (2 * d + i), 8) for i in range(2)])
 
     low, high = sides
     last = (low.nothing, low.nothing)
     for d in (1, 0):
-        last = high.strip(EDGE + d, d, corners(y_after, d), last)
-    high.strip(EDGE - 1, 1, (x_before[EDGE - 1], x_after[EDGE - 1]), last)
-    v = (x_before[0], x_after[0])
+        last = high.strip(EDGE + d, d, corners(1, d), last)
+    high.strip(EDGE - 1, 1, order("grp", x_first[EDGE - 1], x_second[EDGE - 1]), last)
+    v = order("grp", x_first[0], x_second[0])
     last = tuple(0.5 * a * pltpu.roll(a, turn, 0) for a, turn in zip(v, (3, 5)))
     for d in (1, 0):
-        last = low.strip(d - 2, d, corners(y_before, d), last)
+        last = low.strip(d - 2, d, corners(0, d), last)
     low.mix[1, tile(0)], low.mix[1, tile(ROWS - 8)] = last
 
     low_shut = (dev == 0).astype(jnp.int32)
@@ -471,11 +499,14 @@
     counts = jnp.pad(old_counts, (0, -devices % LANES)).reshape(-1, LANES)
     chain = [(i, i + 1) for i in range(devices - 1)]
 
-    def ends(count):
-        up = [(i, i + 1) for i in range(count - 1)]
-        return up, [(j, i) for i, j in up]
-
-    y_ways, x_ways = ends(columns), ends(groups)
+    def swaps(count):
+        ways = []
+        for first in range(2):
+            pairs = [(i, i + 1) for i in range(first, count - 1, 2)]
+            ways.append(pairs + [(j, i) for i, j in pairs])
+        return ways
+
+    y_ways, x_ways = swaps(columns), swaps(groups)
 
     def read(body, outputs, after=None, limit=54400000):
         table = counts if after is None else lax.optimization_barrier((counts, after))[0]
@@ -488,20 +519,19 @@
 
     strip, message = (EDGE, 8, LANES), (YMSG, LANES)
     deep, block = (DEEP, ROWS, LANES), (EDGE, EDGE, LANES)
-    (shell,) = read(pack_shell, [(KINDS, GROUPS, 8, LANES)])
-    rim, core = read(pack_rest, [(KINDS, RIM, 8, LANES), (KINDS, CORE, 8, LANES)], shell)
+    (shell,) = read(pack_shell, [(KINDS, SHELL, 8, LANES)])
+    (core,) = read(pack_core, [(KINDS, CORE, 8, LANES)], shell)
     shell = lax.ppermute(shell, ("grp", "dev"), chain)
-    rim = lax.ppermute(rim, ("grp", "dev"), chain)
     core = lax.ppermute(core, ("grp", "dev"), chain)
     edges, slabs = read(relayout_edges, [(FIELDS, EDGE, 8, LANES), (FIELDS, 2, 4, EDGE, LANES)])
-    x_up, x_down = call(make_faces, (counts, shell, edges), [strip, strip], [], 10**6, 10**6)
-    x_before = lax.ppermute(x_up, "grp", x_ways[0])
-    x_after = lax.ppermute(x_down, "grp", x_ways[1])
-    table = lax.optimization_barrier((counts, x_up))[0]
-    y_up, y_down = call(make_slabs, (table, shell, rim, slabs), [message, message], [], 10**6, 10**6)
-    y_up, y_down = call(
+    x_first, x_second = call(make_faces, (counts, shell, edges), [strip, strip], [], 10**6, 10**6)
+    table = lax.optimization_barrier((counts, x_first))[0]
+    x_first = lax.ppermute(x_first, "grp", x_ways[0])
+    x_second = lax.ppermute(x_second, "grp", x_ways[1])
+    y_first, y_second = call(make_slabs, (table, shell, slabs), [message, message], [], 10**6, 10**6)
+    y_first, y_second = call(
         add_corners,
-        (x_before, x_after, y_up, y_down),
+        (x_first, x_second, y_first, y_second),
         [message, message],
         [pltpu.SemaphoreType.DMA((2, 2, 2))],
         10**4,
@@ -509,14 +539,15 @@
         aliases={2: 0, 3: 1},
         anywhere=True,
     )
-    y_before = lax.ppermute(y_up, "dev", y_ways[0])
-    y_after = lax.ppermute(y_down, "dev", y_ways[1])
-    (own,) = read(relayout, [(FIELDS, EDGE, EDGE, LANES)], y_up, 40 * 2**20)
-    half, mix, rhs = call(assemble, (counts, own, shell, rim, core), [block] * 3, [], 10**6, 10**6)
+    after = y_first
+    y_first = lax.ppermute(y_first, "dev", y_ways[0])
+    y_second = lax.ppermute(y_second, "dev", y_ways[1])
+    (own,) = read(relayout, [(FIELDS, EDGE, EDGE, LANES)], after, 40 * 2**20)
+    half, mix, rhs = call(assemble, (counts, own, shell, core), [block] * 3, [], 10**6, 10**6)
     flat = (EDGE * EDGE, LANES)
     part_p, part_r, *kept = call(
         sweep_inner,
-        (half, mix, rhs, x_before, x_after),
+        (half, mix, rhs, x_first, x_second),
         [flat, flat] + [deep] * len(KEPT),
         [],
         10**8,
@@ -524,7 +555,7 @@
     )
     outs = call(
         sweep_outer,
-        (y_before, y_after, x_before, x_after, part_p, part_r, *kept),
+        (y_first, y_second, x_first, x_second, part_p, part_r, *kept),
         [flat, flat],
         [VMEM((2, 10, ROWS, LANES), F32)] * len(KEPT),
         10**7,

time: 48 us -> 42.5 us (0.89)
  the two profiles are of different devices: /device:TPU:193 before, /device:TPU:220 now
where the time goes in v5:
time: 42.5 us; the launch traced here: 42.2 us
  starting transfers between devices  26.5 us (62%)
  Pallas kernels  13.3 us (31%)
  waiting for transfers between devices  0.87 us (2%)
  between operations  0.8 us (2%)
  local copies, waits for them, and re-layouts  0.69 us (2%)
    pallas_call x10, Pallas kernels, call(): pl.pallas_call(body, out_shape=[jax.ShapeDtypeStruct(shape, F32) for shap...  13.3 us
    ppermute x1, starting transfers between devices, per_device(): y_first = lax.ppermute(y_first, 'dev', y_ways[0])  8.59 us
    ppermute x1, starting transfers between devices, per_device(): x_first = lax.ppermute(x_first, 'grp', x_ways[0])  5.59 us
    ppermute x1, starting transfers between devices, per_device(): core = lax.ppermute(core, ('grp', 'dev'), chain)  4.87 us
    ppermute x1, starting transfers between devices, per_device(): shell = lax.ppermute(shell, ('grp', 'dev'), chain)  3.11 us
    ppermute x1, starting transfers between devices, per_device(): y_second = lax.ppermute(y_second, 'dev', y_ways[1])  2.44 us
    ppermute x1, starting transfers between devices, per_device(): x_second = lax.ppermute(x_second, 'grp', x_ways[1])  1.92 us
  transfers between devices with their start and end apart: 6, of which 2 were waited for; matrix products, arithmetic and copies ran while one was open for 0% of the time, Pallas kernels for 24%

profile of v5, /device:TPU:220, one launch (start us, length us, event | category | flops | bytes accessed | tf_op | source)
XLA Modules:
  0.0 42.2 jit_solution(16493052534308789758)
XLA Ops:
  0.6 0.0 copy-start.1
  0.6 0.7 %copy-done.1 = s32[512]{0:T(512)S(1)} copy-done((s32[512]{0:T(512)S(1)}, s32[512]{0:T(512)}, u32[]{:S(2)}) %copy-start.1) | copy-done | bytes 2072
  1.3 1.5 %shard_map.41 = f32[5,14,8,128]{3,2,1,0:T(8,128)S(1)} custom-call(s32[4,128]{1,0:T(4,128)S(1)} %bitcast.3, f32[3,8,32,1024]{3,2,1,0:T(8,128)} %old_ref.7), custom_call_target="tpu_custom_call" | custom-call | flops 1000000 | bytes 2000000 | tf_op jit(solution)/shard_map/pallas_call | solution.py:484
  2.8 0.0 copy-start.2
  2.8 3.1 %collective-permute-start = (f32[5,14,8,128]{3,2,1,0:T(8,128)S(1)}, f32[5,14,8,128]{3,2,1,0:T(8,128)S(1)}, u32[]{:S(2)}, u32[]{:S(2)}) collective-permute-start(f32[5,14,8,128]{3,2,1,0:T(8,128)S(1)} %shard_map.41), channel_id=1, source_target_pairs={{0,1},{1,2},{2,3},{3,4},{4,5},{5,6},{6,7},{7,8},{8,9},{9,10},{10,1... | collective-permute-start | bytes 860168 | tf_op jit(solution)/shard_map/ppermute | solution.py:524
  6.0 1.5 %shard_map.47 = f32[5,18,8,128]{3,2,1,0:T(8,128)S(1)} custom-call(s32[4,128]{1,0:T(4,128)S(1)} %bitcast.4, f32[3,8,32,1024]{3,2,1,0:T(8,128)} %old_ref.7), custom_call_target="tpu_custom_call" | custom-call | flops 1000000 | bytes 2000000 | tf_op jit(solution)/shard_map/pallas_call | solution.py:484
  7.5 0.0 copy-start
  7.5 4.9 %collective-permute-start.5 = (f32[5,18,8,128]{3,2,1,0:T(8,128)S(1)}, f32[5,18,8,128]{3,2,1,0:T(8,128)S(1)}, u32[]{:S(2)}, u32[]{:S(2)}) collective-permute-start(f32[5,18,8,128]{3,2,1,0:T(8,128)S(1)} %shard_map.47), channel_id=1, source_target_pairs={{0,1},{1,2},{2,3},{3,4},{4,5},{5,6},{6,7},{7,8},{8,9},{9,10},{10,1... | collective-permute-start | bytes 1105928 | tf_op jit(solution)/shard_map/ppermute | solution.py:525
  12.4 1.9 %shard_map.42 = (f32[3,32,8,128]{3,2,1,0:T(8,128)S(1)}, f32[3,2,4,32,128]{4,3,2,1,0:T(8,128)S(1)}) custom-call(s32[4,128]{1,0:T(4,128)S(1)} %bitcast.5, f32[3,8,32,1024]{3,2,1,0:T(8,128)} %old_ref.7), custom_call_target="tpu_custom_call" | custom-call | flops 1000000 | bytes 2000000 | tf_op jit(solution)/shard_map/pallas_call | solution.py:484
  14.3 0.1 collective-permute-done.shell
  14.4 0.2 shard_map.43
  14.6 1.9 %collective-permute-start.2 = (f32[32,8,128]{2,1,0:T(8,128)S(1)}, f32[32,8,128]{2,1,0:T(8,128)S(1)}, u32[]{:S(2)}, u32[]{:S(2)}) collective-permute-start(f32[32,8,128]{2,1,0:T(8,128)S(1)} %get-tuple-element.32), channel_id=1, source_target_pairs={{32,64},{96,128},{160,192},{224,256},{288,320},{352,384},{416,448}... | collective-permute-start | bytes 393224 | tf_op jit(solution)/shard_map/ppermute | solution.py:530
  16.6 5.6 %collective-permute-start.1 = (f32[32,8,128]{2,1,0:T(8,128)S(1)}, f32[32,8,128]{2,1,0:T(8,128)S(1)}, u32[]{:S(2)}, u32[]{:S(2)}) collective-permute-start(f32[32,8,128]{2,1,0:T(8,128)S(1)} %get-tuple-element.31), channel_id=1, source_target_pairs={{0,32},{64,96},{128,160},{192,224},{256,288},{320,352},{384,416},{... | collective-permute-start | bytes 393224 | tf_op jit(solution)/shard_map/ppermute | solution.py:529
  22.2 0.2 shard_map.44
  22.4 0.0 collective-permute-done.2.x_second
  22.4 0.7 %collective-permute-done.1.x_first = f32[32,8,128]{2,1,0:T(8,128)S(1)} collective-permute-done((f32[32,8,128]{2,1,0:T(8,128)S(1)}, f32[32,8,128]{2,1,0:T(8,128)S(1)}, u32[]{:S(2)}, u32[]{:S(2)}) %collective-permute-start.1) | collective-permute-done | bytes 131104 | tf_op jit(solution)/shard_map/ppermute | solution.py:529
  23.1 0.1 shard_map.45
  23.3 2.4 %collective-permute-start.4 = (f32[224,128]{1,0:T(8,128)S(1)}, f32[224,128]{1,0:T(8,128)S(1)}, u32[]{:S(2)}, u32[]{:S(2)}) collective-permute-start(f32[224,128]{1,0:T(8,128)S(1)} %get-tuple-element.38), channel_id=1, source_target_pairs={{1,2},{3,4},{5,6},{7,8},{9,10},{11,12},{13,14},{15,16},{17,18},{19... | collective-permute-start | bytes 344072 | tf_op jit(solution)/shard_map/ppermute | solution.py:544
  25.7 8.6 %collective-permute-start.3 = (f32[224,128]{1,0:T(8,128)S(1)}, f32[224,128]{1,0:T(8,128)S(1)}, u32[]{:S(2)}, u32[]{:S(2)}) collective-permute-start(f32[224,128]{1,0:T(8,128)S(1)} %get-tuple-element.37), channel_id=1, source_target_pairs={{0,1},{2,3},{4,5},{6,7},{8,9},{10,11},{12,13},{14,15},{16,17},{18,... | collective-permute-start | bytes 344072 | tf_op jit(solution)/shard_map/ppermute | solution.py:543
  34.3 2.3 %shard_map.46.own = f32[3,32,32,128]{3,2,1,0:T(8,128)S(1)} custom-call(s32[4,128]{1,0:T(4,128)S(1)} %bitcast.8, f32[3,8,32,1024]{3,2,1,0:T(8,128)S(1)} %copy-done), custom_call_target="tpu_custom_call" | custom-call | flops 1000000 | bytes 2000000 | tf_op jit(solution)/shard_map/pallas_call | solution.py:484
  36.7 0.4 %shard_map.48 = (f32[32,32,128]{2,1,0:T(8,128)S(1)}, f32[32,32,128]{2,1,0:T(8,128)S(1)}, f32[32,32,128]{2,1,0:T(8,128)S(1)}) custom-call(s32[4,128]{1,0:T(4,128)S(1)} %bitcast.9, f32[3,32,32,128]{3,2,1,0:T(8,128)S(1)} %shard_map.46.own, f32[5,14,8,128]{3,2,1,0:T(8,128)S(1)} %collective-permute-done.shell, f32[5,18,8,128]{3,2,1,0:T(8,128)S(1)} %collective-permute-done.5.core), custom_call_target="tpu_custom_call" | custom-call | flops 1000000 | bytes 1000000 | tf_op jit(solution)/shard_map/pallas_call | solution.py:484
  37.1 3.6 %shard_map.49 = (f32[1024,128]{1,0:T(8,128)S(1)}, f32[1024,128]{1,0:T(8,128)S(1)}, f32[40,48,128]{2,1,0:T(8,128)S(1)}, f32[40,48,128]{2,1,0:T(8,128)S(1)}, f32[4...) custom-call(f32[32,32,128]{2,1,0:T(8,128)S(1)} %get-tuple-element.41, ...), custom_call_target="tpu_custom_call" | custom-call | flops 100000000 | bytes 5000000 | tf_op jit(solution)/shard_map/pallas_call | solution.py:484
  40.7 0.0 collective-permute-done.4.y_second
  40.7 1.5 %shard_map.50 = (f32[1024,128]{1,0:T(8,128)}, f32[1024,128]{1,0:T(8,128)}) custom-call(f32[224,128]{1,0:T(8,128)S(1)} %collective-permute-done.3.y_first, f32[224,128]{1,0:T(8,128)S(1)} %collective-permute-done.4.y_second, f32[32,8,128]{2,1,0:T(8,128)S(1)} %collective-permute-done.1.x_first, f32[32,8,128]{2,1,0:T(8,128)S(1)} %collective-permute-done.2.x_second, ...), custom_call_target="tpu_custom_call" | custom-call | flops 10000000 | bytes 1000000 | tf_op jit(solution)/shard_map/pallas_call | solution.py:484
  (4 shorter events, 0.0 us)
Async XLA Ops:
  0.6 0.7 %copy-start.1 = (s32[512]{0:T(512)S(1)}, s32[512]{0:T(512)}, u32[]{:S(2)}) copy-start(s32[512]{0:T(512)} %param.3) | copy-start | bytes 6148
  2.8 19.3 %copy-start.2 = (s32[512]{0:T(512)S(1)}, s32[512]{0:T(512)}, u32[]{:S(2)}) copy-start(s32[512]{0:T(512)} %param.3) | copy-start | bytes 6148
  2.8 11.6 %collective-permute-start = (f32[5,14,8,128]{3,2,1,0:T(8,128)S(1)}, f32[5,14,8,128]{3,2,1,0:T(8,128)S(1)}, u32[]{:S(2)}, u32[]{:S(2)}) collective-permute-start(f32[5,14,8,128]{3,2,1,0:T(8,128)S(1)} %shard_map.41), channel_id=1, source_target_pairs={{0,1},{1,2},{2,3},{3,4},{4,5},{5,6},{6,7},{7,8},{8,9},{9,10},{10,1... | collective-permute-start | bytes 860168 | tf_op jit(solution)/shard_map/ppermute | solution.py:524
  7.5 26.8 %copy-start = (f32[3,8,32,1024]{3,2,1,0:T(8,128)S(1)}, f32[3,8,32,1024]{3,2,1,0:T(8,128)}, u32[]{:S(2)}) copy-start(f32[3,8,32,1024]{3,2,1,0:T(8,128)} %old_ref.7) | copy-start | bytes 9437188
  7.5 29.1 %collective-permute-start.5 = (f32[5,18,8,128]{3,2,1,0:T(8,128)S(1)}, f32[5,18,8,128]{3,2,1,0:T(8,128)S(1)}, u32[]{:S(2)}, u32[]{:S(2)}) collective-permute-start(f32[5,18,8,128]{3,2,1,0:T(8,128)S(1)} %shard_map.47), channel_id=1, source_target_pairs={{0,1},{1,2},{2,3},{3,4},{4,5},{5,6},{6,7},{7,8},{8,9},{9,10},{10,1... | collective-permute-start | bytes 1105928 | tf_op jit(solution)/shard_map/ppermute | solution.py:525
  14.6 7.8 %collective-permute-start.2 = (f32[32,8,128]{2,1,0:T(8,128)S(1)}, f32[32,8,128]{2,1,0:T(8,128)S(1)}, u32[]{:S(2)}, u32[]{:S(2)}) collective-permute-start(f32[32,8,128]{2,1,0:T(8,128)S(1)} %get-tuple-element.32), channel_id=1, source_target_pairs={{32,64},{96,128},{160,192},{224,256},{288,320},{352,384},{416,448}... | collective-permute-start | bytes 393224 | tf_op jit(solution)/shard_map/ppermute | solution.py:530
  16.6 6.6 %collective-permute-start.1 = (f32[32,8,128]{2,1,0:T(8,128)S(1)}, f32[32,8,128]{2,1,0:T(8,128)S(1)}, u32[]{:S(2)}, u32[]{:S(2)}) collective-permute-start(f32[32,8,128]{2,1,0:T(8,128)S(1)} %get-tuple-element.31), channel_id=1, source_target_pairs={{0,32},{64,96},{128,160},{192,224},{256,288},{320,352},{384,416},{... | collective-permute-start | bytes 393224 | tf_op jit(solution)/shard_map/ppermute | solution.py:529
  23.3 17.4 %collective-permute-start.4 = (f32[224,128]{1,0:T(8,128)S(1)}, f32[224,128]{1,0:T(8,128)S(1)}, u32[]{:S(2)}, u32[]{:S(2)}) collective-permute-start(f32[224,128]{1,0:T(8,128)S(1)} %get-tuple-element.38), channel_id=1, source_target_pairs={{1,2},{3,4},{5,6},{7,8},{9,10},{11,12},{13,14},{15,16},{17,18},{19... | collective-permute-start | bytes 344072 | tf_op jit(solution)/shard_map/ppermute | solution.py:544
  25.7 15.0 %collective-permute-start.3 = (f32[224,128]{1,0:T(8,128)S(1)}, f32[224,128]{1,0:T(8,128)S(1)}, u32[]{:S(2)}, u32[]{:S(2)}) collective-permute-start(f32[224,128]{1,0:T(8,128)S(1)} %get-tuple-element.37), channel_id=1, source_target_pairs={{0,1},{2,3},{4,5},{6,7},{8,9},{10,11},{12,13},{14,15},{16,17},{18,... | collective-permute-start | bytes 344072 | tf_op jit(solution)/shard_map/ppermute | solution.py:543

commit v6 on v5

--- a/solution.py
+++ b/solution.py
@@ -20,6 +20,7 @@
 CORNERS = 6 * EDGE
 YMSG = CORNERS + 32
 F32 = jnp.float32
+INNER = pl.ds(8, EDGE)
 VMEM = pltpu.VMEM
 
 
@@ -98,37 +99,33 @@
     lane = iota(v[0].shape, 1)
     half = lane < 2 * EDGE
     even = (lane // EDGE) % 2 == 0
-    w = [pltpu.roll(a, 2 * EDGE, 1) for a in v]
-    a0, a1 = jnp.where(half, v[0], w[2]), jnp.where(half, v[1], w[3])
-    a2, a3 = jnp.where(half, w[0], v[2]), jnp.where(half, w[1], v[3])
-    rows = []
-    for a, b in ((a0, a1), (a2, a3)):
-        rows.append(jnp.where(even, a, pltpu.roll(b, EDGE, 1)))
-        rows.append(jnp.where(even, pltpu.roll(a, LANES - EDGE, 1), b))
-    return rows
-
-
-def relayout_edges(counts_ref, old_ref, edges, slabs, counts, boxes, sems):
+    outer = (lane < EDGE) | (lane >= 3 * EDGE)
+    pairs = []
+    for a, b in ((v[0], v[1]), (v[2], v[3])):
+        turned = pltpu.roll(jnp.where(even, b, a), EDGE, 1)
+        pairs.append((jnp.where(even, a, turned), jnp.where(even, turned, b)))
+    (a0, a1), (b0, b1) = pairs
+    turned = pltpu.roll(jnp.where(half, b0, a0), 2 * EDGE, 1)
+    crossed = pltpu.roll(jnp.where(half, b1, a1), 2 * EDGE, 1)
+    kept = jnp.where(half, a1, b1)
+    return [
+        jnp.where(half, a0, turned),
+        jnp.where(outer, crossed, kept),
+        jnp.where(half, turned, b0),
+        jnp.where(outer, kept, crossed),
+    ]
+
+
+def relayout(counts_ref, old_ref, out, edges, counts, boxes, sems):
     copies, moved = fetch(counts_ref, old_ref, counts, boxes, sems, 0)
     slots = [jnp.maximum(c - moved, 0) for c in range(COLUMN)]
-    for f in range(FIELDS):
-        copies[f].wait()
-        for g in range(GROUPS):
-            for r, row in enumerate(interleave([box_tiles(boxes, f, slot, g, "edge") for slot in slots])):
-                edges[f, 4 * g + r] = row
-        for side, g in enumerate((0, GROUPS - 1)):
-            for r, row in enumerate(interleave([boxes[f, slot, :, lane_group(g)] for slot in slots])):
-                slabs[f, side, r] = row
-
-
-def relayout(counts_ref, old_ref, out, counts, boxes, sems):
-    copies, moved = fetch(counts_ref, old_ref, counts, boxes, sems, 0)
-    slots = [jnp.maximum(c - moved, 0) for c in range(COLUMN)]
+    low = iota((8, LANES), 0) < 4
     for f in range(FIELDS):
         copies[f].wait()
         for g in range(GROUPS):
             for r, row in enumerate(interleave([boxes[f, slot, :, lane_group(g)] for slot in slots])):
                 out[f, 4 * g + r] = row
+                edges[f, 4 * g + r] = jnp.where(low, row[0:8], row[24:32])
 
 
 def unmix(kinds, f):
@@ -179,13 +176,13 @@
             second[y] = jnp.where(odd, up, down)
 
 
-def make_slabs(counts_ref, shell, slabs, first, second):
+def make_slabs(counts_ref, shell, own, first, second):
     taken = iota((EDGE, LANES), 1) < moved_boxes(counts_ref) * EDGE
     blacks = [~is_red((EDGE, LANES), y) for y in range(2)]
     sides = []
     for side, g in enumerate((0, GROUPS - 1)):
         kinds = [wire_rows(shell, None, k, g) for k in range(KINDS)]
-        p, f, b = [[jnp.where(taken, row, slabs[i, side, r]) for r, row in enumerate(unmix(kinds, i))] for i in range(FIELDS)]
+        p, f, b = [[jnp.where(taken, row, own[i, 4 * g + r]) for r, row in enumerate(unmix(kinds, i))] for i in range(FIELDS)]
         near, next_, far = (3, 2, 1) if side else (0, 1, 2)
         sides.append(
             [
@@ -227,7 +224,7 @@
     limit = moved_boxes(counts_ref) * EDGE
     taken = iota((EDGE, LANES), 1) < limit
     reds = [is_red((EDGE, LANES), y) for y in range(2)]
-    before = None
+    before = jnp.zeros((EDGE, LANES), F32)
     for g in range(GROUPS):
         kinds = [wire_rows(shell, core, k, g) for k in range(KINDS)]
         parts = [unmix(kinds, f) for f in range(FIELDS)]
@@ -235,12 +232,11 @@
             y = 4 * g + r
             p, f, b = [jnp.where(taken, parts[i][r], own[i, y]) for i in range(FIELDS)]
             h = 0.5 * b
-            half[y] = h
-            rhs[y] = f
-            if y:
-                mix[y - 1] = jnp.where(reds[(y - 1) % 2], h * p, before)
+            half[y + 4, INNER] = h
+            rhs[y + 4, INNER] = f
+            mix[y + 3, INNER] = jnp.where(reds[(y - 1) % 2], h * p, before)
             before = p
-    mix[EDGE - 1] = before
+    mix[EDGE + 3, INNER] = before
 
 
 def tile(row):
@@ -347,25 +343,14 @@
     return lax.fori_loop(0, count // 4, body, carry)
 
 
-INNER = pl.ds(8, EDGE)
-
-
 def order(axis, first, second):
     odd = is_odd(axis)
     return jnp.where(odd, first, second), jnp.where(odd, second, first)
 
 
-def sweep_inner(half_in, mix_in, rhs_in, x_first, x_second, *refs):
+def sweep_inner(counts_ref, own, shell, core, x_first, x_second, *refs):
     w = Sweep(4, *refs)
-    w.mix[3, INNER] = half_in[0] * mix_in[0]
-
-    def take_in(y, odd, carry):
-        w.half[y + 4, INNER] = half_in[y]
-        w.mix[y + 4, INNER] = mix_in[y]
-        w.rhs[y + 4, INNER] = rhs_in[y]
-        return carry
-
-    fours(0, EDGE, take_in, 0)
+    assemble(counts_ref, own, shell, core, w.half, w.mix, w.rhs)
 
     def strips(k, odd, carry):
         y = EDGE - 1 - k
@@ -518,17 +503,17 @@
         return call(body, (table, old_fields), outputs, scratch, 10**6, 2 * 10**6, hbm=(0, 1), limit=limit)
 
     strip, message = (EDGE, 8, LANES), (YMSG, LANES)
-    deep, block = (DEEP, ROWS, LANES), (EDGE, EDGE, LANES)
+    deep = (DEEP, ROWS, LANES)
     (shell,) = read(pack_shell, [(KINDS, SHELL, 8, LANES)])
     (core,) = read(pack_core, [(KINDS, CORE, 8, LANES)], shell)
     shell = lax.ppermute(shell, ("grp", "dev"), chain)
     core = lax.ppermute(core, ("grp", "dev"), chain)
-    edges, slabs = read(relayout_edges, [(FIELDS, EDGE, 8, LANES), (FIELDS, 2, 4, EDGE, LANES)])
+    own, edges = read(relayout, [(FIELDS, EDGE, EDGE, LANES), (FIELDS, EDGE, 8, LANES)])
     x_first, x_second = call(make_faces, (counts, shell, edges), [strip, strip], [], 10**6, 10**6)
     table = lax.optimization_barrier((counts, x_first))[0]
     x_first = lax.ppermute(x_first, "grp", x_ways[0])
     x_second = lax.ppermute(x_second, "grp", x_ways[1])
-    y_first, y_second = call(make_slabs, (table, shell, slabs), [message, message], [], 10**6, 10**6)
+    y_first, y_second = call(make_slabs, (table, shell, own), [message, message], [], 10**6, 10**6)
     y_first, y_second = call(
         add_corners,
         (x_first, x_second, y_first, y_second),
@@ -539,15 +524,12 @@
         aliases={2: 0, 3: 1},
         anywhere=True,
     )
-    after = y_first
     y_first = lax.ppermute(y_first, "dev", y_ways[0])
     y_second = lax.ppermute(y_second, "dev", y_ways[1])
-    (own,) = read(relayout, [(FIELDS, EDGE, EDGE, LANES)], after, 40 * 2**20)
-    half, mix, rhs = call(assemble, (counts, own, shell, core), [block] * 3, [], 10**6, 10**6)
     flat = (EDGE * EDGE, LANES)
     part_p, part_r, *kept = call(
         sweep_inner,
-        (half, mix, rhs, x_first, x_second),
+        (counts, own, shell, core, x_first, x_second),
         [flat, flat] + [deep] * len(KEPT),
         [],
         10**8,

time: 42.5 us -> 41.3 us (0.972)
  the two profiles are of different devices: /device:TPU:220 before, /device:TPU:225 now
where the time goes in v6:
time: 41.3 us; the launch traced here: 40.9 us
  starting transfers between devices  19.8 us (48%)
  Pallas kernels  10.9 us (26%)
  waiting for transfers between devices  8.8 us (21%)
  between operations  0.76 us (2%)
  local copies, waits for them, and re-layouts  0.68 us (2%)
    pallas_call x8, Pallas kernels, call(): pl.pallas_call(body, out_shape=[jax.ShapeDtypeStruct(shape, F32) for shap...  10.9 us
    ppermute x1, starting transfers between devices, per_device(): x_second = lax.ppermute(x_second, 'grp', x_ways[1])  5.11 us
    ppermute x1, starting transfers between devices, per_device(): x_first = lax.ppermute(x_first, 'grp', x_ways[0])  4.57 us
    ppermute x1, waiting for transfers between devices, per_device(): shell = lax.ppermute(shell, ('grp', 'dev'), chain)  3.24 us
    ppermute x1, waiting for transfers between devices, per_device(): y_second = lax.ppermute(y_second, 'dev', y_ways[1])  3.15 us
    ppermute x1, starting transfers between devices, per_device(): shell = lax.ppermute(shell, ('grp', 'dev'), chain)  3.12 us
    ppermute x1, starting transfers between devices, per_device(): core = lax.ppermute(core, ('grp', 'dev'), chain)  3.12 us
    ppermute x1, waiting for transfers between devices, per_device(): x_second = lax.ppermute(x_second, 'grp', x_ways[1])  2.4 us
  transfers between devices with their start and end apart: 6, of which 3 were waited for; matrix products, arithmetic and copies ran while one was open for 0% of the time, Pallas kernels for 19%

profile of v6, /device:TPU:225, one launch (start us, length us, event | category | flops | bytes accessed | tf_op | source)
XLA Modules:
  0.0 40.9 jit_solution(6181245078027527367)
XLA Ops:
  0.6 0.0 copy-start
  0.6 0.7 %copy-done = s32[512]{0:T(512)S(1)} copy-done((s32[512]{0:T(512)S(1)}, s32[512]{0:T(512)}, u32[]{:S(2)}) %copy-start) | copy-done | bytes 2072
  1.3 1.5 %shard_map.41 = f32[5,14,8,128]{3,2,1,0:T(8,128)S(1)} custom-call(s32[4,128]{1,0:T(4,128)S(1)} %bitcast.3, f32[3,8,32,1024]{3,2,1,0:T(8,128)} %old_ref.5), custom_call_target="tpu_custom_call" | custom-call | flops 1000000 | bytes 2000000 | tf_op jit(solution)/shard_map/pallas_call | solution.py:469
  2.8 3.1 %collective-permute-start = (f32[5,14,8,128]{3,2,1,0:T(8,128)S(1)}, f32[5,14,8,128]{3,2,1,0:T(8,128)S(1)}, u32[]{:S(2)}, u32[]{:S(2)}) collective-permute-start(f32[5,14,8,128]{3,2,1,0:T(8,128)S(1)} %shard_map.41), channel_id=1, source_target_pairs={{0,1},{1,2},{2,3},{3,4},{4,5},{5,6},{6,7},{7,8},{8,9},{9,10},{10,1... | collective-permute-start | bytes 860168 | tf_op jit(solution)/shard_map/ppermute | solution.py:509
  6.0 1.5 %shard_map.46 = f32[5,18,8,128]{3,2,1,0:T(8,128)S(1)} custom-call(s32[4,128]{1,0:T(4,128)S(1)} %bitcast.4, f32[3,8,32,1024]{3,2,1,0:T(8,128)} %old_ref.5), custom_call_target="tpu_custom_call" | custom-call | flops 1000000 | bytes 2000000 | tf_op jit(solution)/shard_map/pallas_call | solution.py:469
  7.5 0.0 copy-start.1
  7.5 3.1 %collective-permute-start.5 = (f32[5,18,8,128]{3,2,1,0:T(8,128)S(1)}, f32[5,18,8,128]{3,2,1,0:T(8,128)S(1)}, u32[]{:S(2)}, u32[]{:S(2)}) collective-permute-start(f32[5,18,8,128]{3,2,1,0:T(8,128)S(1)} %shard_map.46), channel_id=1, source_target_pairs={{0,1},{1,2},{2,3},{3,4},{4,5},{5,6},{6,7},{7,8},{8,9},{9,10},{10,1... | collective-permute-start | bytes 1105928 | tf_op jit(solution)/shard_map/ppermute | solution.py:510
  10.6 1.9 %shard_map.42 = (f32[3,32,32,128]{3,2,1,0:T(8,128)S(1)}, f32[3,32,8,128]{3,2,1,0:T(8,128)S(1)}) custom-call(s32[4,128]{1,0:T(4,128)S(1)} %bitcast.5, f32[3,8,32,1024]{3,2,1,0:T(8,128)} %old_ref.5), custom_call_target="tpu_custom_call" | custom-call | flops 1000000 | bytes 2000000 | tf_op jit(solution)/shard_map/pallas_call | solution.py:469
  12.5 3.2 %collective-permute-done.shell = f32[5,14,8,128]{3,2,1,0:T(8,128)S(1)} collective-permute-done((f32[5,14,8,128]{3,2,1,0:T(8,128)S(1)}, f32[5,14,8,128]{3,2,1,0:T(8,128)S(1)}, u32[]{:S(2)}, u32[]{:S(2)}) %collective-permute-start) | collective-permute-done | bytes 286752 | tf_op jit(solution)/shard_map/ppermute | solution.py:509
  15.8 0.2 shard_map.43
  16.0 4.6 %collective-permute-start.1 = (f32[32,8,128]{2,1,0:T(8,128)S(1)}, f32[32,8,128]{2,1,0:T(8,128)S(1)}, u32[]{:S(2)}, u32[]{:S(2)}) collective-permute-start(f32[32,8,128]{2,1,0:T(8,128)S(1)} %get-tuple-element.27), channel_id=1, source_target_pairs={{0,32},{64,96},{128,160},{192,224},{256,288},{320,352},{384,416},{... | collective-permute-start | bytes 393224 | tf_op jit(solution)/shard_map/ppermute | solution.py:514
  20.5 5.1 %collective-permute-start.2 = (f32[32,8,128]{2,1,0:T(8,128)S(1)}, f32[32,8,128]{2,1,0:T(8,128)S(1)}, u32[]{:S(2)}, u32[]{:S(2)}) collective-permute-start(f32[32,8,128]{2,1,0:T(8,128)S(1)} %get-tuple-element.28), channel_id=1, source_target_pairs={{32,64},{96,128},{160,192},{224,256},{288,320},{352,384},{416,448}... | collective-permute-start | bytes 393224 | tf_op jit(solution)/shard_map/ppermute | solution.py:515
  25.7 0.2 shard_map.44
  25.9 0.0 collective-permute-done.1.x_first
  25.9 2.4 %collective-permute-done.2.x_second = f32[32,8,128]{2,1,0:T(8,128)S(1)} collective-permute-done((f32[32,8,128]{2,1,0:T(8,128)S(1)}, f32[32,8,128]{2,1,0:T(8,128)S(1)}, u32[]{:S(2)}, u32[]{:S(2)}) %collective-permute-start.2) | collective-permute-done | bytes 131104 | tf_op jit(solution)/shard_map/ppermute | solution.py:515
  28.3 0.1 shard_map.45
  28.4 1.9 %collective-permute-start.3 = (f32[224,128]{1,0:T(8,128)S(1)}, f32[224,128]{1,0:T(8,128)S(1)}, u32[]{:S(2)}, u32[]{:S(2)}) collective-permute-start(f32[224,128]{1,0:T(8,128)S(1)} %get-tuple-element.33), channel_id=1, source_target_pairs={{0,1},{2,3},{4,5},{6,7},{8,9},{10,11},{12,13},{14,15},{16,17},{18,... | collective-permute-start | bytes 344072 | tf_op jit(solution)/shard_map/ppermute | solution.py:527
  30.3 1.9 %collective-permute-start.4 = (f32[224,128]{1,0:T(8,128)S(1)}, f32[224,128]{1,0:T(8,128)S(1)}, u32[]{:S(2)}, u32[]{:S(2)}) collective-permute-start(f32[224,128]{1,0:T(8,128)S(1)} %get-tuple-element.34), channel_id=1, source_target_pairs={{1,2},{3,4},{5,6},{7,8},{9,10},{11,12},{13,14},{15,16},{17,18},{19... | collective-permute-start | bytes 344072 | tf_op jit(solution)/shard_map/ppermute | solution.py:528
  32.3 0.0 collective-permute-done.5.core
  32.3 0.0 copy-done.1
  32.3 4.0 %shard_map.47 = (f32[1024,128]{1,0:T(8,128)S(1)}, f32[1024,128]{1,0:T(8,128)S(1)}, f32[40,48,128]{2,1,0:T(8,128)S(1)}, f32[40,48,128]{2,1,0:T(8,128)S(1)}, f32[4...) custom-call(s32[4,128]{1,0:T(4,128)S(1)} %bitcast.8, ...), custom_call_target="tpu_custom_call" | custom-call | flops 100000000 | bytes 5000000 | tf_op jit(solution)/shard_map/pallas_call | solution.py:469
  36.3 0.0 collective-permute-done.3.y_first
  36.3 3.2 %collective-permute-done.4.y_second = f32[224,128]{1,0:T(8,128)S(1)} collective-permute-done((f32[224,128]{1,0:T(8,128)S(1)}, f32[224,128]{1,0:T(8,128)S(1)}, u32[]{:S(2)}, u32[]{:S(2)}) %collective-permute-start.4) | collective-permute-done | bytes 114720 | tf_op jit(solution)/shard_map/ppermute | solution.py:528
  39.4 1.5 %shard_map.48 = (f32[1024,128]{1,0:T(8,128)}, f32[1024,128]{1,0:T(8,128)}) custom-call(f32[224,128]{1,0:T(8,128)S(1)} %collective-permute-done.3.y_first, f32[224,128]{1,0:T(8,128)S(1)} %collective-permute-done.4.y_second, f32[32,8,128]{2,1,0:T(8,128)S(1)} %collective-permute-done.1.x_first, f32[32,8,128]{2,1,0:T(8,128)S(1)} %collective-permute-done.2.x_second, ...), custom_call_target="tpu_custom_call" | custom-call | flops 10000000 | bytes 1000000 | tf_op jit(solution)/shard_map/pallas_call | solution.py:469
Async XLA Ops:
  0.6 0.7 %copy-start = (s32[512]{0:T(512)S(1)}, s32[512]{0:T(512)}, u32[]{:S(2)}) copy-start(s32[512]{0:T(512)} %param.3) | copy-start | bytes 6148
  2.8 12.9 %collective-permute-start = (f32[5,14,8,128]{3,2,1,0:T(8,128)S(1)}, f32[5,14,8,128]{3,2,1,0:T(8,128)S(1)}, u32[]{:S(2)}, u32[]{:S(2)}) collective-permute-start(f32[5,14,8,128]{3,2,1,0:T(8,128)S(1)} %shard_map.41), channel_id=1, source_target_pairs={{0,1},{1,2},{2,3},{3,4},{4,5},{5,6},{6,7},{7,8},{8,9},{9,10},{10,1... | collective-permute-start | bytes 860168 | tf_op jit(solution)/shard_map/ppermute | solution.py:509
  7.5 24.8 %copy-start.1 = (s32[512]{0:T(512)S(1)}, s32[512]{0:T(512)}, u32[]{:S(2)}) copy-start(s32[512]{0:T(512)} %param.3) | copy-start | bytes 6148
  7.5 24.8 %collective-permute-start.5 = (f32[5,18,8,128]{3,2,1,0:T(8,128)S(1)}, f32[5,18,8,128]{3,2,1,0:T(8,128)S(1)}, u32[]{:S(2)}, u32[]{:S(2)}) collective-permute-start(f32[5,18,8,128]{3,2,1,0:T(8,128)S(1)} %shard_map.46), channel_id=1, source_target_pairs={{0,1},{1,2},{2,3},{3,4},{4,5},{5,6},{6,7},{7,8},{8,9},{9,10},{10,1... | collective-permute-start | bytes 1105928 | tf_op jit(solution)/shard_map/ppermute | solution.py:510
  16.0 9.9 %collective-permute-start.1 = (f32[32,8,128]{2,1,0:T(8,128)S(1)}, f32[32,8,128]{2,1,0:T(8,128)S(1)}, u32[]{:S(2)}, u32[]{:S(2)}) collective-permute-start(f32[32,8,128]{2,1,0:T(8,128)S(1)} %get-tuple-element.27), channel_id=1, source_target_pairs={{0,32},{64,96},{128,160},{192,224},{256,288},{320,352},{384,416},{... | collective-permute-start | bytes 393224 | tf_op jit(solution)/shard_map/ppermute | solution.py:514
  20.5 7.8 %collective-permute-start.2 = (f32[32,8,128]{2,1,0:T(8,128)S(1)}, f32[32,8,128]{2,1,0:T(8,128)S(1)}, u32[]{:S(2)}, u32[]{:S(2)}) collective-permute-start(f32[32,8,128]{2,1,0:T(8,128)S(1)} %get-tuple-element.28), channel_id=1, source_target_pairs={{32,64},{96,128},{160,192},{224,256},{288,320},{352,384},{416,448}... | collective-permute-start | bytes 393224 | tf_op jit(solution)/shard_map/ppermute | solution.py:515
  28.4 7.9 %collective-permute-start.3 = (f32[224,128]{1,0:T(8,128)S(1)}, f32[224,128]{1,0:T(8,128)S(1)}, u32[]{:S(2)}, u32[]{:S(2)}) collective-permute-start(f32[224,128]{1,0:T(8,128)S(1)} %get-tuple-element.33), channel_id=1, source_target_pairs={{0,1},{2,3},{4,5},{6,7},{8,9},{10,11},{12,13},{14,15},{16,17},{18,... | collective-permute-start | bytes 344072 | tf_op jit(solution)/shard_map/ppermute | solution.py:527
  30.3 9.1 %collective-permute-start.4 = (f32[224,128]{1,0:T(8,128)S(1)}, f32[224,128]{1,0:T(8,128)S(1)}, u32[]{:S(2)}, u32[]{:S(2)}) collective-permute-start(f32[224,128]{1,0:T(8,128)S(1)} %get-tuple-element.34), channel_id=1, source_target_pairs={{1,2},{3,4},{5,6},{7,8},{9,10},{11,12},{13,14},{15,16},{17,18},{19... | collective-permute-start | bytes 344072 | tf_op jit(solution)/shard_map/ppermute | solution.py:528

commit v7 on v6

--- a/solution.py
+++ b/solution.py
@@ -13,7 +13,7 @@
 FIELDS = 3
 MOVED = 2
 KINDS = 5
-SHELL = GROUPS + 6
+RIM = 6
 CORE = 3 * (GROUPS - 2)
 ROWS = EDGE + 16
 DEEP = EDGE + 8
@@ -75,24 +75,18 @@
         out[2 * f, at] = jnp.where(even, turned[f], first[f])
 
 
-def pack_shell(counts_ref, old_ref, out, counts, boxes, sems):
+def pack_all(counts_ref, old_ref, shell, rim, core, counts, boxes, sems):
     copies, moved = fetch(counts_ref, old_ref, counts, boxes, sems, MOVED)
     for copy in copies:
         copy.wait()
     for g in range(GROUPS):
-        pack(boxes, moved, out, g, g, "edge")
-    for side, g in enumerate((0, GROUPS - 1)):
+        pack(boxes, moved, shell, g, g, "edge")
+    for g in range(GROUPS):
         for which in range(3):
-            pack(boxes, moved, out, GROUPS + 3 * side + which, g, which)
-
-
-def pack_core(counts_ref, old_ref, out, counts, boxes, sems):
-    copies, moved = fetch(counts_ref, old_ref, counts, boxes, sems, MOVED)
-    for copy in copies:
-        copy.wait()
-    for g in range(1, GROUPS - 1):
-        for which in range(3):
-            pack(boxes, moved, out, 3 * (g - 1) + which, g, which)
+            if g in (0, GROUPS - 1):
+                pack(boxes, moved, rim, (3 if g else 0) + which, g, which)
+            else:
+                pack(boxes, moved, core, 3 * (g - 1) + which, g, which)
 
 
 def interleave(v):
@@ -116,16 +110,27 @@
     ]
 
 
-def relayout(counts_ref, old_ref, out, edges, counts, boxes, sems):
+def relayout_edges(counts_ref, old_ref, edges, slabs, counts, boxes, sems):
     copies, moved = fetch(counts_ref, old_ref, counts, boxes, sems, 0)
     slots = [jnp.maximum(c - moved, 0) for c in range(COLUMN)]
-    low = iota((8, LANES), 0) < 4
+    for f in range(FIELDS):
+        copies[f].wait()
+        for g in range(GROUPS):
+            for r, row in enumerate(interleave([box_tiles(boxes, f, slot, g, "edge") for slot in slots])):
+                edges[f, 4 * g + r] = row
+        for side, g in enumerate((0, GROUPS - 1)):
+            for r, row in enumerate(interleave([boxes[f, slot, :, lane_group(g)] for slot in slots])):
+                slabs[f, side, r] = row
+
+
+def relayout(counts_ref, old_ref, out, counts, boxes, sems):
+    copies, moved = fetch(counts_ref, old_ref, counts, boxes, sems, 0)
+    slots = [jnp.maximum(c - moved, 0) for c in range(COLUMN)]
     for f in range(FIELDS):
         copies[f].wait()
         for g in range(GROUPS):
             for r, row in enumerate(interleave([boxes[f, slot, :, lane_group(g)] for slot in slots])):
                 out[f, 4 * g + r] = row
-                edges[f, 4 * g + r] = jnp.where(low, row[0:8], row[24:32])
 
 
 def unmix(kinds, f):
@@ -136,11 +141,11 @@
     return [a, pltpu.roll(b, LANES - EDGE, 1), pltpu.roll(a, 2 * EDGE, 1), pltpu.roll(b, EDGE, 1)]
 
 
-def wire_rows(shell, core, k, g):
+def wire_rows(shell, rim, core, k, g):
     low = iota((8, LANES), 0) < 4
     edge = shell[k, g]
     if g in (0, GROUPS - 1):
-        mid = [shell[k, GROUPS + (3 if g else 0) + which] for which in range(3)]
+        mid = [rim[k, (3 if g else 0) + which] for which in range(3)]
     else:
         mid = [core[k, 3 * (g - 1) + which] for which in range(3)]
     return jnp.concatenate([jnp.where(low, edge, mid[0]), mid[1], mid[2], jnp.where(low, mid[0], edge)], axis=0)
@@ -176,13 +181,13 @@
             second[y] = jnp.where(odd, up, down)
 
 
-def make_slabs(counts_ref, shell, own, first, second):
+def make_slabs(counts_ref, shell, rim, slabs, first, second):
     taken = iota((EDGE, LANES), 1) < moved_boxes(counts_ref) * EDGE
     blacks = [~is_red((EDGE, LANES), y) for y in range(2)]
     sides = []
     for side, g in enumerate((0, GROUPS - 1)):
-        kinds = [wire_rows(shell, None, k, g) for k in range(KINDS)]
-        p, f, b = [[jnp.where(taken, row, own[i, 4 * g + r]) for r, row in enumerate(unmix(kinds, i))] for i in range(FIELDS)]
+        kinds = [wire_rows(shell, rim, None, k, g) for k in range(KINDS)]
+        p, f, b = [[jnp.where(taken, row, slabs[i, side, r]) for r, row in enumerate(unmix(kinds, i))] for i in range(FIELDS)]
         near, next_, far = (3, 2, 1) if side else (0, 1, 2)
         sides.append(
             [
@@ -220,13 +225,13 @@
     return (iota(shape, 0) + iota(shape, 1) + shift) & 1 == 0
 
 
-def assemble(counts_ref, own, shell, core, half, mix, rhs):
+def assemble(counts_ref, own, shell, rim, core, half, mix, rhs):
     limit = moved_boxes(counts_ref) * EDGE
     taken = iota((EDGE, LANES), 1) < limit
     reds = [is_red((EDGE, LANES), y) for y in range(2)]
     before = jnp.zeros((EDGE, LANES), F32)
     for g in range(GROUPS):
-        kinds = [wire_rows(shell, core, k, g) for k in range(KINDS)]
+        kinds = [wire_rows(shell, rim, core, k, g) for k in range(KINDS)]
         parts = [unmix(kinds, f) for f in range(FIELDS)]
         for r in range(4):
             y = 4 * g + r
@@ -348,9 +353,9 @@
     return jnp.where(odd, first, second), jnp.where(odd, second, first)
 
 
-def sweep_inner(counts_ref, own, shell, core, x_first, x_second, *refs):
+def sweep_inner(counts_ref, own, shell, rim, core, x_first, x_second, *refs):
     w = Sweep(4, *refs)
-    assemble(counts_ref, own, shell, core, w.half, w.mix, w.rhs)
+    assemble(counts_ref, own, shell, rim, core, w.half, w.mix, w.rhs)
 
     def strips(k, odd, carry):
         y = EDGE - 1 - k
@@ -504,16 +509,16 @@
 
     strip, message = (EDGE, 8, LANES), (YMSG, LANES)
     deep = (DEEP, ROWS, LANES)
-    (shell,) = read(pack_shell, [(KINDS, SHELL, 8, LANES)])
-    (core,) = read(pack_core, [(KINDS, CORE, 8, LANES)], shell)
+    shell, rim, core = read(pack_all, [(KINDS, n, 8, LANES) for n in (GROUPS, RIM, CORE)])
     shell = lax.ppermute(shell, ("grp", "dev"), chain)
+    rim = lax.ppermute(rim, ("grp", "dev"), chain)
     core = lax.ppermute(core, ("grp", "dev"), chain)
-    own, edges = read(relayout, [(FIELDS, EDGE, EDGE, LANES), (FIELDS, EDGE, 8, LANES)])
+    edges, slabs = read(relayout_edges, [(FIELDS, EDGE, 8, LANES), (FIELDS, 2, 4, EDGE, LANES)])
     x_first, x_second = call(make_faces, (counts, shell, edges), [strip, strip], [], 10**6, 10**6)
     table = lax.optimization_barrier((counts, x_first))[0]
     x_first = lax.ppermute(x_first, "grp", x_ways[0])
     x_second = lax.ppermute(x_second, "grp", x_ways[1])
-    y_first, y_second = call(make_slabs, (table, shell, own), [message, message], [], 10**6, 10**6)
+    y_first, y_second = call(make_slabs, (table, shell, rim, slabs), [message, message], [], 10**6, 10**6)
     y_first, y_second = call(
         add_corners,
         (x_first, x_second, y_first, y_second),
@@ -524,12 +529,13 @@
         aliases={2: 0, 3: 1},
         anywhere=True,
     )
+    (own,) = read(relayout, [(FIELDS, EDGE, EDGE, LANES)], y_first)
     y_first = lax.ppermute(y_first, "dev", y_ways[0])
     y_second = lax.ppermute(y_second, "dev", y_ways[1])
     flat = (EDGE * EDGE, LANES)
     part_p, part_r, *kept = call(
         sweep_inner,
-        (counts, own, shell, core, x_first, x_second),
+        (counts, own, shell, rim, core, x_first, x_second),
         [flat, flat] + [deep] * len(KEPT),
         [],
         10**8,

time: 41.3 us -> 48.5 us (1.17)
  the two profiles are of different devices: /device:TPU:225 before, /device:TPU:220 now
where the time goes in v7:
time: 48.5 us; the launch traced here: 48.1 us
  starting transfers between devices  31.8 us (66%)
  Pallas kernels  11.1 us (23%)
  waiting for transfers between devices  3.74 us (8%)
  between operations  0.79 us (2%)
  local copies, waits for them, and re-layouts  0.68 us (1%)
    pallas_call x8, Pallas kernels, call(): pl.pallas_call(body, out_shape=[jax.ShapeDtypeStruct(shape, F32) for shap...  11.1 us
    ppermute x1, starting transfers between devices, per_device(): y_first = lax.ppermute(y_first, 'dev', y_ways[0])  11 us
    ppermute x1, starting transfers between devices, per_device(): x_first = lax.ppermute(x_first, 'grp', x_ways[0])  5.59 us
    ppermute x1, starting transfers between devices, per_device(): core = lax.ppermute(core, ('grp', 'dev'), chain)  4.61 us
    ppermute x1, waiting for transfers between devices, per_device(): rim = lax.ppermute(rim, ('grp', 'dev'), chain)  3.73 us
    ppermute x1, starting transfers between devices, per_device(): rim = lax.ppermute(rim, ('grp', 'dev'), chain)  3.4 us
    ppermute x1, starting transfers between devices, per_device(): shell = lax.ppermute(shell, ('grp', 'dev'), chain)  3.11 us
    ppermute x1, starting transfers between devices, per_device(): y_second = lax.ppermute(y_second, 'dev', y_ways[1])  2.15 us
  transfers between devices with their start and end apart: 7, of which 1 were waited for; matrix products, arithmetic and copies ran while one was open for 0% of the time, Pallas kernels for 17%

profile of v7, /device:TPU:220, one launch (start us, length us, event | category | flops | bytes accessed | tf_op | source)
XLA Modules:
  0.0 48.1 jit_solution(11862342326176807659)
XLA Ops:
  0.6 0.0 copy-start
  0.6 0.7 %copy-done = s32[512]{0:T(512)S(1)} copy-done((s32[512]{0:T(512)S(1)}, s32[512]{0:T(512)}, u32[]{:S(2)}) %copy-start) | copy-done | bytes 2072
  1.3 1.6 %shard_map.41 = (f32[5,8,8,128]{3,2,1,0:T(8,128)S(1)}, f32[5,6,8,128]{3,2,1,0:T(8,128)S(1)}, f32[5,18,8,128]{3,2,1,0:T(8,128)S(1)}) custom-call(s32[4,128]{1,0:T(4,128)S(1)} %bitcast.3, f32[3,8,32,1024]{3,2,1,0:T(8,128)} %old_ref.5), custom_call_target="tpu_custom_call" | custom-call | flops 1000000 | bytes 2000000 | tf_op jit(solution)/shard_map/pallas_call | solution.py:474
  2.9 3.1 %collective-permute-start = (f32[5,8,8,128]{3,2,1,0:T(8,128)S(1)}, f32[5,8,8,128]{3,2,1,0:T(8,128)S(1)}, u32[]{:S(2)}, u32[]{:S(2)}) collective-permute-start(f32[5,8,8,128]{3,2,1,0:T(8,128)S(1)} %get-tuple-element.29), channel_id=1, source_target_pairs={{0,1},{1,2},{2,3},{3,4},{4,5},{5,6},{6,7},{7,8},{8,9},{9,10},{10,1... | collective-permute-start | bytes 491528 | tf_op jit(solution)/shard_map/ppermute | solution.py:513
  6.0 4.6 %collective-permute-start.6 = (f32[5,18,8,128]{3,2,1,0:T(8,128)S(1)}, f32[5,18,8,128]{3,2,1,0:T(8,128)S(1)}, u32[]{:S(2)}, u32[]{:S(2)}) collective-permute-start(f32[5,18,8,128]{3,2,1,0:T(8,128)S(1)} %get-tuple-element.41), channel_id=1, source_target_pairs={{0,1},{1,2},{2,3},{3,4},{4,5},{5,6},{6,7},{7,8},{8,9},{9,10},{10,1... | collective-permute-start | bytes 1105928 | tf_op jit(solution)/shard_map/ppermute | solution.py:515
  10.6 1.7 %shard_map.42 = (f32[3,32,8,128]{3,2,1,0:T(8,128)S(1)}, f32[3,2,4,32,128]{4,3,2,1,0:T(8,128)S(1)}) custom-call(s32[4,128]{1,0:T(4,128)S(1)} %bitcast.4, f32[3,8,32,1024]{3,2,1,0:T(8,128)} %old_ref.5), custom_call_target="tpu_custom_call" | custom-call | flops 1000000 | bytes 2000000 | tf_op jit(solution)/shard_map/pallas_call | solution.py:474
  12.3 0.0 collective-permute-done.shell
  12.3 0.0 copy-start.1
  12.3 0.2 shard_map.43
  12.5 1.9 %collective-permute-start.2 = (f32[32,8,128]{2,1,0:T(8,128)S(1)}, f32[32,8,128]{2,1,0:T(8,128)S(1)}, u32[]{:S(2)}, u32[]{:S(2)}) collective-permute-start(f32[32,8,128]{2,1,0:T(8,128)S(1)} %get-tuple-element.32), channel_id=1, source_target_pairs={{32,64},{96,128},{160,192},{224,256},{288,320},{352,384},{416,448}... | collective-permute-start | bytes 393224 | tf_op jit(solution)/shard_map/ppermute | solution.py:520
  14.4 5.6 %collective-permute-start.1 = (f32[32,8,128]{2,1,0:T(8,128)S(1)}, f32[32,8,128]{2,1,0:T(8,128)S(1)}, u32[]{:S(2)}, u32[]{:S(2)}) collective-permute-start(f32[32,8,128]{2,1,0:T(8,128)S(1)} %get-tuple-element.31), channel_id=1, source_target_pairs={{0,32},{64,96},{128,160},{192,224},{256,288},{320,352},{384,416},{... | collective-permute-start | bytes 393224 | tf_op jit(solution)/shard_map/ppermute | solution.py:519
  20.0 3.4 %collective-permute-start.3 = (f32[5,6,8,128]{3,2,1,0:T(8,128)S(1)}, f32[5,6,8,128]{3,2,1,0:T(8,128)S(1)}, u32[]{:S(2)}, u32[]{:S(2)}) collective-permute-start(f32[5,6,8,128]{3,2,1,0:T(8,128)S(1)} %get-tuple-element.34), channel_id=1, source_target_pairs={{0,1},{1,2},{2,3},{3,4},{4,5},{5,6},{6,7},{7,8},{8,9},{9,10},{10,1... | collective-permute-start | bytes 368648 | tf_op jit(solution)/shard_map/ppermute | solution.py:514
  23.4 3.7 %collective-permute-done.3.rim = f32[5,6,8,128]{3,2,1,0:T(8,128)S(1)} collective-permute-done((f32[5,6,8,128]{3,2,1,0:T(8,128)S(1)}, f32[5,6,8,128]{3,2,1,0:T(8,128)S(1)}, u32[]{:S(2)}, u32[]{:S(2)}) %collective-permute-start.3) | collective-permute-done | bytes 122912 | tf_op jit(solution)/shard_map/ppermute | solution.py:514
  27.2 0.2 shard_map.44
  27.4 0.0 collective-permute-done.2.x_second
  27.4 0.0 collective-permute-done.1.x_first
  27.4 0.1 shard_map.45
  27.6 2.2 %collective-permute-start.5 = (f32[224,128]{1,0:T(8,128)S(1)}, f32[224,128]{1,0:T(8,128)S(1)}, u32[]{:S(2)}, u32[]{:S(2)}) collective-permute-start(f32[224,128]{1,0:T(8,128)S(1)} %get-tuple-element.39), channel_id=1, source_target_pairs={{1,2},{3,4},{5,6},{7,8},{9,10},{11,12},{13,14},{15,16},{17,18},{19... | collective-permute-start | bytes 344072 | tf_op jit(solution)/shard_map/ppermute | solution.py:534
  29.7 11.0 %collective-permute-start.4 = (f32[224,128]{1,0:T(8,128)S(1)}, f32[224,128]{1,0:T(8,128)S(1)}, u32[]{:S(2)}, u32[]{:S(2)}) collective-permute-start(f32[224,128]{1,0:T(8,128)S(1)} %get-tuple-element.38), channel_id=1, source_target_pairs={{0,1},{2,3},{4,5},{6,7},{8,9},{10,11},{12,13},{14,15},{16,17},{18,... | collective-permute-start | bytes 344072 | tf_op jit(solution)/shard_map/ppermute | solution.py:533
  40.7 1.9 %shard_map.46.own = f32[3,32,32,128]{3,2,1,0:T(8,128)S(1)} custom-call(s32[4,128]{1,0:T(4,128)S(1)} %bitcast.7, f32[3,8,32,1024]{3,2,1,0:T(8,128)} %old_ref.5), custom_call_target="tpu_custom_call" | custom-call | flops 1000000 | bytes 2000000 | tf_op jit(solution)/shard_map/pallas_call | solution.py:474
  42.6 0.0 collective-permute-done.6.core
  42.7 3.9 %shard_map.47 = (f32[1024,128]{1,0:T(8,128)S(1)}, f32[1024,128]{1,0:T(8,128)S(1)}, f32[40,48,128]{2,1,0:T(8,128)S(1)}, f32[40,48,128]{2,1,0:T(8,128)S(1)}, f32[4...) custom-call(s32[4,128]{1,0:T(4,128)S(1)} %bitcast.8, ...), custom_call_target="tpu_custom_call" | custom-call | flops 100000000 | bytes 5000000 | tf_op jit(solution)/shard_map/pallas_call | solution.py:474
  46.6 0.0 collective-permute-done.5.y_second
  46.6 1.5 %shard_map.48 = (f32[1024,128]{1,0:T(8,128)}, f32[1024,128]{1,0:T(8,128)}) custom-call(f32[224,128]{1,0:T(8,128)S(1)} %collective-permute-done.4.y_first, f32[224,128]{1,0:T(8,128)S(1)} %collective-permute-done.5.y_second, f32[32,8,128]{2,1,0:T(8,128)S(1)} %collective-permute-done.1.x_first, f32[32,8,128]{2,1,0:T(8,128)S(1)} %collective-permute-done.2.x_second, ...), custom_call_target="tpu_custom_call" | custom-call | flops 10000000 | bytes 1000000 | tf_op jit(solution)/shard_map/pallas_call | solution.py:474
  (2 shorter events, 0.0 us)
Async XLA Ops:
  0.6 0.7 %copy-start = (s32[512]{0:T(512)S(1)}, s32[512]{0:T(512)}, u32[]{:S(2)}) copy-start(s32[512]{0:T(512)} %param.3) | copy-start | bytes 6148
  2.9 9.4 %collective-permute-start = (f32[5,8,8,128]{3,2,1,0:T(8,128)S(1)}, f32[5,8,8,128]{3,2,1,0:T(8,128)S(1)}, u32[]{:S(2)}, u32[]{:S(2)}) collective-permute-start(f32[5,8,8,128]{3,2,1,0:T(8,128)S(1)} %get-tuple-element.29), channel_id=1, source_target_pairs={{0,1},{1,2},{2,3},{3,4},{4,5},{5,6},{6,7},{7,8},{8,9},{9,10},{10,1... | collective-permute-start | bytes 491528 | tf_op jit(solution)/shard_map/ppermute | solution.py:513
  6.0 36.6 %collective-permute-start.6 = (f32[5,18,8,128]{3,2,1,0:T(8,128)S(1)}, f32[5,18,8,128]{3,2,1,0:T(8,128)S(1)}, u32[]{:S(2)}, u32[]{:S(2)}) collective-permute-start(f32[5,18,8,128]{3,2,1,0:T(8,128)S(1)} %get-tuple-element.41), channel_id=1, source_target_pairs={{0,1},{1,2},{2,3},{3,4},{4,5},{5,6},{6,7},{7,8},{8,9},{9,10},{10,1... | collective-permute-start | bytes 1105928 | tf_op jit(solution)/shard_map/ppermute | solution.py:515
  12.3 30.4 %copy-start.1 = (s32[512]{0:T(512)S(1)}, s32[512]{0:T(512)}, u32[]{:S(2)}) copy-start(s32[512]{0:T(512)} %param.3) | copy-start | bytes 6148
  12.5 14.9 %collective-permute-start.2 = (f32[32,8,128]{2,1,0:T(8,128)S(1)}, f32[32,8,128]{2,1,0:T(8,128)S(1)}, u32[]{:S(2)}, u32[]{:S(2)}) collective-permute-start(f32[32,8,128]{2,1,0:T(8,128)S(1)} %get-tuple-element.32), channel_id=1, source_target_pairs={{32,64},{96,128},{160,192},{224,256},{288,320},{352,384},{416,448}... | collective-permute-start | bytes 393224 | tf_op jit(solution)/shard_map/ppermute | solution.py:520
  14.4 13.0 %collective-permute-start.1 = (f32[32,8,128]{2,1,0:T(8,128)S(1)}, f32[32,8,128]{2,1,0:T(8,128)S(1)}, u32[]{:S(2)}, u32[]{:S(2)}) collective-permute-start(f32[32,8,128]{2,1,0:T(8,128)S(1)} %get-tuple-element.31), channel_id=1, source_target_pairs={{0,32},{64,96},{128,160},{192,224},{256,288},{320,352},{384,416},{... | collective-permute-start | bytes 393224 | tf_op jit(solution)/shard_map/ppermute | solution.py:519
  20.0 7.1 %collective-permute-start.3 = (f32[5,6,8,128]{3,2,1,0:T(8,128)S(1)}, f32[5,6,8,128]{3,2,1,0:T(8,128)S(1)}, u32[]{:S(2)}, u32[]{:S(2)}) collective-permute-start(f32[5,6,8,128]{3,2,1,0:T(8,128)S(1)} %get-tuple-element.34), channel_id=1, source_target_pairs={{0,1},{1,2},{2,3},{3,4},{4,5},{5,6},{6,7},{7,8},{8,9},{9,10},{10,1... | collective-permute-start | bytes 368648 | tf_op jit(solution)/shard_map/ppermute | solution.py:514
  27.6 19.0 %collective-permute-start.5 = (f32[224,128]{1,0:T(8,128)S(1)}, f32[224,128]{1,0:T(8,128)S(1)}, u32[]{:S(2)}, u32[]{:S(2)}) collective-permute-start(f32[224,128]{1,0:T(8,128)S(1)} %get-tuple-element.39), channel_id=1, source_target_pairs={{1,2},{3,4},{5,6},{7,8},{9,10},{11,12},{13,14},{15,16},{17,18},{19... | collective-permute-start | bytes 344072 | tf_op jit(solution)/shard_map/ppermute | solution.py:534
  29.7 16.9 %collective-permute-start.4 = (f32[224,128]{1,0:T(8,128)S(1)}, f32[224,128]{1,0:T(8,128)S(1)}, u32[]{:S(2)}, u32[]{:S(2)}) collective-permute-start(f32[224,128]{1,0:T(8,128)S(1)} %get-tuple-element.38), channel_id=1, source_target_pairs={{0,1},{2,3},{4,5},{6,7},{8,9},{10,11},{12,13},{14,15},{16,17},{18,... | collective-permute-start | bytes 344072 | tf_op jit(solution)/shard_map/ppermute | solution.py:533

commit v8 on v7

--- a/solution.py
+++ b/solution.py
@@ -110,27 +110,16 @@
     ]
 
 
-def relayout_edges(counts_ref, old_ref, edges, slabs, counts, boxes, sems):
+def relayout(counts_ref, old_ref, out, edges, counts, boxes, sems):
     copies, moved = fetch(counts_ref, old_ref, counts, boxes, sems, 0)
     slots = [jnp.maximum(c - moved, 0) for c in range(COLUMN)]
-    for f in range(FIELDS):
-        copies[f].wait()
-        for g in range(GROUPS):
-            for r, row in enumerate(interleave([box_tiles(boxes, f, slot, g, "edge") for slot in slots])):
-                edges[f, 4 * g + r] = row
-        for side, g in enumerate((0, GROUPS - 1)):
-            for r, row in enumerate(interleave([boxes[f, slot, :, lane_group(g)] for slot in slots])):
-                slabs[f, side, r] = row
-
-
-def relayout(counts_ref, old_ref, out, counts, boxes, sems):
-    copies, moved = fetch(counts_ref, old_ref, counts, boxes, sems, 0)
-    slots = [jnp.maximum(c - moved, 0) for c in range(COLUMN)]
+    low = iota((8, LANES), 0) < 4
     for f in range(FIELDS):
         copies[f].wait()
         for g in range(GROUPS):
             for r, row in enumerate(interleave([boxes[f, slot, :, lane_group(g)] for slot in slots])):
                 out[f, 4 * g + r] = row
+                edges[f, 4 * g + r] = jnp.where(low, row[0:8], row[24:32])
 
 
 def unmix(kinds, f):
@@ -181,13 +170,13 @@
             second[y] = jnp.where(odd, up, down)
 
 
-def make_slabs(counts_ref, shell, rim, slabs, first, second):
+def make_slabs(counts_ref, shell, rim, own, first, second):
     taken = iota((EDGE, LANES), 1) < moved_boxes(counts_ref) * EDGE
     blacks = [~is_red((EDGE, LANES), y) for y in range(2)]
     sides = []
     for side, g in enumerate((0, GROUPS - 1)):
         kinds = [wire_rows(shell, rim, None, k, g) for k in range(KINDS)]
-        p, f, b = [[jnp.where(taken, row, slabs[i, side, r]) for r, row in enumerate(unmix(kinds, i))] for i in range(FIELDS)]
+        p, f, b = [[jnp.where(taken, row, own[i, 4 * g + r]) for r, row in enumerate(unmix(kinds, i))] for i in range(FIELDS)]
         near, next_, far = (3, 2, 1) if side else (0, 1, 2)
         sides.append(
             [
@@ -513,12 +502,12 @@
     shell = lax.ppermute(shell, ("grp", "dev"), chain)
     rim = lax.ppermute(rim, ("grp", "dev"), chain)
     core = lax.ppermute(core, ("grp", "dev"), chain)
-    edges, slabs = read(relayout_edges, [(FIELDS, EDGE, 8, LANES), (FIELDS, 2, 4, EDGE, LANES)])
+    own, edges = read(relayout, [(FIELDS, EDGE, EDGE, LANES), (FIELDS, EDGE, 8, LANES)])
     x_first, x_second = call(make_faces, (counts, shell, edges), [strip, strip], [], 10**6, 10**6)
     table = lax.optimization_barrier((counts, x_first))[0]
     x_first = lax.ppermute(x_first, "grp", x_ways[0])
     x_second = lax.ppermute(x_second, "grp", x_ways[1])
-    y_first, y_second = call(make_slabs, (table, shell, rim, slabs), [message, message], [], 10**6, 10**6)
+    y_first, y_second = call(make_slabs, (table, shell, rim, own), [message, message], [], 10**6, 10**6)
     y_first, y_second = call(
         add_corners,
         (x_first, x_second, y_first, y_second),
@@ -529,7 +518,6 @@
         aliases={2: 0, 3: 1},
         anywhere=True,
     )
-    (own,) = read(relayout, [(FIELDS, EDGE, EDGE, LANES)], y_first)
     y_first = lax.ppermute(y_first, "dev", y_ways[0])
     y_second = lax.ppermute(y_second, "dev", y_ways[1])
     flat = (EDGE * EDGE, LANES)

time: 48.5 us -> 45.2 us (0.932)
  the two profiles are of different devices: /device:TPU:220 before, /device:TPU:197 now
where the time goes in v8:
time: 45.2 us; the launch traced here: 44.9 us
  starting transfers between devices  31.3 us (69%)
  Pallas kernels  9.53 us (21%)
  waiting for transfers between devices  2.59 us (6%)
  between operations  0.79 us (2%)
  local copies, waits for them, and re-layouts  0.68 us (2%)
    ppermute x1, starting transfers between devices, per_device(): y_second = lax.ppermute(y_second, 'dev', y_ways[1])  9.95 us
    pallas_call x7, Pallas kernels, call(): pl.pallas_call(body, out_shape=[jax.ShapeDtypeStruct(shape, F32) for shap...  9.53 us
    ppermute x1, starting transfers between devices, per_device(): x_second = lax.ppermute(x_second, 'grp', x_ways[1])  5.11 us
    ppermute x1, starting transfers between devices, per_device(): y_first = lax.ppermute(y_first, 'dev', y_ways[0])  3.99 us
    ppermute x1, starting transfers between devices, per_device(): x_first = lax.ppermute(x_first, 'grp', x_ways[0])  3.22 us
    ppermute x1, starting transfers between devices, per_device(): core = lax.ppermute(core, ('grp', 'dev'), chain)  3.12 us
    ppermute x1, starting transfers between devices, per_device(): rim = lax.ppermute(rim, ('grp', 'dev'), chain)  3.04 us
    ppermute x1, starting transfers between devices, per_device(): shell = lax.ppermute(shell, ('grp', 'dev'), chain)  2.83 us
  transfers between devices with their start and end apart: 7, of which 1 were waited for; matrix products, arithmetic and copies ran while one was open for 0% of the time, Pallas kernels for 14%

profile of v8, /device:TPU:197, one launch (start us, length us, event | category | flops | bytes accessed | tf_op | source)
XLA Modules:
  0.0 44.9 jit_solution(63699844308006743)
XLA Ops:
  0.6 0.0 copy-start
  0.6 0.7 %copy-done = s32[512]{0:T(512)S(1)} copy-done((s32[512]{0:T(512)S(1)}, s32[512]{0:T(512)}, u32[]{:S(2)}) %copy-start) | copy-done | bytes 2072
  1.3 1.6 %shard_map.41 = (f32[5,8,8,128]{3,2,1,0:T(8,128)S(1)}, f32[5,6,8,128]{3,2,1,0:T(8,128)S(1)}, f32[5,18,8,128]{3,2,1,0:T(8,128)S(1)}) custom-call(s32[4,128]{1,0:T(4,128)S(1)} %bitcast.3, f32[3,8,32,1024]{3,2,1,0:T(8,128)} %old_ref.3), custom_call_target="tpu_custom_call" | custom-call | flops 1000000 | bytes 2000000 | tf_op jit(solution)/shard_map/pallas_call | solution.py:463
  2.9 0.0 copy-start.1
  2.9 2.8 %collective-permute-start = (f32[5,8,8,128]{3,2,1,0:T(8,128)S(1)}, f32[5,8,8,128]{3,2,1,0:T(8,128)S(1)}, u32[]{:S(2)}, u32[]{:S(2)}) collective-permute-start(f32[5,8,8,128]{3,2,1,0:T(8,128)S(1)} %get-tuple-element.28), channel_id=1, source_target_pairs={{0,1},{1,2},{2,3},{3,4},{4,5},{5,6},{6,7},{7,8},{8,9},{9,10},{10,1... | collective-permute-start | bytes 491528 | tf_op jit(solution)/shard_map/ppermute | solution.py:502
  5.7 3.1 %collective-permute-start.6 = (f32[5,18,8,128]{3,2,1,0:T(8,128)S(1)}, f32[5,18,8,128]{3,2,1,0:T(8,128)S(1)}, u32[]{:S(2)}, u32[]{:S(2)}) collective-permute-start(f32[5,18,8,128]{3,2,1,0:T(8,128)S(1)} %get-tuple-element.39), channel_id=1, source_target_pairs={{0,1},{1,2},{2,3},{3,4},{4,5},{5,6},{6,7},{7,8},{8,9},{9,10},{10,1... | collective-permute-start | bytes 1105928 | tf_op jit(solution)/shard_map/ppermute | solution.py:504
  8.9 1.9 %shard_map.42 = (f32[3,32,32,128]{3,2,1,0:T(8,128)S(1)}, f32[3,32,8,128]{3,2,1,0:T(8,128)S(1)}) custom-call(s32[4,128]{1,0:T(4,128)S(1)} %bitcast.4, f32[3,8,32,1024]{3,2,1,0:T(8,128)} %old_ref.3), custom_call_target="tpu_custom_call" | custom-call | flops 1000000 | bytes 2000000 | tf_op jit(solution)/shard_map/pallas_call | solution.py:463
  10.8 0.0 collective-permute-done.shell
  10.8 0.2 shard_map.43
  11.0 3.2 %collective-permute-start.1 = (f32[32,8,128]{2,1,0:T(8,128)S(1)}, f32[32,8,128]{2,1,0:T(8,128)S(1)}, u32[]{:S(2)}, u32[]{:S(2)}) collective-permute-start(f32[32,8,128]{2,1,0:T(8,128)S(1)} %get-tuple-element.30), channel_id=1, source_target_pairs={{0,32},{64,96},{128,160},{192,224},{256,288},{320,352},{384,416},{... | collective-permute-start | bytes 393224 | tf_op jit(solution)/shard_map/ppermute | solution.py:508
  14.2 5.1 %collective-permute-start.2 = (f32[32,8,128]{2,1,0:T(8,128)S(1)}, f32[32,8,128]{2,1,0:T(8,128)S(1)}, u32[]{:S(2)}, u32[]{:S(2)}) collective-permute-start(f32[32,8,128]{2,1,0:T(8,128)S(1)} %get-tuple-element.31), channel_id=1, source_target_pairs={{32,64},{96,128},{160,192},{224,256},{288,320},{352,384},{416,448}... | collective-permute-start | bytes 393224 | tf_op jit(solution)/shard_map/ppermute | solution.py:509
  19.3 3.0 %collective-permute-start.3 = (f32[5,6,8,128]{3,2,1,0:T(8,128)S(1)}, f32[5,6,8,128]{3,2,1,0:T(8,128)S(1)}, u32[]{:S(2)}, u32[]{:S(2)}) collective-permute-start(f32[5,6,8,128]{3,2,1,0:T(8,128)S(1)} %get-tuple-element.33), channel_id=1, source_target_pairs={{0,1},{1,2},{2,3},{3,4},{4,5},{5,6},{6,7},{7,8},{8,9},{9,10},{10,1... | collective-permute-start | bytes 368648 | tf_op jit(solution)/shard_map/ppermute | solution.py:503
  22.4 2.6 %collective-permute-done.3.rim = f32[5,6,8,128]{3,2,1,0:T(8,128)S(1)} collective-permute-done((f32[5,6,8,128]{3,2,1,0:T(8,128)S(1)}, f32[5,6,8,128]{3,2,1,0:T(8,128)S(1)}, u32[]{:S(2)}, u32[]{:S(2)}) %collective-permute-start.3) | collective-permute-done | bytes 122912 | tf_op jit(solution)/shard_map/ppermute | solution.py:503
  24.9 0.2 shard_map.44
  25.2 0.0 collective-permute-done.1.x_first
  25.2 0.0 collective-permute-done.2.x_second
  25.2 0.1 shard_map.45
  25.3 4.0 %collective-permute-start.4 = (f32[224,128]{1,0:T(8,128)S(1)}, f32[224,128]{1,0:T(8,128)S(1)}, u32[]{:S(2)}, u32[]{:S(2)}) collective-permute-start(f32[224,128]{1,0:T(8,128)S(1)} %get-tuple-element.37), channel_id=1, source_target_pairs={{0,1},{2,3},{4,5},{6,7},{8,9},{10,11},{12,13},{14,15},{16,17},{18,... | collective-permute-start | bytes 344072 | tf_op jit(solution)/shard_map/ppermute | solution.py:521
  29.3 10.0 %collective-permute-start.5 = (f32[224,128]{1,0:T(8,128)S(1)}, f32[224,128]{1,0:T(8,128)S(1)}, u32[]{:S(2)}, u32[]{:S(2)}) collective-permute-start(f32[224,128]{1,0:T(8,128)S(1)} %get-tuple-element.38), channel_id=1, source_target_pairs={{1,2},{3,4},{5,6},{7,8},{9,10},{11,12},{13,14},{15,16},{17,18},{19... | collective-permute-start | bytes 344072 | tf_op jit(solution)/shard_map/ppermute | solution.py:522
  39.3 0.0 collective-permute-done.6.core
  39.3 4.0 %shard_map.46 = (f32[1024,128]{1,0:T(8,128)S(1)}, f32[1024,128]{1,0:T(8,128)S(1)}, f32[40,48,128]{2,1,0:T(8,128)S(1)}, f32[40,48,128]{2,1,0:T(8,128)S(1)}, f32[4...) custom-call(s32[4,128]{1,0:T(4,128)S(1)} %bitcast.7, ...), custom_call_target="tpu_custom_call" | custom-call | flops 100000000 | bytes 5000000 | tf_op jit(solution)/shard_map/pallas_call | solution.py:463
  43.3 0.0 collective-permute-done.4.y_first
  43.3 0.0 collective-permute-done.5.y_second
  43.3 1.5 %shard_map.47 = (f32[1024,128]{1,0:T(8,128)}, f32[1024,128]{1,0:T(8,128)}) custom-call(f32[224,128]{1,0:T(8,128)S(1)} %collective-permute-done.4.y_first, f32[224,128]{1,0:T(8,128)S(1)} %collective-permute-done.5.y_second, f32[32,8,128]{2,1,0:T(8,128)S(1)} %collective-permute-done.1.x_first, f32[32,8,128]{2,1,0:T(8,128)S(1)} %collective-permute-done.2.x_second, ...), custom_call_target="tpu_custom_call" | custom-call | flops 10000000 | bytes 1000000 | tf_op jit(solution)/shard_map/pallas_call | solution.py:463
  (1 shorter events, 0.0 us)
Async XLA Ops:
  0.6 0.7 %copy-start = (s32[512]{0:T(512)S(1)}, s32[512]{0:T(512)}, u32[]{:S(2)}) copy-start(s32[512]{0:T(512)} %param.3) | copy-start | bytes 6148
  2.9 36.4 %copy-start.1 = (s32[512]{0:T(512)S(1)}, s32[512]{0:T(512)}, u32[]{:S(2)}) copy-start(s32[512]{0:T(512)} %param.3) | copy-start | bytes 6148
  2.9 7.9 %collective-permute-start = (f32[5,8,8,128]{3,2,1,0:T(8,128)S(1)}, f32[5,8,8,128]{3,2,1,0:T(8,128)S(1)}, u32[]{:S(2)}, u32[]{:S(2)}) collective-permute-start(f32[5,8,8,128]{3,2,1,0:T(8,128)S(1)} %get-tuple-element.28), channel_id=1, source_target_pairs={{0,1},{1,2},{2,3},{3,4},{4,5},{5,6},{6,7},{7,8},{8,9},{9,10},{10,1... | collective-permute-start | bytes 491528 | tf_op jit(solution)/shard_map/ppermute | solution.py:502
  5.7 33.6 %collective-permute-start.6 = (f32[5,18,8,128]{3,2,1,0:T(8,128)S(1)}, f32[5,18,8,128]{3,2,1,0:T(8,128)S(1)}, u32[]{:S(2)}, u32[]{:S(2)}) collective-permute-start(f32[5,18,8,128]{3,2,1,0:T(8,128)S(1)} %get-tuple-element.39), channel_id=1, source_target_pairs={{0,1},{1,2},{2,3},{3,4},{4,5},{5,6},{6,7},{7,8},{8,9},{9,10},{10,1... | collective-permute-start | bytes 1105928 | tf_op jit(solution)/shard_map/ppermute | solution.py:504
  11.0 14.2 %collective-permute-start.1 = (f32[32,8,128]{2,1,0:T(8,128)S(1)}, f32[32,8,128]{2,1,0:T(8,128)S(1)}, u32[]{:S(2)}, u32[]{:S(2)}) collective-permute-start(f32[32,8,128]{2,1,0:T(8,128)S(1)} %get-tuple-element.30), channel_id=1, source_target_pairs={{0,32},{64,96},{128,160},{192,224},{256,288},{320,352},{384,416},{... | collective-permute-start | bytes 393224 | tf_op jit(solution)/shard_map/ppermute | solution.py:508
  14.2 11.0 %collective-permute-start.2 = (f32[32,8,128]{2,1,0:T(8,128)S(1)}, f32[32,8,128]{2,1,0:T(8,128)S(1)}, u32[]{:S(2)}, u32[]{:S(2)}) collective-permute-start(f32[32,8,128]{2,1,0:T(8,128)S(1)} %get-tuple-element.31), channel_id=1, source_target_pairs={{32,64},{96,128},{160,192},{224,256},{288,320},{352,384},{416,448}... | collective-permute-start | bytes 393224 | tf_op jit(solution)/shard_map/ppermute | solution.py:509
  19.3 5.6 %collective-permute-start.3 = (f32[5,6,8,128]{3,2,1,0:T(8,128)S(1)}, f32[5,6,8,128]{3,2,1,0:T(8,128)S(1)}, u32[]{:S(2)}, u32[]{:S(2)}) collective-permute-start(f32[5,6,8,128]{3,2,1,0:T(8,128)S(1)} %get-tuple-element.33), channel_id=1, source_target_pairs={{0,1},{1,2},{2,3},{3,4},{4,5},{5,6},{6,7},{7,8},{8,9},{9,10},{10,1... | collective-permute-start | bytes 368648 | tf_op jit(solution)/shard_map/ppermute | solution.py:503
  25.3 18.0 %collective-permute-start.4 = (f32[224,128]{1,0:T(8,128)S(1)}, f32[224,128]{1,0:T(8,128)S(1)}, u32[]{:S(2)}, u32[]{:S(2)}) collective-permute-start(f32[224,128]{1,0:T(8,128)S(1)} %get-tuple-element.37), channel_id=1, source_target_pairs={{0,1},{2,3},{4,5},{6,7},{8,9},{10,11},{12,13},{14,15},{16,17},{18,... | collective-permute-start | bytes 344072 | tf_op jit(solution)/shard_map/ppermute | solution.py:521
  29.3 14.0 %collective-permute-start.5 = (f32[224,128]{1,0:T(8,128)S(1)}, f32[224,128]{1,0:T(8,128)S(1)}, u32[]{:S(2)}, u32[]{:S(2)}) collective-permute-start(f32[224,128]{1,0:T(8,128)S(1)} %get-tuple-element.38), channel_id=1, source_target_pairs={{1,2},{3,4},{5,6},{7,8},{9,10},{11,12},{13,14},{15,16},{17,18},{19... | collective-permute-start | bytes 344072 | tf_op jit(solution)/shard_map/ppermute | solution.py:522

commit v9 on v6

--- a/solution.py
+++ b/solution.py
@@ -13,8 +13,7 @@
 FIELDS = 3
 MOVED = 2
 KINDS = 5
-SHELL = GROUPS + 6
-CORE = 3 * (GROUPS - 2)
+CORE = 3 * GROUPS
 ROWS = EDGE + 16
 DEEP = EDGE + 8
 CORNERS = 6 * EDGE
@@ -75,24 +74,15 @@
         out[2 * f, at] = jnp.where(even, turned[f], first[f])
 
 
-def pack_shell(counts_ref, old_ref, out, counts, boxes, sems):
+def pack_all(counts_ref, old_ref, shell, core, counts, boxes, sems):
     copies, moved = fetch(counts_ref, old_ref, counts, boxes, sems, MOVED)
     for copy in copies:
         copy.wait()
     for g in range(GROUPS):
-        pack(boxes, moved, out, g, g, "edge")
-    for side, g in enumerate((0, GROUPS - 1)):
+        pack(boxes, moved, shell, g, g, "edge")
+    for g in range(GROUPS):
         for which in range(3):
-            pack(boxes, moved, out, GROUPS + 3 * side + which, g, which)
-
-
-def pack_core(counts_ref, old_ref, out, counts, boxes, sems):
-    copies, moved = fetch(counts_ref, old_ref, counts, boxes, sems, MOVED)
-    for copy in copies:
-        copy.wait()
-    for g in range(1, GROUPS - 1):
-        for which in range(3):
-            pack(boxes, moved, out, 3 * (g - 1) + which, g, which)
+            pack(boxes, moved, core, 3 * g + which, g, which)
 
 
 def interleave(v):
@@ -139,10 +129,7 @@
 def wire_rows(shell, core, k, g):
     low = iota((8, LANES), 0) < 4
     edge = shell[k, g]
-    if g in (0, GROUPS - 1):
-        mid = [shell[k, GROUPS + (3 if g else 0) + which] for which in range(3)]
-    else:
-        mid = [core[k, 3 * (g - 1) + which] for which in range(3)]
+    mid = [core[k, 3 * g + which] for which in range(3)]
     return jnp.concatenate([jnp.where(low, edge, mid[0]), mid[1], mid[2], jnp.where(low, mid[0], edge)], axis=0)
 
 
@@ -176,12 +163,12 @@
             second[y] = jnp.where(odd, up, down)
 
 
-def make_slabs(counts_ref, shell, own, first, second):
+def make_slabs(counts_ref, shell, core, own, first, second):
     taken = iota((EDGE, LANES), 1) < moved_boxes(counts_ref) * EDGE
     blacks = [~is_red((EDGE, LANES), y) for y in range(2)]
     sides = []
     for side, g in enumerate((0, GROUPS - 1)):
-        kinds = [wire_rows(shell, None, k, g) for k in range(KINDS)]
+        kinds = [wire_rows(shell, core, k, g) for k in range(KINDS)]
         p, f, b = [[jnp.where(taken, row, own[i, 4 * g + r]) for r, row in enumerate(unmix(kinds, i))] for i in range(FIELDS)]
         near, next_, far = (3, 2, 1) if side else (0, 1, 2)
         sides.append(
@@ -495,6 +482,7 @@
 
     def read(body, outputs, after=None, limit=54400000):
         table = counts if after is None else lax.optimization_barrier((counts, after))[0]
+        table = pltpu.with_memory_space_constraint(table, pltpu.HBM)
         scratch = [
             VMEM(counts.shape, jnp.int32),
             VMEM((FIELDS, COLUMN, EDGE, EDGE * EDGE), F32),
@@ -504,8 +492,7 @@
 
     strip, message = (EDGE, 8, LANES), (YMSG, LANES)
     deep = (DEEP, ROWS, LANES)
-    (shell,) = read(pack_shell, [(KINDS, SHELL, 8, LANES)])
-    (core,) = read(pack_core, [(KINDS, CORE, 8, LANES)], shell)
+    shell, core = read(pack_all, [(KINDS, GROUPS, 8, LANES), (KINDS, CORE, 8, LANES)])
     shell = lax.ppermute(shell, ("grp", "dev"), chain)
     core = lax.ppermute(core, ("grp", "dev"), chain)
     own, edges = read(relayout, [(FIELDS, EDGE, EDGE, LANES), (FIELDS, EDGE, 8, LANES)])
@@ -513,7 +500,7 @@
     table = lax.optimization_barrier((counts, x_first))[0]
     x_first = lax.ppermute(x_first, "grp", x_ways[0])
     x_second = lax.ppermute(x_second, "grp", x_ways[1])
-    y_first, y_second = call(make_slabs, (table, shell, own), [message, message], [], 10**6, 10**6)
+    y_first, y_second = call(make_slabs, (table, shell, core, own), [message, message], [], 10**6, 10**6)
     y_first, y_second = call(
         add_corners,
         (x_first, x_second, y_first, y_second),

time: 41.3 us -> 47.4 us (1.15)
  waiting for transfers between devices: 8.8 us -> 18.2 us
  Pallas kernels: 10.9 us -> 9.49 us
  starting transfers between devices: 19.8 us -> 18.6 us
  local copies, waits for them, and re-layouts: 0.68 us -> 0.01 us
    ppermute x1, waiting for transfers between devices: 3.24 us -> 12.7 us  [per_device(): shell = lax.ppermute(shell, ('grp', 'dev'), chain)]
    pallas_call x8 -> x7, Pallas kernels: 10.9 us -> 9.49 us  [call(): pl.pallas_call(body, out_shape=[jax.ShapeDtypeStruct(shape, F32) for shap...]
    ppermute x1, starting transfers between devices: 4.57 us -> 3.44 us  [per_device(): x_first = lax.ppermute(x_first, 'grp', x_ways[0])]
    unnamed x4 -> x2, local copies, waits for them, and re-layouts: 0.68 us -> 0.01 us
  transfers between devices with their start and end apart: 6 -> 6, of which waited for: 3 -> 3; matrix products, arithmetic and copies ran while one was open for 0% -> 0% of each run, Pallas kernels for 19% -> 13%
where the time goes in v9:
time: 47.4 us; the launch traced here: 47.1 us
  starting transfers between devices  18.6 us (39%)
  waiting for transfers between devices  18.2 us (38%)
  Pallas kernels  9.49 us (20%)
  between operations  0.74 us (2%)
    ppermute x1, waiting for transfers between devices, per_device(): shell = lax.ppermute(shell, ('grp', 'dev'), chain)  12.7 us
    pallas_call x7, Pallas kernels, call(): pl.pallas_call(body, out_shape=[jax.ShapeDtypeStruct(shape, F32) for shap...  9.49 us
    ppermute x1, starting transfers between devices, per_device(): x_second = lax.ppermute(x_second, 'grp', x_ways[1])  5.11 us
    ppermute x1, starting transfers between devices, per_device(): x_first = lax.ppermute(x_first, 'grp', x_ways[0])  3.44 us
    ppermute x1, waiting for transfers between devices, per_device(): y_second = lax.ppermute(y_second, 'dev', y_ways[1])  3.18 us
    ppermute x1, starting transfers between devices, per_device(): core = lax.ppermute(core, ('grp', 'dev'), chain)  3.12 us
    ppermute x1, starting transfers between devices, per_device(): shell = lax.ppermute(shell, ('grp', 'dev'), chain)  3.12 us
    ppermute x1, waiting for transfers between devices, per_device(): x_second = lax.ppermute(x_second, 'grp', x_ways[1])  2.39 us
  transfers between devices with their start and end apart: 6, of which 3 were waited for; matrix products, arithmetic and copies ran while one was open for 0% of the time, Pallas kernels for 13%

profile of v9, /device:TPU:225, one launch (start us, length us, event | category | flops | bytes accessed | tf_op | source)
XLA Modules:
  0.0 47.1 jit_solution(1002366064915145855)
XLA Ops:
  0.6 0.0 copy-start
  0.6 1.6 %shard_map.41 = (f32[5,8,8,128]{3,2,1,0:T(8,128)S(1)}, f32[5,24,8,128]{3,2,1,0:T(8,128)S(1)}) custom-call(s32[4,128]{1,0:T(4,128)} %bitcast.3, f32[3,8,32,1024]{3,2,1,0:T(8,128)} %old_ref.3), custom_call_target="tpu_custom_call" | custom-call | flops 1000000 | bytes 2000000 | tf_op jit(solution)/shard_map/pallas_call | solution.py:456
  2.2 3.1 %collective-permute-start.3 = (f32[5,24,8,128]{3,2,1,0:T(8,128)S(1)}, f32[5,24,8,128]{3,2,1,0:T(8,128)S(1)}, u32[]{:S(2)}, u32[]{:S(2)}) collective-permute-start(f32[5,24,8,128]{3,2,1,0:T(8,128)S(1)} %get-tuple-element.32), channel_id=1, source_target_pairs={{0,1},{1,2},{2,3},{3,4},{4,5},{5,6},{6,7},{7,8},{8,9},{9,10},{10,1... | collective-permute-start | bytes 1474568 | tf_op jit(solution)/shard_map/ppermute | solution.py:497
  5.4 3.1 %collective-permute-start = (f32[5,8,8,128]{3,2,1,0:T(8,128)S(1)}, f32[5,8,8,128]{3,2,1,0:T(8,128)S(1)}, u32[]{:S(2)}, u32[]{:S(2)}) collective-permute-start(f32[5,8,8,128]{3,2,1,0:T(8,128)S(1)} %get-tuple-element.27), channel_id=1, source_target_pairs={{0,1},{1,2},{2,3},{3,4},{4,5},{5,6},{6,7},{7,8},{8,9},{9,10},{10,1... | collective-permute-start | bytes 491528 | tf_op jit(solution)/shard_map/ppermute | solution.py:496
  8.5 1.9 %shard_map.42 = (f32[3,32,32,128]{3,2,1,0:T(8,128)S(1)}, f32[3,32,8,128]{3,2,1,0:T(8,128)S(1)}) custom-call(s32[4,128]{1,0:T(4,128)} %bitcast.4, f32[3,8,32,1024]{3,2,1,0:T(8,128)} %old_ref.3), custom_call_target="tpu_custom_call" | custom-call | flops 1000000 | bytes 2000000 | tf_op jit(solution)/shard_map/pallas_call | solution.py:456
  10.4 12.7 %collective-permute-done.shell = f32[5,8,8,128]{3,2,1,0:T(8,128)S(1)} collective-permute-done((f32[5,8,8,128]{3,2,1,0:T(8,128)S(1)}, f32[5,8,8,128]{3,2,1,0:T(8,128)S(1)}, u32[]{:S(2)}, u32[]{:S(2)}) %collective-permute-start) | collective-permute-done | bytes 163872 | tf_op jit(solution)/shard_map/ppermute | solution.py:496
  23.1 0.0 copy-done
  23.1 0.2 shard_map.43
  23.3 3.4 %collective-permute-start.1 = (f32[32,8,128]{2,1,0:T(8,128)S(1)}, f32[32,8,128]{2,1,0:T(8,128)S(1)}, u32[]{:S(2)}, u32[]{:S(2)}) collective-permute-start(f32[32,8,128]{2,1,0:T(8,128)S(1)} %get-tuple-element.29), channel_id=1, source_target_pairs={{0,32},{64,96},{128,160},{192,224},{256,288},{320,352},{384,416},{... | collective-permute-start | bytes 393224 | tf_op jit(solution)/shard_map/ppermute | solution.py:501
  26.7 5.1 %collective-permute-start.2 = (f32[32,8,128]{2,1,0:T(8,128)S(1)}, f32[32,8,128]{2,1,0:T(8,128)S(1)}, u32[]{:S(2)}, u32[]{:S(2)}) collective-permute-start(f32[32,8,128]{2,1,0:T(8,128)S(1)} %get-tuple-element.30), channel_id=1, source_target_pairs={{32,64},{96,128},{160,192},{224,256},{288,320},{352,384},{416,448}... | collective-permute-start | bytes 393224 | tf_op jit(solution)/shard_map/ppermute | solution.py:502
  31.8 0.0 collective-permute-done.3.core
  31.8 0.2 shard_map.44
  32.1 0.0 collective-permute-done.1.x_first
  32.1 2.4 %collective-permute-done.2.x_second = f32[32,8,128]{2,1,0:T(8,128)S(1)} collective-permute-done((f32[32,8,128]{2,1,0:T(8,128)S(1)}, f32[32,8,128]{2,1,0:T(8,128)S(1)}, u32[]{:S(2)}, u32[]{:S(2)}) %collective-permute-start.2) | collective-permute-done | bytes 131104 | tf_op jit(solution)/shard_map/ppermute | solution.py:502
  34.5 0.1 shard_map.45
  34.6 1.9 %collective-permute-start.4 = (f32[224,128]{1,0:T(8,128)S(1)}, f32[224,128]{1,0:T(8,128)S(1)}, u32[]{:S(2)}, u32[]{:S(2)}) collective-permute-start(f32[224,128]{1,0:T(8,128)S(1)} %get-tuple-element.36), channel_id=1, source_target_pairs={{0,1},{2,3},{4,5},{6,7},{8,9},{10,11},{12,13},{14,15},{16,17},{18,... | collective-permute-start | bytes 344072 | tf_op jit(solution)/shard_map/ppermute | solution.py:514
  36.5 1.9 %collective-permute-start.5 = (f32[224,128]{1,0:T(8,128)S(1)}, f32[224,128]{1,0:T(8,128)S(1)}, u32[]{:S(2)}, u32[]{:S(2)}) collective-permute-start(f32[224,128]{1,0:T(8,128)S(1)} %get-tuple-element.37), channel_id=1, source_target_pairs={{1,2},{3,4},{5,6},{7,8},{9,10},{11,12},{13,14},{15,16},{17,18},{19... | collective-permute-start | bytes 344072 | tf_op jit(solution)/shard_map/ppermute | solution.py:515
  38.4 4.0 %shard_map.46 = (f32[1024,128]{1,0:T(8,128)S(1)}, f32[1024,128]{1,0:T(8,128)S(1)}, f32[40,48,128]{2,1,0:T(8,128)S(1)}, f32[40,48,128]{2,1,0:T(8,128)S(1)}, f32[4...) custom-call(s32[4,128]{1,0:T(4,128)S(1)} %bitcast.7, ...), custom_call_target="tpu_custom_call" | custom-call | flops 100000000 | bytes 5000000 | tf_op jit(solution)/shard_map/pallas_call | solution.py:456
  42.4 0.0 collective-permute-done.4.y_first
  42.4 3.2 %collective-permute-done.5.y_second = f32[224,128]{1,0:T(8,128)S(1)} collective-permute-done((f32[224,128]{1,0:T(8,128)S(1)}, f32[224,128]{1,0:T(8,128)S(1)}, u32[]{:S(2)}, u32[]{:S(2)}) %collective-permute-start.5) | collective-permute-done | bytes 114720 | tf_op jit(solution)/shard_map/ppermute | solution.py:515
  45.6 1.5 %shard_map.47 = (f32[1024,128]{1,0:T(8,128)}, f32[1024,128]{1,0:T(8,128)}) custom-call(f32[224,128]{1,0:T(8,128)S(1)} %collective-permute-done.4.y_first, f32[224,128]{1,0:T(8,128)S(1)} %collective-permute-done.5.y_second, f32[32,8,128]{2,1,0:T(8,128)S(1)} %collective-permute-done.1.x_first, f32[32,8,128]{2,1,0:T(8,128)S(1)} %collective-permute-done.2.x_second, ...), custom_call_target="tpu_custom_call" | custom-call | flops 10000000 | bytes 1000000 | tf_op jit(solution)/shard_map/pallas_call | solution.py:456
Async XLA Ops:
  0.6 22.4 %copy-start = (s32[512]{0:T(512)S(1)}, s32[512]{0:T(512)}, u32[]{:S(2)}) copy-start(s32[512]{0:T(512)} %param.3) | copy-start | bytes 6148
  2.2 29.6 %collective-permute-start.3 = (f32[5,24,8,128]{3,2,1,0:T(8,128)S(1)}, f32[5,24,8,128]{3,2,1,0:T(8,128)S(1)}, u32[]{:S(2)}, u32[]{:S(2)}) collective-permute-start(f32[5,24,8,128]{3,2,1,0:T(8,128)S(1)} %get-tuple-element.32), channel_id=1, source_target_pairs={{0,1},{1,2},{2,3},{3,4},{4,5},{5,6},{6,7},{7,8},{8,9},{9,10},{10,1... | collective-permute-start | bytes 1474568 | tf_op jit(solution)/shard_map/ppermute | solution.py:497
  5.4 17.7 %collective-permute-start = (f32[5,8,8,128]{3,2,1,0:T(8,128)S(1)}, f32[5,8,8,128]{3,2,1,0:T(8,128)S(1)}, u32[]{:S(2)}, u32[]{:S(2)}) collective-permute-start(f32[5,8,8,128]{3,2,1,0:T(8,128)S(1)} %get-tuple-element.27), channel_id=1, source_target_pairs={{0,1},{1,2},{2,3},{3,4},{4,5},{5,6},{6,7},{7,8},{8,9},{9,10},{10,1... | collective-permute-start | bytes 491528 | tf_op jit(solution)/shard_map/ppermute | solution.py:496
  23.3 8.8 %collective-permute-start.1 = (f32[32,8,128]{2,1,0:T(8,128)S(1)}, f32[32,8,128]{2,1,0:T(8,128)S(1)}, u32[]{:S(2)}, u32[]{:S(2)}) collective-permute-start(f32[32,8,128]{2,1,0:T(8,128)S(1)} %get-tuple-element.29), channel_id=1, source_target_pairs={{0,32},{64,96},{128,160},{192,224},{256,288},{320,352},{384,416},{... | collective-permute-start | bytes 393224 | tf_op jit(solution)/shard_map/ppermute | solution.py:501
  26.7 7.8 %collective-permute-start.2 = (f32[32,8,128]{2,1,0:T(8,128)S(1)}, f32[32,8,128]{2,1,0:T(8,128)S(1)}, u32[]{:S(2)}, u32[]{:S(2)}) collective-permute-start(f32[32,8,128]{2,1,0:T(8,128)S(1)} %get-tuple-element.30), channel_id=1, source_target_pairs={{32,64},{96,128},{160,192},{224,256},{288,320},{352,384},{416,448}... | collective-permute-start | bytes 393224 | tf_op jit(solution)/shard_map/ppermute | solution.py:502
  34.6 7.8 %collective-permute-start.4 = (f32[224,128]{1,0:T(8,128)S(1)}, f32[224,128]{1,0:T(8,128)S(1)}, u32[]{:S(2)}, u32[]{:S(2)}) collective-permute-start(f32[224,128]{1,0:T(8,128)S(1)} %get-tuple-element.36), channel_id=1, source_target_pairs={{0,1},{2,3},{4,5},{6,7},{8,9},{10,11},{12,13},{14,15},{16,17},{18,... | collective-permute-start | bytes 344072 | tf_op jit(solution)/shard_map/ppermute | solution.py:514
  36.5 9.1 %collective-permute-start.5 = (f32[224,128]{1,0:T(8,128)S(1)}, f32[224,128]{1,0:T(8,128)S(1)}, u32[]{:S(2)}, u32[]{:S(2)}) collective-permute-start(f32[224,128]{1,0:T(8,128)S(1)} %get-tuple-element.37), channel_id=1, source_target_pairs={{1,2},{3,4},{5,6},{7,8},{9,10},{11,12},{13,14},{15,16},{17,18},{19... | collective-permute-start | bytes 344072 | tf_op jit(solution)/shard_map/ppermute | solution.py:515
